TPU v7x, 32 devices: a whole 2x2x4 slice. The times are simulated.
32 devices in a mesh: grp: 4 (over x, core), slab: 8 (over z, y).
Axes of the slice: x: 2, y: 2, z: 4, core: 2. Of those that a mesh axis runs over, the one named last changes fastest.
Arguments:
- theta: float32 [4, 128, 64, 256], P('grp', 'slab'), may hold values from -6 to 6
- register: float32 [4, 128, 64, 256], P('grp', 'slab'), may hold values from -6 to 6
- velocity: bfloat16 [3, 64, 32, 128], P(None, 'slab', 'grp'), may hold values from -6 to 6
- diffusivity: float32 [4], P('grp'), may hold values from 0.05 to 0.5
Outputs:
- theta_new: float32 [4, 128, 64, 256], P('grp', 'slab')
- register_new: float32 [4, 128, 64, 256], P('grp', 'slab')
All inputs are finite; a program needn't handle non-finite values.
Results may differ from a plain program's by a relative error of at most 0.0014.
Values may be sent and summed in bfloat16 or wider, within the bound.
No kernel may reach another device: no remote copies, remote signals or barrier semaphores. Data moves between devices by JAX's collectives and lax.ppermute only.
A program may use at most 64 MiB of HBM per device.

v0:
```python
import jax
import jax.numpy as jnp
from jax import lax
from jax.sharding import PartitionSpec as P

BLK = 32


ALPHA = 4.0 / 9.0
BETA = 1.0 / 36.0
COEF_A = 40.0 / 27.0
COEF_B = 25.0 / 54.0
RK_A = -5.0 / 9.0
RK_B = 15.0 / 16.0
STEP = 0.2


def with_halo(cells, sides, width):
    for axis, dim in sides:
        count = lax.axis_size(axis)
        head = lax.slice_in_dim(cells, 0, width, axis=dim)
        tail = lax.slice_in_dim(cells, cells.shape[dim] - width, cells.shape[dim], axis=dim)
        cells = jnp.concatenate(
            [
                lax.ppermute(tail, axis, [(i, (i + 1) % count) for i in range(count)]),
                cells,
                lax.ppermute(head, axis, [((i + 1) % count, i) for i in range(count)]),
            ],
            axis=dim,
        )
    return cells


def band_matrices(count, periodic):
    rows = jnp.arange(count)[:, None]
    cols = jnp.arange(count)[None, :]
    offset = cols - rows
    if periodic:
        offset = (offset + count // 2) % count - count // 2
    one = jnp.float32(1.0)
    zero = jnp.float32(0.0)
    lhs = (
        jnp.where(offset == 0, one, zero)
        + ALPHA * jnp.where(jnp.abs(offset) == 1, one, zero)
        + BETA * jnp.where(jnp.abs(offset) == 2, one, zero)
    )
    rhs = 0.5 * COEF_A * (
        jnp.where(offset == 1, one, zero) - jnp.where(offset == -1, one, zero)
    ) + 0.25 * COEF_B * (jnp.where(offset == 2, one, zero) - jnp.where(offset == -2, one, zero))
    return (lhs, rhs)


def block_inverse(count):
    lhs, rhs = band_matrices(count, False)
    factor = jnp.linalg.cholesky(lhs)
    return jax.scipy.linalg.cho_solve((factor, True), jnp.eye(count, dtype=lhs.dtype))


def blocked_operator(count, block):
    lhs, rhs = band_matrices(count, True)
    inverse = block_inverse(block)
    diagonal = jnp.kron(jnp.eye(count // block, dtype=jnp.float32), inverse)
    return jnp.dot(diagonal, rhs, precision=lax.Precision.HIGHEST)


def wrap_pad(field, axis):
    count = field.shape[axis]
    left = lax.slice_in_dim(field, count - 2, count, axis=axis)
    right = lax.slice_in_dim(field, 0, 2, axis=axis)
    return jnp.concatenate([left, field, right], axis=axis)


def refine(padded, axis, count):

    def taken(shift):
        return lax.slice_in_dim(padded, 2 + shift, 2 + shift + count, axis=axis)

    even = (
        -0.0390625 * taken(-2) + 0.2734375 * taken(-1) + 0.8203125 * taken(0) - 0.0546875 * taken(1)
    )
    odd = (
        -0.0546875 * taken(-1) + 0.8203125 * taken(0) + 0.2734375 * taken(1) - 0.0390625 * taken(2)
    )
    stacked = jnp.stack([even, odd], axis=axis + 1)
    shape = list(even.shape)
    shape[axis] = 2 * count
    return stacked.reshape(shape)


def x_block(padded, inverse, planes):
    rhs = 0.5 * COEF_A * (padded[3 : 3 + planes] - padded[1 : 1 + planes]) + 0.25 * COEF_B * (
        padded[4 : 4 + planes] - padded[0:planes]
    )
    return jnp.einsum("ij,jyz->iyz", inverse, rhs, precision=lax.Precision.HIGHEST)


def y_derivative(field, operator):
    return jnp.einsum("ij,xjz->xiz", operator, field, precision=lax.Precision.HIGHEST)


def z_derivative(field, operator):
    return jnp.einsum("ij,xyj->xyi", operator, field, precision=lax.Precision.HIGHEST)


def shards(theta, register, velocity, diffusivity):
    planes = theta.shape[1]
    whole_y = lax.all_gather(velocity, "grp", axis=2, tiled=True)
    padded = with_halo(whole_y, (("slab", 1),), 2)
    coarse = padded.astype(jnp.float32)
    flow = refine(coarse, 1, planes // 2)
    flow = refine(wrap_pad(flow, 2), 2, flow.shape[2])
    flow = refine(wrap_pad(flow, 3), 3, flow.shape[3])
    inverse = block_inverse(planes)
    oper_y = blocked_operator(theta.shape[2], BLK)
    oper_z = blocked_operator(theta.shape[3], BLK)
    field = theta[0]
    kappa = diffusivity[0]
    scalar_pad = with_halo(field.astype(jnp.bfloat16), (("slab", 0),), 2).astype(field.dtype)
    grad_x = x_block(scalar_pad, inverse, planes)
    grad_y = y_derivative(field, oper_y)
    grad_z = z_derivative(field, oper_z)
    flux_x = flow[0] * field - kappa * grad_x
    flux_y = flow[1] * field - kappa * grad_y
    flux_z = flow[2] * field - kappa * grad_z
    flux_pad = with_halo(flux_x, (("slab", 0),), 2)
    rate = -(
        x_block(flux_pad, inverse, planes)
        + y_derivative(flux_y, oper_y)
        + z_derivative(flux_z, oper_z)
    )
    new_saved = RK_A * register[0] + STEP * rate
    new_field = field + RK_B * new_saved
    return (new_field[None], new_saved[None])


def solution(mesh):
    in_specs = (
        P("grp", "slab", None, None),
        P("grp", "slab", None, None),
        P(None, "slab", "grp", None),
        P("grp"),
    )
    out_specs = (P("grp", "slab", None, None), P("grp", "slab", None, None))
    return jax.shard_map(shards, mesh=mesh, in_specs=in_specs, out_specs=out_specs, check_vma=False)
```

profile of v0, /device:TPU:0, one launch (start us, length us, event | category | flops | bytes accessed | tf_op | source)
XLA Modules:
  0.0 87.1 jit_solution(14519969915449498608)
XLA Ops:
  0.6 7.2 %all_gather.3 = bf16[3,8,32,128]{3,2,1,0:T(8,128)(2,1)S(1)} all-gather(bf16[3,8,8,128]{3,2,1,0:T(8,128)(2,1)} %param.9), channel_id=1, replica_groups=mesh['grp'=4,'slab'=8] {'grp'}, dimensions={2}, use_global_device_ids=true | all-gather | bytes 245760 | tf_op jit(solution)/shard_map/all_gather | solution.py:107
  7.9 1.8 %collective-permute-start = (bf16[3,2,32,128]{3,2,1,0:T(8,128)(2,1)S(1)}, bf16[3,2,32,128]{3,2,1,0:T(8,128)(2,1)S(1)}, u32[]{:S(2)}, u32[]{:S(2)}) collective-permute-start(bf16[3,2,32,128]{3,2,1,0:T(8,128)(2,1)S(1)} %get-tuple-element.27), channel_id=1, source_target_pairs={{0,1},{1,2},{2,3},{3,4},{4,5},{5,6},{6,7},{7,0},{8,9},{9,10},{10,1... | collective-permute-start | bytes 147464 | tf_op jit(solution)/shard_map/ppermute | solution.py:25
  9.7 3.1 %collective-permute-start.1 = (bf16[3,2,32,128]{3,2,1,0:T(8,128)(2,1)S(1)}, bf16[3,2,32,128]{3,2,1,0:T(8,128)(2,1)S(1)}, u32[]{:S(2)}, u32[]{:S(2)}) collective-permute-start(bf16[3,2,32,128]{3,2,1,0:T(8,128)(2,1)S(1)} %get-tuple-element.28), channel_id=1, source_target_pairs={{1,0},{2,1},{3,2},{4,3},{5,4},{6,5},{7,6},{0,7},{9,8},{10,9},{11,1... | collective-permute-start | bytes 147464 | tf_op jit(solution)/shard_map/ppermute | solution.py:27
  12.8 1.8 %copy.75 = bf16[1,16,64,256]{3,1,2,0:T(8,128)(2,1)S(1)} copy(f32[1,16,64,256]{3,2,1,0:T(8,128)} %param.7) | data formatting | bytes 1572864 | tf_op args[0]
  16.1 4.7 %collective-permute-start.3 = (bf16[2,64,256]{2,0,1:T(2,128)(2,1)}, bf16[2,64,256]{2,0,1:T(2,128)(2,1)}, u32[]{:S(2)}, u32[]{:S(2)}) collective-permute-start(bf16[2,64,256]{2,0,1:T(2,128)(2,1)} %get-tuple-element.26), channel_id=1, source_target_pairs={{1,0},{2,1},{3,2},{4,3},{5,4},{6,5},{7,6},{0,7},{9,8},{10,9},{11,1... | collective-permute-start | bytes 196616 | tf_op jit(solution)/shard_map/ppermute | solution.py:27
  25.2 2.9 %cholesky.63 = f32[32,32]{1,0:T(8,128)S(1)} custom-call(f32[32,32]{1,0:T(8,128)S(1)} %fusion.121), custom_call_target="Cholesky" | custom-call | tf_op jit(solution)/shard_map/jit(cholesky)/cholesky | solution.py:55
  29.5 2.4 %custom-call.18 = f32[1,32,32]{1,2,0:T(8,128)S(1)} custom-call(f32[1,32,32]{2,1,0:T(8,128)S(1)} %fusion.116), custom_call_target="InvertDiagBlocksLowerTriangular" | custom-call | tf_op jit(solution)/shard_map/jit(_cho_solve)/triangular_solve | solution.py:56
  32.7 2.0 %fusion.38 = f32[64,16,256]{2,0,1:T(8,128)} fusion(f32[64,64,1]{1,0,2:T(8,128)S(1)} %convolution_bitcast_fusion.1, f32[1,16,64,256]{3,2,1,0:T(8,128)S(1)} %copy-done), kind=kOutput, calls=%fused_computation.60 | convolution fusion | flops 201326592 | bytes 2113536 | tf_op jit(solution)/shard_map/ij,xjz->xiz/dot_general | solution.py:98
  39.1 4.0 %fusion.6 = (f32[3,16,64,128,1]{3,1,2,0,4:T(8,128)S(1)}, f32[3,16,64,128,1]{3,1,2,0,4:T(8,128)S(1)}) fusion(f32[3,16,64,2]{3,1,2,0:T(8,128)S(1)} %get-tuple-element.15, f32[3,16,64,128]{3,1,2,0:T(8,128)S(1)} %bitcast.94, f32[3,16,64,2]{3,1,2,0:T(8,128)S(1)} %get-tuple-element.16), kind=kLoop, calls=%fused_computation.14 | loop fusion | flops 7077888 | bytes 4767744 | tf_op jit(solution)/shard_map/stack | solution.py:84
  43.1 1.8 %fusion.24 = (f32[1,16,64,128,2]{3,1,2,0,4:T(8,128)}, f32[1,16,64,128,2]{3,1,2,0,4:T(8,128)}, f32[1,16,64,128,2]{3,1,2,0,4:T(8,128)}) fusion(f32[3,16,64,128,1]{3,1,2,0,4:T(8,128)S(1)} %get-tuple-element.10, f32[3,16,64,128,1]{3,1,2,0,4:T(8,128)S(1)} %get-tuple-element.11), kind=kLoop, calls=%fused_computation.43 | loop fusion | flops 786432 | bytes 6291456 | tf_op jit(solution)/shard_map/stack | solution.py:84
  44.9 3.1 %copy.41 = f32[1,16,64,128,2]{2,1,4,3,0:T(8,128)S(1)} copy(f32[1,16,64,128,2]{3,1,2,0,4:T(8,128)} %get-tuple-element.12) | data formatting | bytes 2097152 | tf_op jit(solution)/shard_map/slice | solution.py:123
  48.0 2.3 %copy.42 = f32[16,64,256]{2,0,1:T(8,128)} copy(f32[16,64,256]{1,0,2:T(8,128)S(1)} %bitcast.95) | data formatting | bytes 2097152 | tf_op jit(solution)/shard_map/squeeze | solution.py:123
  50.3 3.1 %copy.48 = f32[1,16,64,128,2]{2,1,4,3,0:T(8,128)S(1)} copy(f32[1,16,64,128,2]{3,1,2,0,4:T(8,128)} %get-tuple-element.14) | data formatting | bytes 2097152 | tf_op jit(solution)/shard_map/slice | solution.py:124
  53.4 2.3 %copy.49 = f32[16,64,256]{2,0,1:T(8,128)} copy(f32[16,64,256]{1,0,2:T(8,128)S(1)} %bitcast.96) | data formatting | bytes 2097152 | tf_op jit(solution)/shard_map/squeeze | solution.py:124
  55.7 3.8 %bitcast_subtract_fusion = f32[16,64,256]{2,0,1:T(8,128)} fusion(f32[16,64,256]{2,0,1:T(8,128)} %copy.42, f32[64,16,256]{2,0,1:T(8,128)} %fusion.38, f32[1,16,64,256]{3,2,1,0:T(8,128)S(1)} %copy-done, f32[]{:T(128)} %bitcast.91), kind=kLoop, calls=%fused_computation.59 | loop fusion | flops 786432 | bytes 4194308 | tf_op jit(solution)/shard_map/sub | solution.py:123
  59.5 1.9 %fusion.16 = f32[16,64,256]{2,0,1:T(8,128)S(1)} fusion(f32[256,256,1]{1,0,2:T(8,128)S(1)} %convolution_bitcast_fusion, f32[16,64,256]{2,0,1:T(8,128)S(1)} %copy-done.1, f32[1,16,64,256]{3,2,1,0:T(8,128)S(1)} %copy-done, f32[]{:T(128)} %bitcast.92), kind=kOutput, calls=%fused_computation.34 | convolution fusion | flops 806092800 | bytes 3407876 | tf_op jit(solution)/shard_map/ij,xyj->xyi/dot_general | solution.py:102
  61.4 2.0 %fusion.190 = f32[16,64,256]{2,0,1:T(8,128)} fusion(f32[16,64,256]{2,0,1:T(8,128)S(1)} %fusion.16, f32[256,256,1]{1,0,2:T(8,128)S(1)} %convolution_bitcast_fusion), kind=kOutput, calls=%fused_computation.254 | convolution fusion | flops 805306368 | bytes 2359296 | tf_op jit(solution)/shard_map/ij,xyj->xyi/dot_general | solution.py:102
  63.4 3.1 %copy.39 = f32[1,16,64,128,2]{2,1,4,3,0:T(8,128)S(1)} copy(f32[1,16,64,128,2]{3,1,2,0,4:T(8,128)} %get-tuple-element.13) | data formatting | bytes 2097152 | tf_op jit(solution)/shard_map/slice | solution.py:122
  66.5 2.5 %copy.40 = f32[16,64,256]{2,0,1:T(8,128)} copy(f32[16,64,256]{1,0,2:T(8,128)S(1)} %bitcast.97) | data formatting | bytes 2097152 | tf_op jit(solution)/shard_map/squeeze | solution.py:122
  70.5 1.8 %fusion.14 = f32[16,64,256]{2,0,1:T(8,128)S(1)} fusion(f32[16,16,1]{1,0,2:T(8,128)S(1)} %convolution_bitcast_fusion.2, f32[20,64,256]{2,0,1:T(8,128)S(1)} %maximum_convert_fusion, f32[16,64,256]{2,0,1:T(8,128)S(1)} %copy-done.4, f32[1,16,64,256]{3,2,1,0:T(8,128)S(1)} %copy-done, f32[]{:T(128)} %bitcast.90), kind=kOutput, calls=%fused_computation.31 | convolution fusion | flops 52428800 | bytes 7348228 | tf_op jit(solution)/shard_map/ij,jyz->iyz/dot_general | solution.py:94
  72.6 2.0 %collective-permute-start.5 = (f32[2,64,256]{2,0,1:T(2,128)S(1)}, f32[2,64,256]{2,0,1:T(2,128)S(1)}, u32[]{:S(2)}, u32[]{:S(2)}) collective-permute-start(f32[2,64,256]{2,0,1:T(2,128)S(1)} %get-tuple-element.18), channel_id=1, source_target_pairs={{0,1},{1,2},{2,3},{3,4},{4,5},{5,6},{6,7},{7,0},{8,9},{9,10},{10,1... | collective-permute-start | bytes 393224 | tf_op jit(solution)/shard_map/ppermute | solution.py:25
  74.6 1.7 %fusion.42 = f32[16,256,64]{1,2,0:T(8,128)S(1)} fusion(f32[64,64,1]{1,0,2:T(8,128)S(1)} %convolution_bitcast_fusion.1, f32[16,64,256]{2,0,1:T(8,128)S(1)} %copy-done.2), kind=kOutput, calls=%fused_computation.69 | convolution fusion | flops 201326592 | bytes 2113536 | tf_op jit(solution)/shard_map/ij,xjz->xiz/dot_general | solution.py:98
  76.3 4.0 %collective-permute-done.4 = f32[2,64,256]{2,0,1:T(2,128)S(1)} collective-permute-done((f32[2,64,256]{2,0,1:T(2,128)S(1)}, f32[2,64,256]{2,0,1:T(2,128)S(1)}, u32[]{:S(2)}, u32[]{:S(2)}) %collective-permute-start.4) | collective-permute-done | bytes 131104 | tf_op jit(solution)/shard_map/ppermute | solution.py:27
  80.3 2.9 %fusion.13 = f32[16,64,256]{2,0,1:T(8,128)S(1)} fusion(f32[16,64,256]{2,0,1:T(8,128)S(1)} %copy-done.5, f32[16,16,1]{1,0,2:T(8,128)S(1)} %convolution_bitcast_fusion.2, f32[2,64,256]{2,0,1:T(2,128)S(1)} %collective-permute-done.5, f32[16,64,256]{2,0,1:T(8,128)S(1)} %fusion.14, f32[2,64,256]{2,0,1:T(2,128)S(1)} %collective-permute-done.4, ...), kind=kOutput, calls=%fused_computation.29 | convolution fusion | flops 54263808 | bytes 5506048 | tf_op jit(solution)/shard_map/ij,jyz->iyz/dot_general | solution.py:94
  (60 shorter events, 17.3 us)
Async XLA Ops:
  0.6 32.1 %copy-start = (f32[1,16,64,256]{3,2,1,0:T(8,128)S(1)}, f32[1,16,64,256]{3,2,1,0:T(8,128)}, u32[]{:S(2)}) copy-start(f32[1,16,64,256]{3,2,1,0:T(8,128)} %param.7) | copy-start | bytes 3145732
  7.9 28.7 %collective-permute-start = (bf16[3,2,32,128]{3,2,1,0:T(8,128)(2,1)S(1)}, bf16[3,2,32,128]{3,2,1,0:T(8,128)(2,1)S(1)}, u32[]{:S(2)}, u32[]{:S(2)}) collective-permute-start(bf16[3,2,32,128]{3,2,1,0:T(8,128)(2,1)S(1)} %get-tuple-element.27), channel_id=1, source_target_pairs={{0,1},{1,2},{2,3},{3,4},{4,5},{5,6},{6,7},{7,0},{8,9},{9,10},{10,1... | collective-permute-start | bytes 147464 | tf_op jit(solution)/shard_map/ppermute | solution.py:25
  9.7 26.9 %collective-permute-start.1 = (bf16[3,2,32,128]{3,2,1,0:T(8,128)(2,1)S(1)}, bf16[3,2,32,128]{3,2,1,0:T(8,128)(2,1)S(1)}, u32[]{:S(2)}, u32[]{:S(2)}) collective-permute-start(bf16[3,2,32,128]{3,2,1,0:T(8,128)(2,1)S(1)} %get-tuple-element.28), channel_id=1, source_target_pairs={{1,0},{2,1},{3,2},{4,3},{5,4},{6,5},{7,6},{0,7},{9,8},{10,9},{11,1... | collective-permute-start | bytes 147464 | tf_op jit(solution)/shard_map/ppermute | solution.py:27
  14.6 0.8 copy-start.3
  16.1 52.8 %collective-permute-start.2 = (bf16[2,64,256]{2,0,1:T(2,128)(2,1)}, bf16[2,64,256]{2,0,1:T(2,128)(2,1)S(1)}, u32[]{:S(2)}, u32[]{:S(2)}) collective-permute-start(bf16[2,64,256]{2,0,1:T(2,128)(2,1)} %get-tuple-element.25), channel_id=1, source_target_pairs={{0,1},{1,2},{2,3},{3,4},{4,5},{5,6},{6,7},{7,0},{8,9},{9,10},{10,1... | collective-permute-start | bytes 196616 | tf_op jit(solution)/shard_map/ppermute | solution.py:25
  16.1 52.8 %collective-permute-start.3 = (bf16[2,64,256]{2,0,1:T(2,128)(2,1)}, bf16[2,64,256]{2,0,1:T(2,128)(2,1)}, u32[]{:S(2)}, u32[]{:S(2)}) collective-permute-start(bf16[2,64,256]{2,0,1:T(2,128)(2,1)} %get-tuple-element.26), channel_id=1, source_target_pairs={{1,0},{2,1},{3,2},{4,3},{5,4},{6,5},{7,6},{0,7},{9,8},{10,9},{11,1... | collective-permute-start | bytes 196616 | tf_op jit(solution)/shard_map/ppermute | solution.py:27
  55.7 3.8 %copy-start.1 = (f32[16,64,256]{2,0,1:T(8,128)S(1)}, f32[16,64,256]{2,0,1:T(8,128)}, u32[]{:S(2)}) copy-start(f32[16,64,256]{2,0,1:T(8,128)} %copy.49) | copy-start | bytes 3145732
  69.0 1.5 %copy-start.4 = (f32[16,64,256]{2,0,1:T(8,128)S(1)}, f32[16,64,256]{2,0,1:T(8,128)}, u32[]{:S(2)}) copy-start(f32[16,64,256]{2,0,1:T(8,128)} %copy.40) | copy-start | bytes 3145732
  70.5 4.1 %copy-start.2 = (f32[16,64,256]{2,0,1:T(8,128)S(1)}, f32[16,64,256]{2,0,1:T(8,128)}, u32[]{:S(2)}) copy-start(f32[16,64,256]{2,0,1:T(8,128)} %bitcast_subtract_fusion) | copy-start | bytes 3145732
  72.4 8.0 %copy-start.5 = (f32[16,64,256]{2,0,1:T(8,128)S(1)}, f32[16,64,256]{2,0,1:T(8,128)}, u32[]{:S(2)}) copy-start(f32[16,64,256]{2,0,1:T(8,128)} %fusion.190) | copy-start | bytes 3145732
  72.4 8.0 %copy-start.6 = (f32[1,16,64,256]{3,2,1,0:T(8,128)S(1)}, f32[1,16,64,256]{3,2,1,0:T(8,128)}, u32[]{:S(2)}) copy-start(f32[1,16,64,256]{3,2,1,0:T(8,128)} %param.8) | copy-start | bytes 3145732
  72.5 7.8 %collective-permute-start.4 = (f32[2,64,256]{2,0,1:T(2,128)S(1)}, f32[2,64,256]{2,0,1:T(2,128)S(1)}, u32[]{:S(2)}, u32[]{:S(2)}) collective-permute-start(f32[2,64,256]{2,0,1:T(2,128)S(1)} %get-tuple-element.17), channel_id=1, source_target_pairs={{1,0},{2,1},{3,2},{4,3},{5,4},{6,5},{7,6},{0,7},{9,8},{10,9},{11,1... | collective-permute-start | bytes 393224 | tf_op jit(solution)/shard_map/ppermute | solution.py:27
  72.6 7.8 %collective-permute-start.5 = (f32[2,64,256]{2,0,1:T(2,128)S(1)}, f32[2,64,256]{2,0,1:T(2,128)S(1)}, u32[]{:S(2)}, u32[]{:S(2)}) collective-permute-start(f32[2,64,256]{2,0,1:T(2,128)S(1)} %get-tuple-element.18), channel_id=1, source_target_pairs={{0,1},{1,2},{2,3},{3,4},{4,5},{5,6},{6,7},{7,0},{8,9},{9,10},{10,1... | collective-permute-start | bytes 393224 | tf_op jit(solution)/shard_map/ppermute | solution.py:25
where the time goes:
time: 87.5 us; the launch traced here: 87.1 us
  local copies, waits for them, and re-layouts  24.9 us (28%)
  other arithmetic  23.9 us (27%)
  matrix products  13.7 us (16%)
  starting transfers between devices  11.7 us (13%)
  blocking collectives  7.23 us (8%)
  waiting for transfers between devices  4.05 us (5%)
  between operations  1.63 us (2%)
    ppermute x3, starting transfers between devices, with_halo(): lax.ppermute(head, axis, [((i + 1) % count, i) for i in range(count)])  7.88 us
    all_gather x1, blocking collectives, shards(): whole_y = lax.all_gather(velocity, 'grp', axis=2, tiled=True)  7.23 us
    another operation x6, other arithmetic, refine(): stacked = jnp.stack([even, odd], axis=axis + 1)  6.74 us
    unnamed x17, local copies, waits for them, and re-layouts  5.78 us
    another operation x6, other arithmetic, block_inverse(): factor = jnp.linalg.cholesky(lhs)  5.71 us
    another operation x4, other arithmetic, block_inverse(): jax.scipy.linalg.cho_solve((factor, True), jnp.eye(count, dtype=lhs.dtype))  4.96 us
    dot_general x2, matrix products, x_block(): jnp.einsum('ij,jyz->iyz', inverse, rhs, precision=lax.Precision.HIGHEST)  4.7 us
    ppermute x3, waiting for transfers between devices, with_halo(): lax.ppermute(head, axis, [((i + 1) % count, i) for i in range(count)])  4.04 us
  transfers between devices with their start and end apart: 6, of which 1 were waited for; matrix products, arithmetic and copies ran while one was open for 59% of the time, Pallas kernels for 0%

commit v1 on v0

v1 whole, which is shorter than its diff:
```python
import jax
import jax.numpy as jnp
import numpy as np
from jax import lax
from jax.experimental import pallas as pl
from jax.experimental.pallas import tpu as pltpu
from jax.sharding import PartitionSpec as P

BLK = 32
ALPHA = 4.0 / 9.0
BETA = 1.0 / 36.0
COEF_A = 40.0 / 27.0
COEF_B = 25.0 / 54.0
RK_A = -5.0 / 9.0
RK_B = 15.0 / 16.0
STEP = 0.2
EVEN = (-0.0390625, 0.2734375, 0.8203125, -0.0546875)
ODD = (-0.0546875, 0.8203125, 0.2734375, -0.0390625)
MXU = 256


def band(count):
    eye = lambda k: np.eye(count, k=k)
    return eye(0) + ALPHA * (eye(1) + eye(-1)) + BETA * (eye(2) + eye(-2))


def blocked_operator(count, block):
    rhs = np.zeros((count, count))
    for i in range(count):
        for shift, coef in ((1, COEF_A / 2), (-1, -COEF_A / 2), (2, COEF_B / 4), (-2, -COEF_B / 4)):
            rhs[i, (i + shift) % count] += coef
    return np.kron(np.eye(count // block), np.linalg.inv(band(block))) @ rhs


def refine_operator(count):
    out = np.zeros((2 * count, count))
    for k in range(count):
        for t in range(4):
            out[2 * k, (k - 2 + t) % count] += EVEN[t]
            out[2 * k + 1, (k - 1 + t) % count] += ODD[t]
    return out


def split(x):
    hi = x.astype(jnp.bfloat16)
    return hi, (x - hi.astype(jnp.float32)).astype(jnp.bfloat16)


def host_split(x):
    x = jnp.asarray(np.asarray(x, np.float32))
    return jnp.stack(split(x))


def dot(a, b):
    return jnp.dot(a, b, preferred_element_type=jnp.float32)


def dot3(a, b):
    return dot(a[0], b[0]) + (dot(a[0], b[1]) + dot(a[1], b[0]))


def banded_lu(count):
    m = band(count)
    for k in range(count):
        for i in range(k + 1, min(k + 3, count)):
            m[i, k] /= m[k, k]
            m[i, k + 1 : min(k + 3, count)] -= m[i, k] * m[k, k + 1 : min(k + 3, count)]
    return m


def x_derivative(get, put, work, planes):
    m = banded_lu(planes)
    ratio = (COEF_B / 4) / (COEF_A / 2)
    y1 = y2 = None
    for i in range(planes):
        y = (get(i + 1) - get(i - 1)) + ratio * (get(i + 2) - get(i - 2))
        if i >= 1:
            y = y - float(m[i, i - 1]) * y1
        if i >= 2:
            y = y - float(m[i, i - 2]) * y2
        work[i] = y
        y1, y2 = y, y1
    x1 = x2 = None
    for i in reversed(range(planes)):
        inv = 1.0 / m[i, i]
        x = work[i] * float(inv * COEF_A / 2)
        if i + 1 < planes:
            x = x - float(m[i, i + 1] * inv) * x1
        if i + 2 < planes:
            x = x - float(m[i, i + 2] * inv) * x2
        put(i, x)
        x1, x2 = x, x1


def second_kernel(th, ky2, kz2, out):
    planes, ny, nz = th.shape
    per = ky2.shape[1] // ny
    for g in range(planes // per):
        x = split(th[g * per : (g + 1) * per].reshape(per * ny, nz))
        value = dot3(ky2, x) + dot3(x, kz2)
        out[g * per : (g + 1) * per] = value.reshape(per, ny, nz)


def first_kernel(part, th, tl, tr, *refs):
    parts = refs[: -5]
    gx, vel, tail, head, work = refs[-5:]
    planes, ny, nz = th.shape
    ngrp = len(parts)
    rows, nzc = parts[0].shape[2:]
    nyc = rows * ngrp
    coarse = planes // 2
    for s in range(ngrp):
        at = pl.multiple_of(((part[0] + (ngrp - s)) % ngrp) * rows, rows)
        vel[:, :, pl.ds(at, rows), :] = parts[s][...].astype(jnp.float32)

    def get(p):
        if p < 0:
            return tl[p + 2].astype(jnp.float32)
        if p >= planes:
            return tr[p - planes].astype(jnp.float32)
        return th[p]

    def put(i, value):
        gx[i] = value
        if i < 2:
            head[i] = value.astype(jnp.bfloat16)
        if i >= planes - 2:
            tail[i - (planes - 2)] = value.astype(jnp.bfloat16)

    x_derivative(get, put, work, planes)
    for q in range(8):
        c, k = ((0, 0), (0, 1), (0, 2), (1, 0), (1, 1), (2, 0), (2, 1), (2, 1))[q]
        count = 3 if c == 0 else 2
        at = (2 + q // 4, slice(nyc * (q // 2 % 2), nyc * (q // 2 % 2 + 1)), slice(nzc * (q % 2), nzc * (q % 2 + 1)))
        head[at] = vel[c, k].astype(jnp.bfloat16)
        tail[at] = vel[c, coarse - count + k].astype(jnp.bfloat16)


def final_kernel(kap, th, reg, lap, gx, tl, tr, pay_l, pay_r, vel, ky, kz, ry, rz, new, saved, flux, acc):
    planes, ny, nz = th.shape
    nyc, nzc = vel.shape[2:]
    coarse = planes // 2
    per = ky.shape[1] // ny
    kappa = kap[0]

    def slot(pay, q):
        return pay[2 + q // 4, nyc * (q // 2 % 2) : nyc * (q // 2 % 2 + 1), nzc * (q % 2) : nzc * (q % 2 + 1)].astype(jnp.float32)

    def plane(c, k):
        first, count = ((0, 3), (3, 2), (5, 2))[c]
        if k < 0:
            return slot(pay_l, first + count + k)
        if k >= coarse:
            return slot(pay_r, first + k - coarse)
        return vel[c, k]

    def fine(c, p):
        k = p // 2
        coefs, start = (EVEN, k - 2) if p % 2 == 0 else (ODD, k - 1)
        total = coefs[0] * plane(c, start)
        for t in range(1, 4):
            total = total + coefs[t] * plane(c, start + t)
        return total

    def flow(c, p):
        x = split(jnp.concatenate([fine(c, p + i) for i in range(per)], axis=0))
        z = split(dot(x[0], rz[...]) + dot(x[1], rz[...]))
        return dot(ry[...], z[0]) + dot(ry[...], z[1])

    for g in range(planes // per):
        at = slice(g * per, (g + 1) * per)
        x = th[at].reshape(per * ny, nz)
        fy = split(flow(1, g * per) * x)
        fz = split(flow(2, g * per) * x)
        acc[at] = (dot3(ky, fy) + dot3(fz, kz)).reshape(per, ny, nz) - kappa * lap[at]
    for g in range((planes + 4) // per):
        f = flow(0, g * per - 2).reshape(per, ny, nz)
        for i in range(per):
            p = g * per - 2 + i
            if p < 0:
                t, d = tl[p + 2].astype(jnp.float32), pay_l[p + 2].astype(jnp.float32)
            elif p >= planes:
                t, d = tr[p - planes].astype(jnp.float32), pay_r[p - planes].astype(jnp.float32)
            else:
                t, d = th[p], gx[p]
            flux[p + 2] = f[i] * t - kappa * d

    def put(i, value):
        kept = RK_A * reg[i] - STEP * (value + acc[i])
        saved[i] = kept
        new[i] = th[i] + RK_B * kept

    x_derivative(lambda p: flux[p + 2], put, saved, planes)


def shards(theta, register, velocity, diffusivity):
    planes, ny, nz = theta.shape[1:]
    nslab, ngrp = lax.axis_size("slab"), lax.axis_size("grp")
    nyc, nzc = ny // 2, nz // 2
    per = max(1, MXU // ny)
    f32, bf16 = jnp.float32, jnp.bfloat16
    up = [(i, (i + 1) % nslab) for i in range(nslab)]
    down = [((i + 1) % nslab, i) for i in range(nslab)]
    op_y, op_z = blocked_operator(ny, BLK), blocked_operator(nz, BLK)
    eye = np.eye(per)
    ky2, kz2 = host_split(np.kron(eye, op_y @ op_y)), host_split((op_z @ op_z).T)
    ky, kz = host_split(np.kron(eye, op_y)), host_split(op_z.T)
    ry = jnp.asarray(np.kron(eye, refine_operator(nyc)), bf16)
    rz = jnp.asarray(refine_operator(nzc).T, bf16)

    field, saved = theta[0], register[0]
    head = field[:2].astype(bf16)
    tail = field[planes - 2 :].astype(bf16)
    left = lax.ppermute(tail, "slab", up)
    right = lax.ppermute(head, "slab", down)
    parts = [velocity]
    for s in range(1, ngrp):
        parts.append(lax.ppermute(velocity, "grp", [(i, (i + s) % ngrp) for i in range(ngrp)]))
    full = jax.ShapeDtypeStruct((planes, ny, nz), f32)
    vmem = pl.BlockSpec(memory_space=pltpu.VMEM)
    smem = pl.BlockSpec(memory_space=pltpu.SMEM)
    params = pltpu.CompilerParams(vmem_limit_bytes=30 * 1024 * 1024)
    lap = pl.pallas_call(
        second_kernel, out_shape=full, in_specs=[vmem] * 3, out_specs=vmem, compiler_params=params, name="second"
    )(field, ky2, kz2)
    part = lax.axis_index("grp").astype(jnp.int32)[None]
    pay = jax.ShapeDtypeStruct((4, ny, nz), bf16)
    gx, vel, tail, head = pl.pallas_call(
        first_kernel,
        out_shape=(full, jax.ShapeDtypeStruct((3, planes // 2, nyc, nzc), f32), pay, pay),
        in_specs=[smem] + [vmem] * (3 + ngrp),
        out_specs=(vmem,) * 4,
        scratch_shapes=[pltpu.VMEM((planes, ny, nz), f32)],
        compiler_params=params,
        name="first",
    )(part, field, left, right, *parts)
    pay_l = lax.ppermute(tail, "slab", up)
    pay_r = lax.ppermute(head, "slab", down)
    new, kept = pl.pallas_call(
        final_kernel,
        out_shape=(full, full),
        in_specs=[smem] + [vmem] * 13,
        out_specs=(vmem,) * 2,
        scratch_shapes=[pltpu.VMEM((planes + 4, ny, nz), f32), pltpu.VMEM((planes, ny, nz), f32)],
        compiler_params=params,
        name="final",
    )(diffusivity, field, saved, lap, gx, left, right, pay_l, pay_r, vel, ky, kz, ry, rz)
    return (new[None], kept[None])


def solution(mesh):
    in_specs = (
        P("grp", "slab", None, None),
        P("grp", "slab", None, None),
        P(None, "slab", "grp", None),
        P("grp"),
    )
    out_specs = (P("grp", "slab", None, None), P("grp", "slab", None, None))
    return jax.shard_map(shards, mesh=mesh, in_specs=in_specs, out_specs=out_specs, check_vma=False)
```

time: 87.5 us -> 29.5 us (0.34)
  local copies, waits for them, and re-layouts: 24.9 us -> 0.06 us
  other arithmetic: 23.9 us -> 1.37 us
  matrix products: 13.7 us -> 0 us
  Pallas kernels: 0 us -> 7.27 us
  blocking collectives: 7.23 us -> 0 us
  starting transfers between devices: 11.7 us -> 14.1 us
  waiting for transfers between devices: 4.05 us -> 5.09 us
    another operation x16 -> x1, other arithmetic: 17.4 us -> 1.37 us  [the longest x6 6.74 us: refine(): stacked = jnp.stack([even, odd], axis=axis + 1)]
    dot_general x8 -> x0, matrix products: 13 us -> none  [the longest x2 4.7 us: x_block(): jnp.einsum('ij,jyz->iyz', inverse, rhs, precision=lax.Precision.HIGHEST)]
    slice x8 -> x0, local copies, waits for them, and re-layouts: 10.6 us -> none  [the longest x1 3.07 us: shards(): flux_z = flow[2] * field - kappa * grad_z]
    pallas_call x0 -> x3, Pallas kernels: none -> 7.27 us  [the longest x1 5.62 us: shards(): pl.pallas_call(final_kernel, out_shape=(full, full), in_specs=[smem] + [v...]
    all_gather x1 -> x0, blocking collectives: 7.23 us -> none  [shards(): whole_y = lax.all_gather(velocity, 'grp', axis=2, tiled=True)]
    squeeze x3 -> x0, local copies, waits for them, and re-layouts: 7.13 us -> none  [the longest x1 2.51 us: shards(): flux_x = flow[0] * field - kappa * grad_x]
    unnamed x17 -> x18, local copies, waits for them, and re-layouts: 5.78 us -> 0.05 us
    sub x1 -> x0, other arithmetic: 3.81 us -> none  [shards(): flux_y = flow[1] * field - kappa * grad_y]
  transfers between devices with their start and end apart: 6 -> 7, of which waited for: 1 -> 5; matrix products, arithmetic and copies ran while one was open for 59% -> 0% of each run, Pallas kernels for 0% -> 3%
where the time goes in v1:
time: 29.5 us; the launch traced here: 29.3 us
  starting transfers between devices  14.1 us (48%)
  Pallas kernels  7.27 us (25%)
  waiting for transfers between devices  5.09 us (17%)
  between operations  1.42 us (5%)
  other arithmetic  1.37 us (5%)
    ppermute x1, starting transfers between devices, shards(): right = lax.ppermute(head, 'slab', down)  6.09 us
    pallas_call x1, Pallas kernels, shards(): pl.pallas_call(final_kernel, out_shape=(full, full), in_specs=[smem] + [v...  5.62 us
    ppermute x1, starting transfers between devices, shards(): pay_r = lax.ppermute(head, 'slab', down)  4.71 us
    ppermute x3, starting transfers between devices, shards(): lax.ppermute(velocity, 'grp', [(i, (i + s) % ngrp) for i in range(ngrp)])  3.24 us
    ppermute x1, waiting for transfers between devices, shards(): left = lax.ppermute(tail, 'slab', up)  1.94 us
    ppermute x3, waiting for transfers between devices, shards(): lax.ppermute(velocity, 'grp', [(i, (i + s) % ngrp) for i in range(ngrp)])  1.77 us
    another operation x1, other arithmetic  1.37 us
    ppermute x1, waiting for transfers between devices, shards(): pay_l = lax.ppermute(tail, 'slab', up)  1.2 us
  transfers between devices with their start and end apart: 7, of which 5 were waited for; matrix products, arithmetic and copies ran while one was open for 0% of the time, Pallas kernels for 3%

profile of v1, /device:TPU:0, one launch (start us, length us, event | category | flops | bytes accessed | tf_op | source)
XLA Modules:
  0.0 29.3 jit_solution(15369646837007245918)
XLA Ops:
  0.6 1.4 %convert.4 = bf16[1,16,64,256]{3,2,1,0:T(8,128)(2,1)S(1)} convert(f32[1,16,64,256]{3,2,1,0:T(8,128)} %param.10) | non-fusion elementwise | flops 262144 | bytes 1572864 | tf_op jit(solution)/shard_map/convert.1
  2.0 0.0 copy-start.8
  2.1 6.1 %collective-permute-start.1 = (bf16[2,64,256]{2,1,0:T(8,128)(2,1)S(1)}, bf16[2,64,256]{2,1,0:T(8,128)(2,1)S(1)}, u32[]{:S(2)}, u32[]{:S(2)}) collective-permute-start(bf16[2,64,256]{2,1,0:T(8,128)(2,1)S(1)} %get-tuple-element.14), channel_id=1, source_target_pairs={{1,0},{2,1},{3,2},{4,3},{5,4},{6,5},{7,6},{0,7},{9,8},{10,9},{11,1... | collective-permute-start | bytes 196616 | tf_op jit(solution)/shard_map/ppermute | solution.py:215
  8.1 0.0 collective-permute-start
  8.1 1.5 %collective-permute-start.3 = (bf16[3,8,8,128]{3,2,1,0:T(8,128)(2,1)S(1)}, bf16[3,8,8,128]{3,2,1,0:T(8,128)(2,1)S(1)}, u32[]{:S(2)}, u32[]{:S(2)}) collective-permute-start(bf16[3,8,8,128]{3,2,1,0:T(8,128)(2,1)S(1)} %copy-done.8), channel_id=1, source_target_pairs={{0,16},{8,24},{16,0},{24,8},{1,17},{9,25},{17,1},{25,9},{2,18},{10... | collective-permute-start | bytes 147464 | tf_op jit(solution)/shard_map/ppermute | solution.py:218
  9.6 0.0 collective-permute-start.2
  9.6 1.7 %collective-permute-start.4 = (bf16[3,8,8,128]{3,2,1,0:T(8,128)(2,1)S(1)}, bf16[3,8,8,128]{3,2,1,0:T(8,128)(2,1)S(1)}, u32[]{:S(2)}, u32[]{:S(2)}) collective-permute-start(bf16[3,8,8,128]{3,2,1,0:T(8,128)(2,1)S(1)} %copy-done.8), channel_id=1, source_target_pairs={{0,24},{8,0},{16,8},{24,16},{1,25},{9,1},{17,9},{25,17},{2,26},{10... | collective-permute-start | bytes 147464 | tf_op jit(solution)/shard_map/ppermute | solution.py:218
  11.4 0.9 %collective-permute-done.3.refs_2_ = bf16[3,8,8,128]{3,2,1,0:T(8,128)(2,1)S(1)} collective-permute-done((bf16[3,8,8,128]{3,2,1,0:T(8,128)(2,1)S(1)}, bf16[3,8,8,128]{3,2,1,0:T(8,128)(2,1)S(1)}, u32[]{:S(2)}, u32[]{:S(2)}) %collective-permute-start.3) | collective-permute-done | bytes 49184 | tf_op jit(solution)/shard_map/ppermute | solution.py:218
  12.2 0.9 %collective-permute-done.2.refs_1_ = bf16[3,8,8,128]{3,2,1,0:T(8,128)(2,1)S(1)} collective-permute-done((bf16[3,8,8,128]{3,2,1,0:T(8,128)(2,1)S(1)}, bf16[3,8,8,128]{3,2,1,0:T(8,128)(2,1)S(1)}, u32[]{:S(2)}, u32[]{:S(2)}) %collective-permute-start.2) | collective-permute-done | bytes 49184 | tf_op jit(solution)/shard_map/ppermute | solution.py:218
  13.2 0.0 collective-permute-done.4.refs_3_
  13.2 0.0 collective-permute-done.1.tr
  13.2 1.9 %collective-permute-done.tl = bf16[2,64,256]{2,1,0:T(8,128)(2,1)S(1)} collective-permute-done((bf16[2,64,256]{2,1,0:T(8,128)(2,1)S(1)}, bf16[2,64,256]{2,1,0:T(8,128)(2,1)S(1)}, u32[]{:S(2)}, u32[]{:S(2)}) %collective-permute-start) | collective-permute-done | bytes 65568 | tf_op jit(solution)/shard_map/ppermute | solution.py:214
  15.1 0.6 %first.1 = (f32[16,64,256]{2,1,0:T(8,128)S(1)}, f32[3,8,32,128]{3,2,1,0:T(8,128)S(1)}, bf16[4,64,256]{2,1,0:T(8,128)(2,1)S(1)}, bf16[4,64,256]{2,1,0:T(8,128)(2,1)S(1)}) custom-call(s32[1]{0:T(128)} %bitcast.2.part, f32[16,64,256]{2,1,0:T(8,128)S(1)} %bitcast.9, bf16[2,64,256]{2,1,0:T(8,128)(2,1)S(1)} %collective-permute-done.tl, ...), custom_call_target="tpu_custom_call" | custom-call | tf_op jit(solution)/shard_map/first/pallas_call | solution.py:228
  15.8 0.1 collective-permute-start.5
  15.8 4.7 %collective-permute-start.6 = (bf16[4,64,256]{2,1,0:T(8,128)(2,1)S(1)}, bf16[4,64,256]{2,1,0:T(8,128)(2,1)S(1)}, u32[]{:S(2)}, u32[]{:S(2)}) collective-permute-start(bf16[4,64,256]{2,1,0:T(8,128)(2,1)S(1)} %get-tuple-element.10), channel_id=1, source_target_pairs={{1,0},{2,1},{3,2},{4,3},{5,4},{6,5},{7,6},{0,7},{9,8},{10,9},{11,1... | collective-permute-start | bytes 393224 | tf_op jit(solution)/shard_map/ppermute | solution.py:238
  21.2 0.0 copy-start.1
  21.2 0.0 copy-start.2
  21.2 0.0 copy-start.3
  21.2 0.0 copy-start.6
  21.3 0.0 copy-start.7
  21.3 1.0 %second.1.lap = f32[16,64,256]{2,1,0:T(8,128)S(1)} custom-call(f32[16,64,256]{2,1,0:T(8,128)S(1)} %bitcast.10, bf16[2,256,256]{2,1,0:T(8,128)(2,1)S(1)} %copy-done.5, bf16[2,256,256]{2,1,0:T(8,128)(2,1)S(1)} %copy-done.4), custom_call_target="tpu_custom_call" | custom-call | tf_op jit(solution)/shard_map/second/pallas_call | solution.py:223
  22.3 1.2 %collective-permute-done.5.pay_l = bf16[4,64,256]{2,1,0:T(8,128)(2,1)S(1)} collective-permute-done((bf16[4,64,256]{2,1,0:T(8,128)(2,1)S(1)}, bf16[4,64,256]{2,1,0:T(8,128)(2,1)S(1)}, u32[]{:S(2)}, u32[]{:S(2)}) %collective-permute-start.5) | collective-permute-done | bytes 131104 | tf_op jit(solution)/shard_map/ppermute | solution.py:237
  23.5 0.2 collective-permute-done.6.pay_r
  23.7 5.6 %final.1 = (f32[16,64,256]{2,1,0:T(8,128)}, f32[16,64,256]{2,1,0:T(8,128)}) custom-call(f32[1]{0:T(128)S(6)} %copy.12.kap, f32[16,64,256]{2,1,0:T(8,128)S(1)} %bitcast.11, f32[16,64,256]{2,1,0:T(8,128)S(1)} %bitcast.12, f32[16,64,256]{2,1,0:T(8,128)S(1)} %second.1.lap, f32[16,64,256]{2,1,0:T(8,128)S(1)} %get-tuple-element.8.gx, ...), custom_call_target="tpu_custom_call" | custom-call | tf_op jit(solution)/shard_map/final/pallas_call | solution.py:239
  (13 shorter events, 0.0 us)
Async XLA Ops:
  0.6 14.5 %copy-start = (f32[1,16,64,256]{3,2,1,0:T(8,128)S(1)}, f32[1,16,64,256]{3,2,1,0:T(8,128)}, u32[]{:S(2)}) copy-start(f32[1,16,64,256]{3,2,1,0:T(8,128)} %param.10) | copy-start | bytes 3145732
  2.0 6.1 %copy-start.8 = (bf16[3,8,8,128]{3,2,1,0:T(8,128)(2,1)S(1)}, bf16[3,8,8,128]{3,2,1,0:T(8,128)(2,1)}, u32[]{:S(2)}) copy-start(bf16[3,8,8,128]{3,2,1,0:T(8,128)(2,1)} %refs_0_.1) | copy-start | bytes 147460
  2.1 11.1 %collective-permute-start.1 = (bf16[2,64,256]{2,1,0:T(8,128)(2,1)S(1)}, bf16[2,64,256]{2,1,0:T(8,128)(2,1)S(1)}, u32[]{:S(2)}, u32[]{:S(2)}) collective-permute-start(bf16[2,64,256]{2,1,0:T(8,128)(2,1)S(1)} %get-tuple-element.14), channel_id=1, source_target_pairs={{1,0},{2,1},{3,2},{4,3},{5,4},{6,5},{7,6},{0,7},{9,8},{10,9},{11,1... | collective-permute-start | bytes 196616 | tf_op jit(solution)/shard_map/ppermute | solution.py:215
  8.1 7.0 %collective-permute-start = (bf16[2,64,256]{2,1,0:T(8,128)(2,1)S(1)}, bf16[2,64,256]{2,1,0:T(8,128)(2,1)S(1)}, u32[]{:S(2)}, u32[]{:S(2)}) collective-permute-start(bf16[2,64,256]{2,1,0:T(8,128)(2,1)S(1)} %get-tuple-element.15), channel_id=1, source_target_pairs={{0,1},{1,2},{2,3},{3,4},{4,5},{5,6},{6,7},{7,0},{8,9},{9,10},{10,1... | collective-permute-start | bytes 196616 | tf_op jit(solution)/shard_map/ppermute | solution.py:214
  8.1 4.1 %collective-permute-start.3 = (bf16[3,8,8,128]{3,2,1,0:T(8,128)(2,1)S(1)}, bf16[3,8,8,128]{3,2,1,0:T(8,128)(2,1)S(1)}, u32[]{:S(2)}, u32[]{:S(2)}) collective-permute-start(bf16[3,8,8,128]{3,2,1,0:T(8,128)(2,1)S(1)} %copy-done.8), channel_id=1, source_target_pairs={{0,16},{8,24},{16,0},{24,8},{1,17},{9,25},{17,1},{25,9},{2,18},{10... | collective-permute-start | bytes 147464 | tf_op jit(solution)/shard_map/ppermute | solution.py:218
  9.6 3.5 %collective-permute-start.2 = (bf16[3,8,8,128]{3,2,1,0:T(8,128)(2,1)S(1)}, bf16[3,8,8,128]{3,2,1,0:T(8,128)(2,1)S(1)}, u32[]{:S(2)}, u32[]{:S(2)}) collective-permute-start(bf16[3,8,8,128]{3,2,1,0:T(8,128)(2,1)S(1)} %copy-done.8), channel_id=1, source_target_pairs={{0,8},{8,16},{16,24},{24,0},{1,9},{9,17},{17,25},{25,1},{2,10},{10... | collective-permute-start | bytes 147464 | tf_op jit(solution)/shard_map/ppermute | solution.py:218
  9.6 3.5 %collective-permute-start.4 = (bf16[3,8,8,128]{3,2,1,0:T(8,128)(2,1)S(1)}, bf16[3,8,8,128]{3,2,1,0:T(8,128)(2,1)S(1)}, u32[]{:S(2)}, u32[]{:S(2)}) collective-permute-start(bf16[3,8,8,128]{3,2,1,0:T(8,128)(2,1)S(1)} %copy-done.8), channel_id=1, source_target_pairs={{0,24},{8,0},{16,8},{24,16},{1,25},{9,1},{17,9},{25,17},{2,26},{10... | collective-permute-start | bytes 147464 | tf_op jit(solution)/shard_map/ppermute | solution.py:218
  15.1 6.1 %copy-start.4 = (bf16[2,256,256]{2,1,0:T(8,128)(2,1)S(1)}, bf16[2,256,256]{2,1,0:T(8,128)(2,1)}, u32[]{:S(2)}) copy-start(bf16[2,256,256]{2,1,0:T(8,128)(2,1)} %constant.39.kz2) | copy-start | bytes 786436
  15.1 6.1 %copy-start.5 = (bf16[2,256,256]{2,1,0:T(8,128)(2,1)S(1)}, bf16[2,256,256]{2,1,0:T(8,128)(2,1)}, u32[]{:S(2)}) copy-start(bf16[2,256,256]{2,1,0:T(8,128)(2,1)} %constant.32.ky2) | copy-start | bytes 786436
  15.8 7.7 %collective-permute-start.5 = (bf16[4,64,256]{2,1,0:T(8,128)(2,1)S(1)}, bf16[4,64,256]{2,1,0:T(8,128)(2,1)S(1)}, u32[]{:S(2)}, u32[]{:S(2)}) collective-permute-start(bf16[4,64,256]{2,1,0:T(8,128)(2,1)S(1)} %get-tuple-element.9), channel_id=1, source_target_pairs={{0,1},{1,2},{2,3},{3,4},{4,5},{5,6},{6,7},{7,0},{8,9},{9,10},{10,1... | collective-permute-start | bytes 393224 | tf_op jit(solution)/shard_map/ppermute | solution.py:237
  15.8 7.8 %collective-permute-start.6 = (bf16[4,64,256]{2,1,0:T(8,128)(2,1)S(1)}, bf16[4,64,256]{2,1,0:T(8,128)(2,1)S(1)}, u32[]{:S(2)}, u32[]{:S(2)}) collective-permute-start(bf16[4,64,256]{2,1,0:T(8,128)(2,1)S(1)} %get-tuple-element.10), channel_id=1, source_target_pairs={{1,0},{2,1},{3,2},{4,3},{5,4},{6,5},{7,6},{0,7},{9,8},{10,9},{11,1... | collective-permute-start | bytes 393224 | tf_op jit(solution)/shard_map/ppermute | solution.py:238
  21.2 2.5 %copy-start.1 = (f32[1,16,64,256]{3,2,1,0:T(8,128)S(1)}, f32[1,16,64,256]{3,2,1,0:T(8,128)}, u32[]{:S(2)}) copy-start(f32[1,16,64,256]{3,2,1,0:T(8,128)} %param.11) | copy-start | bytes 3145732
  21.2 2.4 %copy-start.2 = (bf16[2,256,256]{2,1,0:T(8,128)(2,1)S(1)}, bf16[2,256,256]{2,1,0:T(8,128)(2,1)}, u32[]{:S(2)}) copy-start(bf16[2,256,256]{2,1,0:T(8,128)(2,1)} %constant.53.kz) | copy-start | bytes 786436
  21.2 2.4 %copy-start.3 = (bf16[2,256,256]{2,1,0:T(8,128)(2,1)S(1)}, bf16[2,256,256]{2,1,0:T(8,128)(2,1)}, u32[]{:S(2)}) copy-start(bf16[2,256,256]{2,1,0:T(8,128)(2,1)} %constant.46.ky) | copy-start | bytes 786436
  21.2 2.4 %copy-start.6 = (bf16[128,256]{1,0:T(8,128)(2,1)S(1)}, bf16[128,256]{1,0:T(8,128)(2,1)}, u32[]{:S(2)}) copy-start(bf16[128,256]{1,0:T(8,128)(2,1)} %constant.22.clone.rz) | copy-start | bytes 196612
  21.3 2.4 %copy-start.7 = (bf16[256,128]{1,0:T(8,128)(2,1)S(1)}, bf16[256,128]{1,0:T(8,128)(2,1)}, u32[]{:S(2)}) copy-start(bf16[256,128]{1,0:T(8,128)(2,1)} %constant.21.clone.ry) | copy-start | bytes 196612

commit v2 on v1

v2 whole, which is shorter than its diff:
```python
import jax
import jax.numpy as jnp
import numpy as np
from jax import lax
from jax.experimental import pallas as pl
from jax.experimental.pallas import tpu as pltpu
from jax.sharding import PartitionSpec as P

BLK = 32
ALPHA = 4.0 / 9.0
BETA = 1.0 / 36.0
COEF_A = 40.0 / 27.0
COEF_B = 25.0 / 54.0
RK_A = -5.0 / 9.0
RK_B = 15.0 / 16.0
STEP = 0.2
EVEN = (-0.0390625, 0.2734375, 0.8203125, -0.0546875)
ODD = (-0.0546875, 0.8203125, 0.2734375, -0.0390625)
MXU = 256


def band(count):
    eye = lambda k: np.eye(count, k=k)
    return eye(0) + ALPHA * (eye(1) + eye(-1)) + BETA * (eye(2) + eye(-2))


def blocked_operator(count, block):
    rhs = np.zeros((count, count))
    for i in range(count):
        for shift, coef in ((1, COEF_A / 2), (-1, -COEF_A / 2), (2, COEF_B / 4), (-2, -COEF_B / 4)):
            rhs[i, (i + shift) % count] += coef
    return np.kron(np.eye(count // block), np.linalg.inv(band(block))) @ rhs


def refine_operator(count):
    out = np.zeros((2 * count, count))
    for k in range(count):
        for t in range(4):
            out[2 * k, (k - 2 + t) % count] += EVEN[t]
            out[2 * k + 1, (k - 1 + t) % count] += ODD[t]
    return out


def split(x):
    hi = x.astype(jnp.bfloat16)
    return hi, (x - hi.astype(jnp.float32)).astype(jnp.bfloat16)


def host_split(x):
    x = jnp.asarray(np.asarray(x, np.float32))
    return jnp.stack(split(x))


def dot(a, b):
    return jnp.dot(a, b, preferred_element_type=jnp.float32)


def dot3(a, b):
    return dot(a[0], b[0]) + (dot(a[0], b[1]) + dot(a[1], b[0]))


def banded_lu(count):
    m = band(count)
    for k in range(count):
        for i in range(k + 1, min(k + 3, count)):
            m[i, k] /= m[k, k]
            m[i, k + 1 : min(k + 3, count)] -= m[i, k] * m[k, k + 1 : min(k + 3, count)]
    return m


def x_derivative(get, put, work, planes):
    m = banded_lu(planes)
    ratio = (COEF_B / 4) / (COEF_A / 2)
    y1 = y2 = None
    for i in range(planes):
        y = (get(i + 1) - get(i - 1)) + ratio * (get(i + 2) - get(i - 2))
        if i >= 1:
            y = y - float(m[i, i - 1]) * y1
        if i >= 2:
            y = y - float(m[i, i - 2]) * y2
        work[i] = y
        y1, y2 = y, y1
    x1 = x2 = None
    for i in reversed(range(planes)):
        inv = 1.0 / m[i, i]
        x = work[i] * float(inv * COEF_A / 2)
        if i + 1 < planes:
            x = x - float(m[i, i + 1] * inv) * x1
        if i + 2 < planes:
            x = x - float(m[i, i + 2] * inv) * x2
        put(i, x)
        x1, x2 = x, x1


SLOTS = ((0, 0), (0, 1), (0, 2), (1, 0), (1, 1), (2, 0), (2, 1))
FIRST, COUNT = (0, 3, 5), (3, 2, 2)


def pack_kernel(low, high, vel, head, tail):
    ny, nz = low.shape[2:]
    coarse, rows, nzc = vel.shape[1:]
    for out, edge, upper in ((head, low, False), (tail, high, True)):
        out[: 2 * ny] = edge[0].reshape(2 * ny, nz).astype(jnp.bfloat16)
        for q in range(8):
            c, k = SLOTS[min(q, 6)]
            k = coarse - COUNT[c] + k if upper else k
            top = 2 * ny + rows * (q // 2)
            out[top : top + rows, nzc * (q % 2) : nzc * (q % 2 + 1)] = vel[c, k]


def padded(th, tl, tr):
    planes, ny = th.shape[:2]

    def get(p):
        if p < 0:
            return tl[ny * (p + 2) : ny * (p + 3)].astype(jnp.float32)
        if p >= planes:
            return tr[ny * (p - planes) : ny * (p - planes + 1)].astype(jnp.float32)
        return th[p]

    return get


def first_kernel(th, tl, tr, gx, halo, tail, head, work):
    planes, ny, nz = th.shape

    def put(i, value):
        gx[i] = value
        if i < 2:
            head[i] = value.astype(jnp.bfloat16)
        if i >= planes - 2:
            tail[i - (planes - 2)] = value.astype(jnp.bfloat16)

    halo[0] = tl[2 * ny :]
    halo[1] = tr[2 * ny :]
    x_derivative(padded(th, tl, tr), put, work, planes)


def flow_of(vel, halo, ry, rz):
    ngrp, _, coarse, rows, nzc = vel.shape

    def plane(c, k):
        if 0 <= k < coarse:
            got = [vel[g, c, k] for g in range(ngrp)]
        else:
            q = FIRST[c] + (COUNT[c] + k if k < 0 else k - coarse)
            top = rows * (q // 2)
            side = 0 if k < 0 else 1
            got = [halo[g, side, top : top + rows, nzc * (q % 2) : nzc * (q % 2 + 1)] for g in range(ngrp)]
        return jnp.concatenate([v.astype(jnp.float32) for v in got], axis=0)

    def fine(c, p):
        k = p // 2
        coefs, start = (EVEN, k - 2) if p % 2 == 0 else (ODD, k - 1)
        total = coefs[0] * plane(c, start)
        for t in range(1, 4):
            total = total + coefs[t] * plane(c, start + t)
        return total

    def flow(c, which):
        x = split(jnp.concatenate([fine(c, p) for p in which], axis=0))
        z = split(dot(x[0], rz[...]) + dot(x[1], rz[...]))
        return dot(ry[...], z[0]) + dot(ry[...], z[1])

    return flow


def is_inner(g, per, planes):
    return g * per >= 4 and (g + 1) * per <= planes - 4


def cross(flow, th, ky, kz, g, per):
    ny, nz = th.shape[1:]
    which = range(g * per, (g + 1) * per)
    x = th[g * per : (g + 1) * per].reshape(per * ny, nz)
    fy = split(flow(1, which) * x)
    fz = split(flow(2, which) * x)
    return (dot3(ky, fy) + dot3(fz, kz)).reshape(per, ny, nz)


def inner_kernel(kap, th, gx, vel, ky, kz, ky2, kz2, ry, rz, acc, flux):
    planes, ny, nz = th.shape
    per = ky.shape[1] // ny
    kappa = kap[0]
    flow = flow_of(vel, None, ry, rz)
    for g in range(planes // per):
        at = slice(g * per, (g + 1) * per)
        x = split(th[at].reshape(per * ny, nz))
        value = -kappa * (dot3(ky2, x) + dot3(x, kz2)).reshape(per, ny, nz)
        if is_inner(g, per, planes):
            value = value + cross(flow, th, ky, kz, g, per)
            flux[at] = flow(0, range(g * per, (g + 1) * per)).reshape(per, ny, nz) * th[at] - kappa * gx[at]
        acc[at] = value


def final_kernel(kap, th, reg, part, inner, gx, tl, tr, gl, gr, vel, halo, ky, kz, ry, rz, new, saved, flux, acc):
    planes, ny, nz = th.shape
    per = ky.shape[1] // ny
    kappa = kap[0]
    flow = flow_of(vel, halo, ry, rz)
    get = padded(th, tl, tr)
    outer = [g for g in range(planes // per) if not is_inner(g, per, planes)]
    for g in outer:
        acc[g * per : (g + 1) * per] = cross(flow, th, ky, kz, g, per) + part[g * per : (g + 1) * per]
    todo = [p for p in range(-2, planes + 2) if not is_inner(p // per, per, planes)]
    for start in range(0, len(todo), per):
        which = todo[start : start + per]
        f = flow(0, which + which[:1] * (per - len(which))).reshape(per, ny, nz)
        for i, p in enumerate(which):
            if p < 0:
                d = gl[p + 2].astype(jnp.float32)
            elif p >= planes:
                d = gr[p - planes].astype(jnp.float32)
            else:
                d = gx[p]
            flux[p + 2] = f[i] * get(p) - kappa * d

    def flux_at(p):
        return inner[p] if is_inner(p // per, per, planes) else flux[p + 2]

    def put(i, value):
        rest = part[i] if is_inner(i // per, per, planes) else acc[i]
        kept = RK_A * reg[i] - STEP * (value + rest)
        saved[i] = kept
        new[i] = th[i] + RK_B * kept

    x_derivative(flux_at, put, saved, planes)


def shards(theta, register, velocity, diffusivity):
    planes, ny, nz = theta.shape[1:]
    nslab, ngrp = lax.axis_size("slab"), lax.axis_size("grp")
    nyc, nzc = ny // 2, nz // 2
    per = max(1, MXU // ny)
    f32, bf16 = jnp.float32, jnp.bfloat16
    up = [(i, (i + 1) % nslab) for i in range(nslab)]
    down = [((i + 1) % nslab, i) for i in range(nslab)]
    op_y, op_z = blocked_operator(ny, BLK), blocked_operator(nz, BLK)
    eye = np.eye(per)
    ky2, kz2 = host_split(np.kron(eye, op_y @ op_y)), host_split((op_z @ op_z).T)
    ky, kz = host_split(np.kron(eye, op_y)), host_split(op_z.T)
    ry = jnp.asarray(np.kron(eye, refine_operator(nyc)), bf16)
    rz = jnp.asarray(refine_operator(nzc).T, bf16)

    field, saved = theta[0], register[0]
    rows, coarse = velocity.shape[2], planes // 2
    full = jax.ShapeDtypeStruct((planes, ny, nz), f32)
    edge = jax.ShapeDtypeStruct((2, ny, nz), bf16)
    packed = jax.ShapeDtypeStruct((2 * ny + 4 * rows, nz), bf16)
    vmem = pl.BlockSpec(memory_space=pltpu.VMEM)
    smem = pl.BlockSpec(memory_space=pltpu.SMEM)
    params = pltpu.CompilerParams(vmem_limit_bytes=30 * 1024 * 1024)

    whole = lambda shape: pl.BlockSpec(shape, lambda i: (0,) * len(shape))
    head, tail = pl.pallas_call(
        pack_kernel,
        out_shape=(packed, packed),
        grid=(1,),
        in_specs=[
            pl.BlockSpec((1, 2, ny, nz), lambda i: (0, 0, 0, 0)),
            pl.BlockSpec((1, 2, ny, nz), lambda i: (0, planes // 2 - 1, 0, 0)),
            whole(velocity.shape),
        ],
        out_specs=(whole(packed.shape),) * 2,
        name="pack",
    )(theta, theta, velocity)
    left = lax.ppermute(tail, "slab", up)
    right = lax.ppermute(head, "slab", down)
    vel = lax.all_gather(velocity, "grp", axis=0, tiled=False)
    gx, halo, tail, head = pl.pallas_call(
        first_kernel,
        out_shape=(full, jax.ShapeDtypeStruct((2, 4 * rows, nz), bf16), edge, edge),
        in_specs=[vmem] * 3,
        out_specs=(vmem,) * 4,
        scratch_shapes=[pltpu.VMEM((planes, ny, nz), f32)],
        compiler_params=params,
        name="first",
    )(field, left, right)
    grad_l = lax.ppermute(tail, "slab", up)
    grad_r = lax.ppermute(head, "slab", down)
    halo = lax.all_gather(halo, "grp", axis=0, tiled=False)
    acc, inner = pl.pallas_call(
        inner_kernel,
        out_shape=(full, full),
        in_specs=[smem] + [vmem] * 9,
        out_specs=(vmem,) * 2,
        compiler_params=params,
        name="inner",
    )(diffusivity, field, gx, vel, ky, kz, ky2, kz2, ry, rz)
    new, kept = pl.pallas_call(
        final_kernel,
        out_shape=(full, full),
        in_specs=[smem] + [vmem] * 15,
        out_specs=(vmem,) * 2,
        scratch_shapes=[pltpu.VMEM((planes + 4, ny, nz), f32), pltpu.VMEM((planes, ny, nz), f32)],
        compiler_params=params,
        name="final",
    )(diffusivity, field, saved, acc, inner, gx, left, right, grad_l, grad_r, vel, halo, ky, kz, ry, rz)
    return (new[None], kept[None])


def solution(mesh):
    in_specs = (
        P("grp", "slab", None, None),
        P("grp", "slab", None, None),
        P(None, "slab", "grp", None),
        P("grp"),
    )
    out_specs = (P("grp", "slab", None, None), P("grp", "slab", None, None))
    return jax.shard_map(shards, mesh=mesh, in_specs=in_specs, out_specs=out_specs, check_vma=False)
```

time: 29.5 us -> 35.9 us (1.22)
  blocking collectives: 0 us -> 11 us
  starting transfers between devices: 14.1 us -> 10.8 us
  Pallas kernels: 7.27 us -> 9.11 us
  waiting for transfers between devices: 5.09 us -> 3.37 us
  other arithmetic: 1.37 us -> 0 us
    all_gather x0 -> x2, blocking collectives: none -> 11 us  [the longest x1 5.58 us: shards(): vel = lax.all_gather(velocity, 'grp', axis=0, tiled=False)]
    pallas_call x2 -> x3, Pallas kernels: 1.65 us -> 5.12 us  [the longest x1 2.94 us: shards(): pl.pallas_call(inner_kernel, out_shape=(full, full), in_specs=[smem] + [v...]
    ppermute x5 -> x2, starting transfers between devices: 8.01 us -> 4.78 us  [the longest x1 4.06 us: shards(): grad_r = lax.ppermute(head, 'slab', down)]
    ppermute x5 -> x2, waiting for transfers between devices: 3.14 us -> 0.01 us  [the longest x1 0.01 us: shards(): grad_r = lax.ppermute(head, 'slab', down)]
    ppermute x1, starting transfers between devices: 6.09 us -> 3.04 us  [shards(): right = lax.ppermute(head, 'slab', down)]
    ppermute x1, starting transfers between devices: 0.01 us -> 3 us  [shards(): left = lax.ppermute(tail, 'slab', up)]
    pallas_call x1, Pallas kernels: 5.62 us -> 3.99 us  [shards(): pl.pallas_call(final_kernel, out_shape=(full, full), in_specs=[smem] + [v...]
    another operation x1 -> x0, other arithmetic: 1.37 us -> none
  transfers between devices with their start and end apart: 7 -> 4, of which waited for: 5 -> 2; matrix products, arithmetic and copies ran while one was open for 0% -> 0% of each run, Pallas kernels for 3% -> 8%
where the time goes in v2:
time: 35.9 us; the launch traced here: 35.7 us
  blocking collectives  11 us (31%)
  starting transfers between devices  10.8 us (30%)
  Pallas kernels  9.11 us (25%)
  waiting for transfers between devices  3.37 us (9%)
  between operations  1.39 us (4%)
    all_gather x1, blocking collectives, shards(): vel = lax.all_gather(velocity, 'grp', axis=0, tiled=False)  5.58 us
    all_gather x1, blocking collectives, shards(): halo = lax.all_gather(halo, 'grp', axis=0, tiled=False)  5.42 us
    ppermute x1, starting transfers between devices, shards(): grad_r = lax.ppermute(head, 'slab', down)  4.06 us
    pallas_call x1, Pallas kernels, shards(): pl.pallas_call(final_kernel, out_shape=(full, full), in_specs=[smem] + [v...  3.99 us
    ppermute x1, starting transfers between devices, shards(): right = lax.ppermute(head, 'slab', down)  3.04 us
    ppermute x1, starting transfers between devices, shards(): left = lax.ppermute(tail, 'slab', up)  3 us
    pallas_call x1, Pallas kernels, shards(): pl.pallas_call(inner_kernel, out_shape=(full, full), in_specs=[smem] + [v...  2.94 us
    ppermute x1, waiting for transfers between devices, shards(): left = lax.ppermute(tail, 'slab', up)  2.75 us
  transfers between devices with their start and end apart: 4, of which 2 were waited for; matrix products, arithmetic and copies ran while one was open for 0% of the time, Pallas kernels for 8%

profile of v2, /device:TPU:0, one launch (start us, length us, event | category | flops | bytes accessed | tf_op | source)
XLA Modules:
  0.0 35.7 jit_solution(17620147685123333655)
XLA Ops:
  0.6 0.0 copy-start
  0.6 1.7 %pack.1 = (bf16[160,256]{1,0:T(8,128)(2,1)}, bf16[160,256]{1,0:T(8,128)(2,1)}) custom-call(f32[1,16,64,256]{3,2,1,0:T(8,128)} %high.1, f32[1,16,64,256]{3,2,1,0:T(8,128)} %high.1, bf16[3,8,8,128]{3,2,1,0:T(8,128)(2,1)} %vel.1), custom_call_target="tpu_custom_call" | custom-call | tf_op jit(solution)/shard_map/pack/pallas_call | solution.py:255
  2.4 3.0 %collective-permute-start = (bf16[160,256]{1,0:T(8,128)(2,1)}, bf16[160,256]{1,0:T(8,128)(2,1)S(1)}, u32[]{:S(2)}, u32[]{:S(2)}) collective-permute-start(bf16[160,256]{1,0:T(8,128)(2,1)} %get-tuple-element.12), channel_id=1, source_target_pairs={{0,1},{1,2},{2,3},{3,4},{4,5},{5,6},{6,7},{7,0},{8,9},{9,10},{10,1... | collective-permute-start | bytes 245768 | tf_op jit(solution)/shard_map/ppermute | solution.py:267
  5.4 3.0 %collective-permute-start.1 = (bf16[160,256]{1,0:T(8,128)(2,1)}, bf16[160,256]{1,0:T(8,128)(2,1)S(1)}, u32[]{:S(2)}, u32[]{:S(2)}) collective-permute-start(bf16[160,256]{1,0:T(8,128)(2,1)} %get-tuple-element.13), channel_id=1, source_target_pairs={{1,0},{2,1},{3,2},{4,3},{5,4},{6,5},{7,6},{0,7},{9,8},{10,9},{11,1... | collective-permute-start | bytes 245768 | tf_op jit(solution)/shard_map/ppermute | solution.py:268
  8.4 2.7 %collective-permute-done.tl = bf16[160,256]{1,0:T(8,128)(2,1)S(1)} collective-permute-done((bf16[160,256]{1,0:T(8,128)(2,1)}, bf16[160,256]{1,0:T(8,128)(2,1)S(1)}, u32[]{:S(2)}, u32[]{:S(2)}) %collective-permute-start) | collective-permute-done | bytes 81952 | tf_op jit(solution)/shard_map/ppermute | solution.py:267
  11.2 0.6 %collective-permute-done.1.tr = bf16[160,256]{1,0:T(8,128)(2,1)S(1)} collective-permute-done((bf16[160,256]{1,0:T(8,128)(2,1)}, bf16[160,256]{1,0:T(8,128)(2,1)S(1)}, u32[]{:S(2)}, u32[]{:S(2)}) %collective-permute-start.1) | collective-permute-done | bytes 81952 | tf_op jit(solution)/shard_map/ppermute | solution.py:268
  11.8 0.0 copy-done
  11.8 0.0 copy-start.6
  11.8 0.0 copy-start.7
  11.8 0.5 %first.1 = (f32[16,64,256]{2,1,0:T(8,128)S(1)}, bf16[2,32,256]{2,1,0:T(8,128)(2,1)S(1)}, bf16[2,64,256]{2,1,0:T(8,128)(2,1)S(1)}, bf16[2,64,256]{2,1,0:T(8,128)(2,1)S(1)}) custom-call(f32[16,64,256]{2,1,0:T(8,128)S(1)} %bitcast.6, bf16[160,256]{1,0:T(8,128)(2,1)S(1)} %collective-permute-done.tl, bf16[160,256]{1,0:T(8,128)(2,1)S(1)} %collective-permute-done.1.tr), custom_call_target="tpu_custom_call" | custom-call | tf_op jit(solution)/shard_map/first/pallas_call | solution.py:270
  12.3 0.7 %collective-permute-start.2 = (bf16[2,64,256]{2,1,0:T(8,128)(2,1)S(1)}, bf16[2,64,256]{2,1,0:T(8,128)(2,1)S(1)}, u32[]{:S(2)}, u32[]{:S(2)}) collective-permute-start(bf16[2,64,256]{2,1,0:T(8,128)(2,1)S(1)} %get-tuple-element.17), channel_id=1, source_target_pairs={{0,1},{1,2},{2,3},{3,4},{4,5},{5,6},{6,7},{7,0},{8,9},{9,10},{10,1... | collective-permute-start | bytes 196616 | tf_op jit(solution)/shard_map/ppermute | solution.py:279
  13.0 4.1 %collective-permute-start.3 = (bf16[2,64,256]{2,1,0:T(8,128)(2,1)S(1)}, bf16[2,64,256]{2,1,0:T(8,128)(2,1)S(1)}, u32[]{:S(2)}, u32[]{:S(2)}) collective-permute-start(bf16[2,64,256]{2,1,0:T(8,128)(2,1)S(1)} %get-tuple-element.18), channel_id=1, source_target_pairs={{1,0},{2,1},{3,2},{4,3},{5,4},{6,5},{7,6},{0,7},{9,8},{10,9},{11,1... | collective-permute-start | bytes 196616 | tf_op jit(solution)/shard_map/ppermute | solution.py:280
  17.1 0.0 copy-done.8
  17.1 5.6 %all-gather = bf16[12,8,8,128]{3,2,1,0:T(8,128)(2,1)S(1)} all-gather(bf16[3,8,8,128]{3,2,1,0:T(8,128)(2,1)S(1)} %copy-done.8), channel_id=2, replica_groups=mesh['grp'=4,'slab'=8] {'grp'}, dimensions={0}, use_global_device_ids=true | all-gather | bytes 245760 | tf_op jit(solution)/shard_map/all_gather | solution.py:269
  23.3 0.0 copy-done.2
  23.3 0.0 copy-done.3
  23.3 0.0 copy-done.6
  23.3 0.0 copy-start.1
  23.4 2.9 %inner.1 = (f32[16,64,256]{2,1,0:T(8,128)S(1)}, f32[16,64,256]{2,1,0:T(8,128)S(1)}) custom-call(f32[1]{0:T(128)S(6)} %copy.12.kap, f32[16,64,256]{2,1,0:T(8,128)S(1)} %bitcast.7, f32[16,64,256]{2,1,0:T(8,128)S(1)} %get-tuple-element.14.gx, bf16[4,3,8,8,128]{4,3,2,1,0:T(8,128)(2,1)S(1)} %bitcast.9, bf16[2,256,256]{2,1,0:T(8,128)(2,1)S(1)} %copy-done.3, ...), custom_call_target="tpu_custom_call" | custom-call | tf_op jit(solution)/shard_map/inner/pallas_call | solution.py:282
  26.3 5.4 %all-gather.1 = bf16[8,32,256]{2,1,0:T(8,128)(2,1)S(1)} all-gather(bf16[2,32,256]{2,1,0:T(8,128)(2,1)S(1)} %get-tuple-element.19), channel_id=3, replica_groups=mesh['grp'=4,'slab'=8] {'grp'}, dimensions={0}, use_global_device_ids=true | all-gather | bytes 163840 | tf_op jit(solution)/shard_map/all_gather | solution.py:281
  31.7 0.0 collective-permute-done.2.gl
  31.7 0.0 collective-permute-done.3.gr
  31.7 0.0 copy-done.1
  31.7 4.0 %final.1 = (f32[16,64,256]{2,1,0:T(8,128)}, f32[16,64,256]{2,1,0:T(8,128)}) custom-call(f32[1]{0:T(128)S(6)} %copy.12.kap, f32[16,64,256]{2,1,0:T(8,128)S(1)} %bitcast.8, f32[16,64,256]{2,1,0:T(8,128)S(1)} %bitcast.11, f32[16,64,256]{2,1,0:T(8,128)S(1)} %get-tuple-element.15.part, f32[16,64,256]{2,1,0:T(8,128)S(1)} %get-tuple-element.16.inner, ...), custom_call_target="tpu_custom_call" | custom-call | tf_op jit(solution)/shard_map/final/pallas_call | solution.py:290
  (8 shorter events, 0.0 us)
Async XLA Ops:
  0.6 11.1 %copy-start = (f32[1,16,64,256]{3,2,1,0:T(8,128)S(1)}, f32[1,16,64,256]{3,2,1,0:T(8,128)}, u32[]{:S(2)}) copy-start(f32[1,16,64,256]{3,2,1,0:T(8,128)} %high.1) | copy-start | bytes 3145732
  2.4 8.8 %collective-permute-start = (bf16[160,256]{1,0:T(8,128)(2,1)}, bf16[160,256]{1,0:T(8,128)(2,1)S(1)}, u32[]{:S(2)}, u32[]{:S(2)}) collective-permute-start(bf16[160,256]{1,0:T(8,128)(2,1)} %get-tuple-element.12), channel_id=1, source_target_pairs={{0,1},{1,2},{2,3},{3,4},{4,5},{5,6},{6,7},{7,0},{8,9},{9,10},{10,1... | collective-permute-start | bytes 245768 | tf_op jit(solution)/shard_map/ppermute | solution.py:267
  5.4 6.4 %collective-permute-start.1 = (bf16[160,256]{1,0:T(8,128)(2,1)}, bf16[160,256]{1,0:T(8,128)(2,1)S(1)}, u32[]{:S(2)}, u32[]{:S(2)}) collective-permute-start(bf16[160,256]{1,0:T(8,128)(2,1)} %get-tuple-element.13), channel_id=1, source_target_pairs={{1,0},{2,1},{3,2},{4,3},{5,4},{6,5},{7,6},{0,7},{9,8},{10,9},{11,1... | collective-permute-start | bytes 245768 | tf_op jit(solution)/shard_map/ppermute | solution.py:268
  11.8 5.3 %copy-start.8 = (bf16[3,8,8,128]{3,2,1,0:T(8,128)(2,1)S(1)}, bf16[3,8,8,128]{3,2,1,0:T(8,128)(2,1)}, u32[]{:S(2)}) copy-start(bf16[3,8,8,128]{3,2,1,0:T(8,128)(2,1)} %vel.1) | copy-start | bytes 147460
  11.8 11.5 %copy-start.2 = (bf16[2,256,256]{2,1,0:T(8,128)(2,1)S(1)}, bf16[2,256,256]{2,1,0:T(8,128)(2,1)}, u32[]{:S(2)}) copy-start(bf16[2,256,256]{2,1,0:T(8,128)(2,1)} %constant.34.kz) | copy-start | bytes 786436
  11.8 11.5 %copy-start.3 = (bf16[2,256,256]{2,1,0:T(8,128)(2,1)S(1)}, bf16[2,256,256]{2,1,0:T(8,128)(2,1)}, u32[]{:S(2)}) copy-start(bf16[2,256,256]{2,1,0:T(8,128)(2,1)} %constant.27.ky) | copy-start | bytes 786436
  11.8 11.5 %copy-start.6 = (bf16[2,256,256]{2,1,0:T(8,128)(2,1)S(1)}, bf16[2,256,256]{2,1,0:T(8,128)(2,1)}, u32[]{:S(2)}) copy-start(bf16[2,256,256]{2,1,0:T(8,128)(2,1)} %constant.48.kz2) | copy-start | bytes 786436
  11.8 11.5 %copy-start.7 = (bf16[2,256,256]{2,1,0:T(8,128)(2,1)S(1)}, bf16[2,256,256]{2,1,0:T(8,128)(2,1)}, u32[]{:S(2)}) copy-start(bf16[2,256,256]{2,1,0:T(8,128)(2,1)} %constant.41.ky2) | copy-start | bytes 786436
  12.3 19.5 %collective-permute-start.2 = (bf16[2,64,256]{2,1,0:T(8,128)(2,1)S(1)}, bf16[2,64,256]{2,1,0:T(8,128)(2,1)S(1)}, u32[]{:S(2)}, u32[]{:S(2)}) collective-permute-start(bf16[2,64,256]{2,1,0:T(8,128)(2,1)S(1)} %get-tuple-element.17), channel_id=1, source_target_pairs={{0,1},{1,2},{2,3},{3,4},{4,5},{5,6},{6,7},{7,0},{8,9},{9,10},{10,1... | collective-permute-start | bytes 196616 | tf_op jit(solution)/shard_map/ppermute | solution.py:279
  13.0 10.3 %copy-start.4 = (bf16[128,256]{1,0:T(8,128)(2,1)S(1)}, bf16[128,256]{1,0:T(8,128)(2,1)}, u32[]{:S(2)}) copy-start(bf16[128,256]{1,0:T(8,128)(2,1)} %constant.17.clone.rz) | copy-start | bytes 196612
  13.0 10.4 %copy-start.5 = (bf16[256,128]{1,0:T(8,128)(2,1)S(1)}, bf16[256,128]{1,0:T(8,128)(2,1)}, u32[]{:S(2)}) copy-start(bf16[256,128]{1,0:T(8,128)(2,1)} %constant.16.clone.ry) | copy-start | bytes 196612
  13.0 18.7 %collective-permute-start.3 = (bf16[2,64,256]{2,1,0:T(8,128)(2,1)S(1)}, bf16[2,64,256]{2,1,0:T(8,128)(2,1)S(1)}, u32[]{:S(2)}, u32[]{:S(2)}) collective-permute-start(bf16[2,64,256]{2,1,0:T(8,128)(2,1)S(1)} %get-tuple-element.18), channel_id=1, source_target_pairs={{1,0},{2,1},{3,2},{4,3},{5,4},{6,5},{7,6},{0,7},{9,8},{10,9},{11,1... | collective-permute-start | bytes 196616 | tf_op jit(solution)/shard_map/ppermute | solution.py:280
  23.3 8.4 %copy-start.1 = (f32[1,16,64,256]{3,2,1,0:T(8,128)S(1)}, f32[1,16,64,256]{3,2,1,0:T(8,128)}, u32[]{:S(2)}) copy-start(f32[1,16,64,256]{3,2,1,0:T(8,128)} %param.11) | copy-start | bytes 3145732

commit v3 on v2

--- a/solution.py
+++ b/solution.py
@@ -1,3 +1,5 @@
+import functools
+
 import jax
 import jax.numpy as jnp
 import numpy as np
@@ -96,11 +98,20 @@
 FIRST, COUNT = (0, 3, 5), (3, 2, 2)
 
 
-def pack_kernel(low, high, vel, head, tail):
-    ny, nz = low.shape[2:]
-    coarse, rows, nzc = vel.shape[1:]
+def pack_kernel(theta, velocity, head, tail, low, high, vel, sems):
+    planes, ny, nz = theta.shape[1:]
+    coarse, rows, nzc = velocity.shape[1:]
+    copies = (
+        pltpu.make_async_copy(theta.at[0, pl.ds(0, 2)], low, sems.at[0]),
+        pltpu.make_async_copy(theta.at[0, pl.ds(planes - 2, 2)], high, sems.at[1]),
+        pltpu.make_async_copy(velocity, vel, sems.at[2]),
+    )
+    for copy in copies:
+        copy.start()
+    for copy in copies:
+        copy.wait()
     for out, edge, upper in ((head, low, False), (tail, high, True)):
-        out[: 2 * ny] = edge[0].reshape(2 * ny, nz).astype(jnp.bfloat16)
+        out[: 2 * ny] = edge[...].reshape(2 * ny, nz).astype(jnp.bfloat16)
         for q in range(8):
             c, k = SLOTS[min(q, 6)]
             k = coarse - COUNT[c] + k if upper else k
@@ -121,10 +132,13 @@
     return get
 
 
-def first_kernel(th, tl, tr, gx, halo, tail, head, work):
+def first_kernel(kap, th, tl, tr, gx, halo, tail, head, kv, work):
     planes, ny, nz = th.shape
+    kappa = kap[0]
+    kv[...] = jnp.full(kv.shape, kappa, jnp.float32)
 
     def put(i, value):
+        value = kappa * value
         gx[i] = value
         if i < 2:
             head[i] = value.astype(jnp.bfloat16)
@@ -136,17 +150,20 @@
     x_derivative(padded(th, tl, tr), put, work, planes)
 
 
-def flow_of(vel, halo, ry, rz):
-    ngrp, _, coarse, rows, nzc = vel.shape
+def flow_of(part, vel, halo, ry, rz):
+    ngrp = len(vel)
+    coarse, rows, nzc = vel[0].shape[1:]
+
+    wide = ry[part[0]]
 
     def plane(c, k):
         if 0 <= k < coarse:
-            got = [vel[g, c, k] for g in range(ngrp)]
+            got = [vel[g][c, k] for g in range(ngrp)]
         else:
             q = FIRST[c] + (COUNT[c] + k if k < 0 else k - coarse)
             top = rows * (q // 2)
             side = 0 if k < 0 else 1
-            got = [halo[g, side, top : top + rows, nzc * (q % 2) : nzc * (q % 2 + 1)] for g in range(ngrp)]
+            got = [halo[g][side, top : top + rows, nzc * (q % 2) : nzc * (q % 2 + 1)] for g in range(ngrp)]
         return jnp.concatenate([v.astype(jnp.float32) for v in got], axis=0)
 
     def fine(c, p):
@@ -160,7 +177,7 @@
     def flow(c, which):
         x = split(jnp.concatenate([fine(c, p) for p in which], axis=0))
         z = split(dot(x[0], rz[...]) + dot(x[1], rz[...]))
-        return dot(ry[...], z[0]) + dot(ry[...], z[1])
+        return dot(wide, z[0]) + dot(wide, z[1])
 
     return flow
 
@@ -178,26 +195,27 @@
     return (dot3(ky, fy) + dot3(fz, kz)).reshape(per, ny, nz)
 
 
-def inner_kernel(kap, th, gx, vel, ky, kz, ky2, kz2, ry, rz, acc, flux):
+def inner_kernel(ngrp, part, kv, th, gx, *refs):
+    vel, (ky, kz, ky2, kz2, ry, rz, acc, flux) = refs[:ngrp], refs[ngrp:]
     planes, ny, nz = th.shape
     per = ky.shape[1] // ny
-    kappa = kap[0]
-    flow = flow_of(vel, None, ry, rz)
+    kappa = kv[0:1, 0:1]
+    flow = flow_of(part, vel, None, ry, rz)
     for g in range(planes // per):
         at = slice(g * per, (g + 1) * per)
         x = split(th[at].reshape(per * ny, nz))
-        value = -kappa * (dot3(ky2, x) + dot3(x, kz2)).reshape(per, ny, nz)
+        value = (-kappa * (dot3(ky2, x) + dot3(x, kz2))).reshape(per, ny, nz)
         if is_inner(g, per, planes):
             value = value + cross(flow, th, ky, kz, g, per)
-            flux[at] = flow(0, range(g * per, (g + 1) * per)).reshape(per, ny, nz) * th[at] - kappa * gx[at]
+            flux[at] = flow(0, range(g * per, (g + 1) * per)).reshape(per, ny, nz) * th[at] - gx[at]
         acc[at] = value
 
 
-def final_kernel(kap, th, reg, part, inner, gx, tl, tr, gl, gr, vel, halo, ky, kz, ry, rz, new, saved, flux, acc):
+def final_kernel(ngrp, index, th, reg, part, inner, gx, tl, tr, gl, gr, *refs):
+    vel, halo, (ky, kz, ry, rz, new, saved, flux, acc) = refs[:ngrp], refs[ngrp : 2 * ngrp], refs[2 * ngrp :]
     planes, ny, nz = th.shape
     per = ky.shape[1] // ny
-    kappa = kap[0]
-    flow = flow_of(vel, halo, ry, rz)
+    flow = flow_of(index, vel, halo, ry, rz)
     get = padded(th, tl, tr)
     outer = [g for g in range(planes // per) if not is_inner(g, per, planes)]
     for g in outer:
@@ -213,7 +231,7 @@
                 d = gr[p - planes].astype(jnp.float32)
             else:
                 d = gx[p]
-            flux[p + 2] = f[i] * get(p) - kappa * d
+            flux[p + 2] = f[i] * get(p) - d
 
     def flux_at(p):
         return inner[p] if is_inner(p // per, per, planes) else flux[p + 2]
@@ -239,7 +257,8 @@
     eye = np.eye(per)
     ky2, kz2 = host_split(np.kron(eye, op_y @ op_y)), host_split((op_z @ op_z).T)
     ky, kz = host_split(np.kron(eye, op_y)), host_split(op_z.T)
-    ry = jnp.asarray(np.kron(eye, refine_operator(nyc)), bf16)
+    turned = [np.roll(refine_operator(nyc), -g * (nyc // ngrp), axis=1) for g in range(ngrp)]
+    ry = jnp.asarray(np.stack([np.kron(eye, m) for m in turned]), bf16)
     rz = jnp.asarray(refine_operator(nzc).T, bf16)
 
     field, saved = theta[0], register[0]
@@ -251,51 +270,58 @@
     smem = pl.BlockSpec(memory_space=pltpu.SMEM)
     params = pltpu.CompilerParams(vmem_limit_bytes=30 * 1024 * 1024)
 
-    whole = lambda shape: pl.BlockSpec(shape, lambda i: (0,) * len(shape))
+    anywhere = pl.BlockSpec(memory_space=pl.ANY)
     head, tail = pl.pallas_call(
         pack_kernel,
         out_shape=(packed, packed),
-        grid=(1,),
-        in_specs=[
-            pl.BlockSpec((1, 2, ny, nz), lambda i: (0, 0, 0, 0)),
-            pl.BlockSpec((1, 2, ny, nz), lambda i: (0, planes // 2 - 1, 0, 0)),
-            whole(velocity.shape),
+        in_specs=[anywhere] * 2,
+        out_specs=(vmem,) * 2,
+        scratch_shapes=[
+            pltpu.VMEM((2, ny, nz), f32),
+            pltpu.VMEM((2, ny, nz), f32),
+            pltpu.VMEM(velocity.shape, bf16),
+            pltpu.SemaphoreType.DMA((3,)),
         ],
-        out_specs=(whole(packed.shape),) * 2,
         name="pack",
-    )(theta, theta, velocity)
+    )(theta, velocity)
+
+    def gathered(x):
+        turns = [[((i + t) % ngrp, i) for i in range(ngrp)] for t in range(1, ngrp)]
+        return [x] + [lax.ppermute(x, "grp", turn) for turn in turns]
+
+    part = lax.axis_index("grp").astype(jnp.int32)[None]
     left = lax.ppermute(tail, "slab", up)
     right = lax.ppermute(head, "slab", down)
-    vel = lax.all_gather(velocity, "grp", axis=0, tiled=False)
-    gx, halo, tail, head = pl.pallas_call(
+    vel = gathered(velocity)
+    gx, halo, tail, head, kv = pl.pallas_call(
         first_kernel,
-        out_shape=(full, jax.ShapeDtypeStruct((2, 4 * rows, nz), bf16), edge, edge),
-        in_specs=[vmem] * 3,
-        out_specs=(vmem,) * 4,
+        out_shape=(full, jax.ShapeDtypeStruct((2, 4 * rows, nz), bf16), edge, edge, jax.ShapeDtypeStruct((8, 128), f32)),
+        in_specs=[smem] + [vmem] * 3,
+        out_specs=(vmem,) * 5,
         scratch_shapes=[pltpu.VMEM((planes, ny, nz), f32)],
         compiler_params=params,
         name="first",
-    )(field, left, right)
+    )(diffusivity, field, left, right)
     grad_l = lax.ppermute(tail, "slab", up)
     grad_r = lax.ppermute(head, "slab", down)
-    halo = lax.all_gather(halo, "grp", axis=0, tiled=False)
+    halo = gathered(halo)
     acc, inner = pl.pallas_call(
-        inner_kernel,
+        functools.partial(inner_kernel, ngrp),
         out_shape=(full, full),
-        in_specs=[smem] + [vmem] * 9,
+        in_specs=[smem] + [vmem] * (9 + ngrp),
         out_specs=(vmem,) * 2,
         compiler_params=params,
         name="inner",
-    )(diffusivity, field, gx, vel, ky, kz, ky2, kz2, ry, rz)
+    )(part, kv, field, gx, *vel, ky, kz, ky2, kz2, ry, rz)
     new, kept = pl.pallas_call(
-        final_kernel,
+        functools.partial(final_kernel, ngrp),
         out_shape=(full, full),
-        in_specs=[smem] + [vmem] * 15,
+        in_specs=[smem] + [vmem] * (13 + 2 * ngrp),
         out_specs=(vmem,) * 2,
         scratch_shapes=[pltpu.VMEM((planes + 4, ny, nz), f32), pltpu.VMEM((planes, ny, nz), f32)],
         compiler_params=params,
         name="final",
-    )(diffusivity, field, saved, acc, inner, gx, left, right, grad_l, grad_r, vel, halo, ky, kz, ry, rz)
+    )(part, field, saved, acc, inner, gx, left, right, grad_l, grad_r, *vel, *halo, ky, kz, ry, rz)
     return (new[None], kept[None])
 
 

time: 35.9 us -> 32 us (0.89)
  blocking collectives: 11 us -> 0 us
  starting transfers between devices: 10.8 us -> 16.4 us
  waiting for transfers between devices: 3.37 us -> 0.03 us
  local copies, waits for them, and re-layouts: 0.04 us -> 3.06 us
  Pallas kernels: 9.11 us -> 10.7 us
    all_gather x2 -> x0, blocking collectives: 11 us -> none  [the longest x1 5.58 us: shards(): vel = lax.all_gather(velocity, 'grp', axis=0, tiled=False)]
    ppermute x0 -> x6, starting transfers between devices: none -> 5.55 us  [gathered(): return [x] + [lax.ppermute(x, 'grp', turn) for turn in turns]]
    unnamed x18 -> x26, local copies, waits for them, and re-layouts: 0.04 us -> 3.06 us
    ppermute x1, waiting for transfers between devices: 2.75 us -> 0.01 us  [shards(): left = lax.ppermute(tail, 'slab', up)]
    pallas_call x3, Pallas kernels: 8.66 us -> 9.64 us  [the longest x1 4.95 us: shards(): pl.pallas_call(functools.partial(final_kernel, ngrp), out_shape=(full, fu...]
    pallas_call x1, Pallas kernels: 0.45 us -> 1.1 us  [shards(): pl.pallas_call(first_kernel, out_shape=(full, jax.ShapeDtypeStruct((2, 4...]
    ppermute x1, waiting for transfers between devices: 0.62 us -> 0.01 us  [shards(): right = lax.ppermute(head, 'slab', down)]
    ppermute x1, starting transfers between devices: 0.72 us -> 0.2 us  [shards(): grad_l = lax.ppermute(tail, 'slab', up)]
  transfers between devices with their start and end apart: 4 -> 10, of which waited for: 2 -> 0; matrix products, arithmetic and copies ran while one was open for 0% -> 0% of each run, Pallas kernels for 8% -> 13%
where the time goes in v3:
time: 32 us; the launch traced here: 31.7 us
  starting transfers between devices  16.4 us (51%)
  Pallas kernels  10.7 us (33%)
  local copies, waits for them, and re-layouts  3.06 us (10%)
  between operations  1.46 us (5%)
    ppermute x6, starting transfers between devices, gathered(): return [x] + [lax.ppermute(x, 'grp', turn) for turn in turns]  5.55 us
    pallas_call x1, Pallas kernels, shards(): pl.pallas_call(functools.partial(final_kernel, ngrp), out_shape=(full, fu...  4.95 us
    ppermute x1, starting transfers between devices, shards(): grad_r = lax.ppermute(head, 'slab', down)  4.52 us
    ppermute x1, starting transfers between devices, shards(): right = lax.ppermute(head, 'slab', down)  3.1 us
    unnamed x26, local copies, waits for them, and re-layouts  3.06 us
    ppermute x1, starting transfers between devices, shards(): left = lax.ppermute(tail, 'slab', up)  3.05 us
    pallas_call x1, Pallas kernels, shards(): pl.pallas_call(functools.partial(inner_kernel, ngrp), out_shape=(full, fu...  2.93 us
    pallas_call x1, Pallas kernels, shards(): pl.pallas_call(pack_kernel, out_shape=(packed, packed), in_specs=[anywher...  1.76 us
  transfers between devices with their start and end apart: 10, of which 0 were waited for; matrix products, arithmetic and copies ran while one was open for 0% of the time, Pallas kernels for 13%

profile of v3, /device:TPU:0, one launch (start us, length us, event | category | flops | bytes accessed | tf_op | source)
XLA Modules:
  0.0 31.7 jit_solution(11127751486413433275)
XLA Ops:
  0.6 1.8 %pack.1 = (bf16[160,256]{1,0:T(8,128)(2,1)}, bf16[160,256]{1,0:T(8,128)(2,1)}) custom-call(f32[1,16,64,256]{3,2,1,0:T(8,128)} %theta.1, bf16[3,8,8,128]{3,2,1,0:T(8,128)(2,1)} %refs_0_.3), custom_call_target="tpu_custom_call" | custom-call | tf_op jit(solution)/shard_map/pack/pallas_call | solution.py:274
  2.4 3.0 %collective-permute-start = (bf16[160,256]{1,0:T(8,128)(2,1)}, bf16[160,256]{1,0:T(8,128)(2,1)S(1)}, u32[]{:S(2)}, u32[]{:S(2)}) collective-permute-start(bf16[160,256]{1,0:T(8,128)(2,1)} %get-tuple-element.13), channel_id=1, source_target_pairs={{0,1},{1,2},{2,3},{3,4},{4,5},{5,6},{6,7},{7,0},{8,9},{9,10},{10,1... | collective-permute-start | bytes 245768 | tf_op jit(solution)/shard_map/ppermute | solution.py:293
  5.5 3.1 %collective-permute-start.1 = (bf16[160,256]{1,0:T(8,128)(2,1)}, bf16[160,256]{1,0:T(8,128)(2,1)S(1)}, u32[]{:S(2)}, u32[]{:S(2)}) collective-permute-start(bf16[160,256]{1,0:T(8,128)(2,1)} %get-tuple-element.14), channel_id=1, source_target_pairs={{1,0},{2,1},{3,2},{4,3},{5,4},{6,5},{7,6},{0,7},{9,8},{10,9},{11,1... | collective-permute-start | bytes 245768 | tf_op jit(solution)/shard_map/ppermute | solution.py:294
  8.6 0.0 collective-permute-start.4
  8.6 1.6 %collective-permute-start.3 = (bf16[3,8,8,128]{3,2,1,0:T(8,128)(2,1)S(1)}, bf16[3,8,8,128]{3,2,1,0:T(8,128)(2,1)S(1)}, u32[]{:S(2)}, u32[]{:S(2)}) collective-permute-start(bf16[3,8,8,128]{3,2,1,0:T(8,128)(2,1)S(1)} %copy-done.5), channel_id=1, source_target_pairs={{16,0},{24,8},{0,16},{8,24},{17,1},{25,9},{1,17},{9,25},{18,2},{26... | collective-permute-start | bytes 147464 | tf_op jit(solution)/shard_map/ppermute | solution.py:290
  10.2 1.5 %collective-permute-start.2 = (bf16[3,8,8,128]{3,2,1,0:T(8,128)(2,1)S(1)}, bf16[3,8,8,128]{3,2,1,0:T(8,128)(2,1)S(1)}, u32[]{:S(2)}, u32[]{:S(2)}) collective-permute-start(bf16[3,8,8,128]{3,2,1,0:T(8,128)(2,1)S(1)} %copy-done.5), channel_id=1, source_target_pairs={{8,0},{16,8},{24,16},{0,24},{9,1},{17,9},{25,17},{1,25},{10,2},{18... | collective-permute-start | bytes 147464 | tf_op jit(solution)/shard_map/ppermute | solution.py:290
  12.3 0.0 collective-permute-done.tl
  12.3 0.0 collective-permute-done.1.tr
  12.3 0.0 copy-start.2
  12.3 0.0 copy-start.3
  12.3 0.0 copy-start.4
  12.3 0.0 copy-start.6
  12.4 0.0 copy-start.7
  12.4 1.1 %first.1 = (f32[16,64,256]{2,1,0:T(8,128)S(1)}, bf16[2,32,256]{2,1,0:T(8,128)(2,1)S(1)}, bf16[2,64,256]{2,1,0:T(8,128)(2,1)}, bf16[2,64,256]{2,1,0:T(8,128)(2,1)}, f32[8,128]{1,0:T(8,128)S(1)}) custom-call(f32[1]{0:T(128)S(6)} %copy.12.kap, f32[16,64,256]{2,1,0:T(8,128)S(1)} %bitcast.5, bf16[160,256]{1,0:T(8,128)(2,1)S(1)} %collective-permute-done.tl, ...), custom_call_target="tpu_custom_call" | custom-call | tf_op jit(solution)/shard_map/first/pallas_call | solution.py:296
  13.5 0.2 collective-permute-start.5
  13.7 4.5 %collective-permute-start.6 = (bf16[2,64,256]{2,1,0:T(8,128)(2,1)}, bf16[2,64,256]{2,1,0:T(8,128)(2,1)}, u32[]{:S(2)}, u32[]{:S(2)}) collective-permute-start(bf16[2,64,256]{2,1,0:T(8,128)(2,1)} %get-tuple-element.20), channel_id=1, source_target_pairs={{1,0},{2,1},{3,2},{4,3},{5,4},{6,5},{7,6},{0,7},{9,8},{10,9},{11,1... | collective-permute-start | bytes 196616 | tf_op jit(solution)/shard_map/ppermute | solution.py:306
  18.2 1.1 %collective-permute-start.8 = (bf16[2,32,256]{2,1,0:T(8,128)(2,1)S(1)}, bf16[2,32,256]{2,1,0:T(8,128)(2,1)}, u32[]{:S(2)}, u32[]{:S(2)}) collective-permute-start(bf16[2,32,256]{2,1,0:T(8,128)(2,1)S(1)} %get-tuple-element.21.refs_4_), channel_id=1, source_target_pairs={{16,0},{24,8},{0,16},{8,24},{17,1},{25,9},{1,17},{9,25},{18,2},{26... | collective-permute-start | bytes 98312 | tf_op jit(solution)/shard_map/ppermute | solution.py:290
  19.3 0.6 %copy-done.9 = bf16[3,8,8,128]{3,2,1,0:T(8,128)(2,1)} copy-done((bf16[3,8,8,128]{3,2,1,0:T(8,128)(2,1)}, bf16[3,8,8,128]{3,2,1,0:T(8,128)(2,1)S(1)}, u32[]{:S(2)}) %copy-start.9) | copy-done | bytes 49176
  19.9 1.4 %collective-permute-start.7 = (bf16[2,32,256]{2,1,0:T(8,128)(2,1)S(1)}, bf16[2,32,256]{2,1,0:T(8,128)(2,1)}, u32[]{:S(2)}, u32[]{:S(2)}) collective-permute-start(bf16[2,32,256]{2,1,0:T(8,128)(2,1)S(1)} %get-tuple-element.21.refs_4_), channel_id=1, source_target_pairs={{8,0},{16,8},{24,16},{0,24},{9,1},{17,9},{25,17},{1,25},{10,2},{18... | collective-permute-start | bytes 98312 | tf_op jit(solution)/shard_map/ppermute | solution.py:290
  21.4 0.6 %copy-done.12 = f32[8,128]{1,0:T(8,128)S(1)} copy-done((f32[8,128]{1,0:T(8,128)S(1)}, f32[8,128]{1,0:T(8,128)}, u32[]{:S(2)}) %copy-start.12) | copy-done | bytes 4120
  22.0 0.9 %copy-done.8 = bf16[2,256,256]{2,1,0:T(8,128)(2,1)S(1)} copy-done((bf16[2,256,256]{2,1,0:T(8,128)(2,1)S(1)}, bf16[2,256,256]{2,1,0:T(8,128)(2,1)}, u32[]{:S(2)}) %copy-start.8) | copy-done | bytes 262168
  23.0 0.8 %copy-done.10 = bf16[3,8,8,128]{3,2,1,0:T(8,128)(2,1)S(1)} copy-done((bf16[3,8,8,128]{3,2,1,0:T(8,128)(2,1)S(1)}, bf16[3,8,8,128]{3,2,1,0:T(8,128)(2,1)}, u32[]{:S(2)}) %copy-start.10) | copy-done | bytes 49176
  23.8 2.9 %inner.1 = (f32[16,64,256]{2,1,0:T(8,128)S(1)}, f32[16,64,256]{2,1,0:T(8,128)S(1)}) custom-call(s32[1]{0:T(128)} %bitcast.part.index, f32[8,128]{1,0:T(8,128)S(1)} %copy-done.12, f32[16,64,256]{2,1,0:T(8,128)S(1)} %bitcast.6, f32[16,64,256]{2,1,0:T(8,128)S(1)} %get-tuple-element.16.gx, bf16[3,8,8,128]{3,2,1,0:T(8,128)(2,1)S(1)} %copy-done.5, ...), custom_call_target="tpu_custom_call" | custom-call | tf_op jit(solution)/shard_map/inner/pallas_call | solution.py:308
  26.8 5.0 %final.1 = (f32[16,64,256]{2,1,0:T(8,128)}, f32[16,64,256]{2,1,0:T(8,128)}) custom-call(s32[1]{0:T(128)} %bitcast.part.index, f32[16,64,256]{2,1,0:T(8,128)S(1)} %bitcast.7, f32[16,64,256]{2,1,0:T(8,128)S(1)} %bitcast.8, f32[16,64,256]{2,1,0:T(8,128)S(1)} %get-tuple-element.17.part, f32[16,64,256]{2,1,0:T(8,128)S(1)} %get-tuple-element.18.inner, ...), custom_call_target="tpu_custom_call" | custom-call | tf_op jit(solution)/shard_map/final/pallas_call | solution.py:316
  (26 shorter events, 0.1 us)
Async XLA Ops:
  0.6 7.9 %copy-start.5 = (bf16[3,8,8,128]{3,2,1,0:T(8,128)(2,1)S(1)}, bf16[3,8,8,128]{3,2,1,0:T(8,128)(2,1)}, u32[]{:S(2)}) copy-start(bf16[3,8,8,128]{3,2,1,0:T(8,128)(2,1)} %refs_0_.3) | copy-start | bytes 147460
  0.6 11.7 %copy-start = (f32[1,16,64,256]{3,2,1,0:T(8,128)S(1)}, f32[1,16,64,256]{3,2,1,0:T(8,128)}, u32[]{:S(2)}) copy-start(f32[1,16,64,256]{3,2,1,0:T(8,128)} %theta.1) | copy-start | bytes 3145732
  2.4 9.9 %collective-permute-start = (bf16[160,256]{1,0:T(8,128)(2,1)}, bf16[160,256]{1,0:T(8,128)(2,1)S(1)}, u32[]{:S(2)}, u32[]{:S(2)}) collective-permute-start(bf16[160,256]{1,0:T(8,128)(2,1)} %get-tuple-element.13), channel_id=1, source_target_pairs={{0,1},{1,2},{2,3},{3,4},{4,5},{5,6},{6,7},{7,0},{8,9},{9,10},{10,1... | collective-permute-start | bytes 245768 | tf_op jit(solution)/shard_map/ppermute | solution.py:293
  5.5 6.8 %collective-permute-start.1 = (bf16[160,256]{1,0:T(8,128)(2,1)}, bf16[160,256]{1,0:T(8,128)(2,1)S(1)}, u32[]{:S(2)}, u32[]{:S(2)}) collective-permute-start(bf16[160,256]{1,0:T(8,128)(2,1)} %get-tuple-element.14), channel_id=1, source_target_pairs={{1,0},{2,1},{3,2},{4,3},{5,4},{6,5},{7,6},{0,7},{9,8},{10,9},{11,1... | collective-permute-start | bytes 245768 | tf_op jit(solution)/shard_map/ppermute | solution.py:294
  8.6 9.6 %collective-permute-start.4 = (bf16[3,8,8,128]{3,2,1,0:T(8,128)(2,1)S(1)}, bf16[3,8,8,128]{3,2,1,0:T(8,128)(2,1)S(1)}, u32[]{:S(2)}, u32[]{:S(2)}) collective-permute-start(bf16[3,8,8,128]{3,2,1,0:T(8,128)(2,1)S(1)} %copy-done.5), channel_id=1, source_target_pairs={{24,0},{0,8},{8,16},{16,24},{25,1},{1,9},{9,17},{17,25},{26,2},{2,... | collective-permute-start | bytes 147464 | tf_op jit(solution)/shard_map/ppermute | solution.py:290
  8.6 9.6 %collective-permute-start.3 = (bf16[3,8,8,128]{3,2,1,0:T(8,128)(2,1)S(1)}, bf16[3,8,8,128]{3,2,1,0:T(8,128)(2,1)S(1)}, u32[]{:S(2)}, u32[]{:S(2)}) collective-permute-start(bf16[3,8,8,128]{3,2,1,0:T(8,128)(2,1)S(1)} %copy-done.5), channel_id=1, source_target_pairs={{16,0},{24,8},{0,16},{8,24},{17,1},{25,9},{1,17},{9,25},{18,2},{26... | collective-permute-start | bytes 147464 | tf_op jit(solution)/shard_map/ppermute | solution.py:290
  10.2 9.1 %collective-permute-start.2 = (bf16[3,8,8,128]{3,2,1,0:T(8,128)(2,1)S(1)}, bf16[3,8,8,128]{3,2,1,0:T(8,128)(2,1)S(1)}, u32[]{:S(2)}, u32[]{:S(2)}) collective-permute-start(bf16[3,8,8,128]{3,2,1,0:T(8,128)(2,1)S(1)} %copy-done.5), channel_id=1, source_target_pairs={{8,0},{16,8},{24,16},{0,24},{9,1},{17,9},{25,17},{1,25},{10,2},{18... | collective-permute-start | bytes 147464 | tf_op jit(solution)/shard_map/ppermute | solution.py:290
  12.3 9.0 %copy-start.2 = (bf16[2,256,256]{2,1,0:T(8,128)(2,1)S(1)}, bf16[2,256,256]{2,1,0:T(8,128)(2,1)}, u32[]{:S(2)}) copy-start(bf16[2,256,256]{2,1,0:T(8,128)(2,1)} %constant.39.refs_5_.refs_9_) | copy-start | bytes 786436
  12.3 9.0 %copy-start.3 = (bf16[2,256,256]{2,1,0:T(8,128)(2,1)S(1)}, bf16[2,256,256]{2,1,0:T(8,128)(2,1)}, u32[]{:S(2)}) copy-start(bf16[2,256,256]{2,1,0:T(8,128)(2,1)} %constant.32.refs_4_.refs_8_) | copy-start | bytes 786436
  12.3 9.0 %copy-start.4 = (bf16[4,256,128]{2,1,0:T(8,128)(2,1)S(1)}, bf16[4,256,128]{2,1,0:T(8,128)(2,1)}, u32[]{:S(2)}) copy-start(bf16[4,256,128]{2,1,0:T(8,128)(2,1)} %constant.21.clone.refs_8_.refs_10_) | copy-start | bytes 786436
  12.3 9.0 %copy-start.6 = (bf16[128,256]{1,0:T(8,128)(2,1)S(1)}, bf16[128,256]{1,0:T(8,128)(2,1)}, u32[]{:S(2)}) copy-start(bf16[128,256]{1,0:T(8,128)(2,1)} %constant.22.clone.refs_9_.refs_11_) | copy-start | bytes 196612
  12.4 9.0 %copy-start.7 = (bf16[2,256,256]{2,1,0:T(8,128)(2,1)S(1)}, bf16[2,256,256]{2,1,0:T(8,128)(2,1)}, u32[]{:S(2)}) copy-start(bf16[2,256,256]{2,1,0:T(8,128)(2,1)} %constant.53.refs_7_) | copy-start | bytes 786436
  13.5 5.8 %copy-start.11 = (f32[8,128]{1,0:T(8,128)}, f32[8,128]{1,0:T(8,128)S(1)}, u32[]{:S(2)}) copy-start(f32[8,128]{1,0:T(8,128)S(1)} %get-tuple-element.15.kv) | copy-start | bytes 12292
  13.5 13.3 %collective-permute-start.5 = (bf16[2,64,256]{2,1,0:T(8,128)(2,1)}, bf16[2,64,256]{2,1,0:T(8,128)(2,1)}, u32[]{:S(2)}, u32[]{:S(2)}) collective-permute-start(bf16[2,64,256]{2,1,0:T(8,128)(2,1)} %get-tuple-element.19), channel_id=1, source_target_pairs={{0,1},{1,2},{2,3},{3,4},{4,5},{5,6},{6,7},{7,0},{8,9},{9,10},{10,1... | collective-permute-start | bytes 196616 | tf_op jit(solution)/shard_map/ppermute | solution.py:305
  13.7 13.1 %collective-permute-start.6 = (bf16[2,64,256]{2,1,0:T(8,128)(2,1)}, bf16[2,64,256]{2,1,0:T(8,128)(2,1)}, u32[]{:S(2)}, u32[]{:S(2)}) collective-permute-start(bf16[2,64,256]{2,1,0:T(8,128)(2,1)} %get-tuple-element.20), channel_id=1, source_target_pairs={{1,0},{2,1},{3,2},{4,3},{5,4},{6,5},{7,6},{0,7},{9,8},{10,9},{11,1... | collective-permute-start | bytes 196616 | tf_op jit(solution)/shard_map/ppermute | solution.py:306
  18.2 8.5 %collective-permute-start.9 = (bf16[2,32,256]{2,1,0:T(8,128)(2,1)S(1)}, bf16[2,32,256]{2,1,0:T(8,128)(2,1)}, u32[]{:S(2)}, u32[]{:S(2)}) collective-permute-start(bf16[2,32,256]{2,1,0:T(8,128)(2,1)S(1)} %get-tuple-element.21.refs_4_), channel_id=1, source_target_pairs={{24,0},{0,8},{8,16},{16,24},{25,1},{1,9},{9,17},{17,25},{26,2},{2,... | collective-permute-start | bytes 98312 | tf_op jit(solution)/shard_map/ppermute | solution.py:290
  18.2 8.5 %collective-permute-start.8 = (bf16[2,32,256]{2,1,0:T(8,128)(2,1)S(1)}, bf16[2,32,256]{2,1,0:T(8,128)(2,1)}, u32[]{:S(2)}, u32[]{:S(2)}) collective-permute-start(bf16[2,32,256]{2,1,0:T(8,128)(2,1)S(1)} %get-tuple-element.21.refs_4_), channel_id=1, source_target_pairs={{16,0},{24,8},{0,16},{8,24},{17,1},{25,9},{1,17},{9,25},{18,2},{26... | collective-permute-start | bytes 98312 | tf_op jit(solution)/shard_map/ppermute | solution.py:290
  19.3 0.6 %copy-start.9 = (bf16[3,8,8,128]{3,2,1,0:T(8,128)(2,1)}, bf16[3,8,8,128]{3,2,1,0:T(8,128)(2,1)S(1)}, u32[]{:S(2)}) copy-start(bf16[3,8,8,128]{3,2,1,0:T(8,128)(2,1)S(1)} %collective-permute-done.2.refs_1_) | copy-start | bytes 147460
  19.9 6.8 %collective-permute-start.7 = (bf16[2,32,256]{2,1,0:T(8,128)(2,1)S(1)}, bf16[2,32,256]{2,1,0:T(8,128)(2,1)}, u32[]{:S(2)}, u32[]{:S(2)}) collective-permute-start(bf16[2,32,256]{2,1,0:T(8,128)(2,1)S(1)} %get-tuple-element.21.refs_4_), channel_id=1, source_target_pairs={{8,0},{16,8},{24,16},{0,24},{9,1},{17,9},{25,17},{1,25},{10,2},{18... | collective-permute-start | bytes 98312 | tf_op jit(solution)/shard_map/ppermute | solution.py:290
  21.3 0.7 %copy-start.12 = (f32[8,128]{1,0:T(8,128)S(1)}, f32[8,128]{1,0:T(8,128)}, u32[]{:S(2)}) copy-start(f32[8,128]{1,0:T(8,128)} %copy-done.11) | copy-start | bytes 12292
  22.0 0.9 %copy-start.8 = (bf16[2,256,256]{2,1,0:T(8,128)(2,1)S(1)}, bf16[2,256,256]{2,1,0:T(8,128)(2,1)}, u32[]{:S(2)}) copy-start(bf16[2,256,256]{2,1,0:T(8,128)(2,1)} %constant.46.refs_6_) | copy-start | bytes 786436
  23.0 0.8 %copy-start.10 = (bf16[3,8,8,128]{3,2,1,0:T(8,128)(2,1)S(1)}, bf16[3,8,8,128]{3,2,1,0:T(8,128)(2,1)}, u32[]{:S(2)}) copy-start(bf16[3,8,8,128]{3,2,1,0:T(8,128)(2,1)} %copy-done.9) | copy-start | bytes 147460
  23.8 3.0 %copy-start.1 = (f32[1,16,64,256]{3,2,1,0:T(8,128)S(1)}, f32[1,16,64,256]{3,2,1,0:T(8,128)}, u32[]{:S(2)}) copy-start(f32[1,16,64,256]{3,2,1,0:T(8,128)} %param.11) | copy-start | bytes 3145732

commit v4 on v3

--- a/solution.py
+++ b/solution.py
@@ -53,12 +53,25 @@
     return jnp.stack(split(x))
 
 
+def host_stack(x):
+    hi, lo = host_split(x)
+    return jnp.concatenate([hi, lo, hi], axis=1)
+
+
 def dot(a, b):
     return jnp.dot(a, b, preferred_element_type=jnp.float32)
 
 
 def dot3(a, b):
     return dot(a[0], b[0]) + (dot(a[0], b[1]) + dot(a[1], b[0]))
+
+
+def along_y(op, x, ny):
+    out = []
+    for top in range(0, x[0].shape[0], ny):
+        hi, lo = x[0][top : top + ny], x[1][top : top + ny]
+        out.append(dot(op[...], jnp.concatenate([hi, hi, lo], axis=0)))
+    return jnp.concatenate(out, axis=0)
 
 
 def banded_lu(count):
@@ -132,11 +145,9 @@
     return get
 
 
-def first_kernel(kap, th, tl, tr, gx, halo, tail, head, kv, work):
+def first_kernel(kap, th, tl, tr, gx, halo, tail, head, work):
     planes, ny, nz = th.shape
     kappa = kap[0]
-    kv[...] = jnp.full(kv.shape, kappa, jnp.float32)
-
     def put(i, value):
         value = kappa * value
         gx[i] = value
@@ -155,6 +166,8 @@
     coarse, rows, nzc = vel[0].shape[1:]
 
     wide = ry[part[0]]
+    deep = jnp.concatenate([rz[...], rz[...]], axis=0)
+    nyc = rows * ngrp
 
     def plane(c, k):
         if 0 <= k < coarse:
@@ -176,8 +189,10 @@
 
     def flow(c, which):
         x = split(jnp.concatenate([fine(c, p) for p in which], axis=0))
-        z = split(dot(x[0], rz[...]) + dot(x[1], rz[...]))
-        return dot(wide, z[0]) + dot(wide, z[1])
+        z = split(dot(jnp.concatenate(x, axis=1), deep))
+        tops = range(0, z[0].shape[0], nyc)
+        pairs = [jnp.concatenate([h[t : t + nyc] for h in z], axis=0) for t in tops]
+        return jnp.concatenate([dot(wide, pair) for pair in pairs], axis=0)
 
     return flow
 
@@ -192,19 +207,19 @@
     x = th[g * per : (g + 1) * per].reshape(per * ny, nz)
     fy = split(flow(1, which) * x)
     fz = split(flow(2, which) * x)
-    return (dot3(ky, fy) + dot3(fz, kz)).reshape(per, ny, nz)
-
-
-def inner_kernel(ngrp, part, kv, th, gx, *refs):
+    return (along_y(ky, fy, ny) + dot3(fz, kz)).reshape(per, ny, nz)
+
+
+def inner_kernel(ngrp, part, kap, th, gx, *refs):
     vel, (ky, kz, ky2, kz2, ry, rz, acc, flux) = refs[:ngrp], refs[ngrp:]
     planes, ny, nz = th.shape
-    per = ky.shape[1] // ny
-    kappa = kv[0:1, 0:1]
+    per = max(1, MXU // ny)
+    kappa = kap[0]
     flow = flow_of(part, vel, None, ry, rz)
     for g in range(planes // per):
         at = slice(g * per, (g + 1) * per)
         x = split(th[at].reshape(per * ny, nz))
-        value = (-kappa * (dot3(ky2, x) + dot3(x, kz2))).reshape(per, ny, nz)
+        value = (-kappa * (along_y(ky2, x, ny) + dot3(x, kz2))).reshape(per, ny, nz)
         if is_inner(g, per, planes):
             value = value + cross(flow, th, ky, kz, g, per)
             flux[at] = flow(0, range(g * per, (g + 1) * per)).reshape(per, ny, nz) * th[at] - gx[at]
@@ -214,7 +229,7 @@
 def final_kernel(ngrp, index, th, reg, part, inner, gx, tl, tr, gl, gr, *refs):
     vel, halo, (ky, kz, ry, rz, new, saved, flux, acc) = refs[:ngrp], refs[ngrp : 2 * ngrp], refs[2 * ngrp :]
     planes, ny, nz = th.shape
-    per = ky.shape[1] // ny
+    per = max(1, MXU // ny)
     flow = flow_of(index, vel, halo, ry, rz)
     get = padded(th, tl, tr)
     outer = [g for g in range(planes // per) if not is_inner(g, per, planes)]
@@ -249,16 +264,14 @@
     planes, ny, nz = theta.shape[1:]
     nslab, ngrp = lax.axis_size("slab"), lax.axis_size("grp")
     nyc, nzc = ny // 2, nz // 2
-    per = max(1, MXU // ny)
     f32, bf16 = jnp.float32, jnp.bfloat16
     up = [(i, (i + 1) % nslab) for i in range(nslab)]
     down = [((i + 1) % nslab, i) for i in range(nslab)]
     op_y, op_z = blocked_operator(ny, BLK), blocked_operator(nz, BLK)
-    eye = np.eye(per)
-    ky2, kz2 = host_split(np.kron(eye, op_y @ op_y)), host_split((op_z @ op_z).T)
-    ky, kz = host_split(np.kron(eye, op_y)), host_split(op_z.T)
+    ky2, kz2 = host_stack(op_y @ op_y), host_split((op_z @ op_z).T)
+    ky, kz = host_stack(op_y), host_split(op_z.T)
     turned = [np.roll(refine_operator(nyc), -g * (nyc // ngrp), axis=1) for g in range(ngrp)]
-    ry = jnp.asarray(np.stack([np.kron(eye, m) for m in turned]), bf16)
+    ry = jnp.asarray(np.stack([np.tile(m, (1, 2)) for m in turned]), bf16)
     rz = jnp.asarray(refine_operator(nzc).T, bf16)
 
     field, saved = theta[0], register[0]
@@ -268,7 +281,7 @@
     packed = jax.ShapeDtypeStruct((2 * ny + 4 * rows, nz), bf16)
     vmem = pl.BlockSpec(memory_space=pltpu.VMEM)
     smem = pl.BlockSpec(memory_space=pltpu.SMEM)
-    params = pltpu.CompilerParams(vmem_limit_bytes=30 * 1024 * 1024)
+    grant = lambda mib: pltpu.CompilerParams(vmem_limit_bytes=mib * 1024 * 1024)
 
     anywhere = pl.BlockSpec(memory_space=pl.ANY)
     head, tail = pl.pallas_call(
@@ -282,6 +295,7 @@
             pltpu.VMEM(velocity.shape, bf16),
             pltpu.SemaphoreType.DMA((3,)),
         ],
+        compiler_params=grant(4),
         name="pack",
     )(theta, velocity)
 
@@ -293,13 +307,13 @@
     left = lax.ppermute(tail, "slab", up)
     right = lax.ppermute(head, "slab", down)
     vel = gathered(velocity)
-    gx, halo, tail, head, kv = pl.pallas_call(
+    gx, halo, tail, head = pl.pallas_call(
         first_kernel,
-        out_shape=(full, jax.ShapeDtypeStruct((2, 4 * rows, nz), bf16), edge, edge, jax.ShapeDtypeStruct((8, 128), f32)),
+        out_shape=(full, jax.ShapeDtypeStruct((2, 4 * rows, nz), bf16), edge, edge),
         in_specs=[smem] + [vmem] * 3,
-        out_specs=(vmem,) * 5,
+        out_specs=(vmem,) * 4,
         scratch_shapes=[pltpu.VMEM((planes, ny, nz), f32)],
-        compiler_params=params,
+        compiler_params=grant(8),
         name="first",
     )(diffusivity, field, left, right)
     grad_l = lax.ppermute(tail, "slab", up)
@@ -308,18 +322,18 @@
     acc, inner = pl.pallas_call(
         functools.partial(inner_kernel, ngrp),
         out_shape=(full, full),
-        in_specs=[smem] + [vmem] * (9 + ngrp),
+        in_specs=[smem] * 2 + [vmem] * (8 + ngrp),
         out_specs=(vmem,) * 2,
-        compiler_params=params,
+        compiler_params=grant(14),
         name="inner",
-    )(part, kv, field, gx, *vel, ky, kz, ky2, kz2, ry, rz)
+    )(part, diffusivity, field, gx, *vel, ky, kz, ky2, kz2, ry, rz)
     new, kept = pl.pallas_call(
         functools.partial(final_kernel, ngrp),
         out_shape=(full, full),
         in_specs=[smem] + [vmem] * (13 + 2 * ngrp),
         out_specs=(vmem,) * 2,
         scratch_shapes=[pltpu.VMEM((planes + 4, ny, nz), f32), pltpu.VMEM((planes, ny, nz), f32)],
-        compiler_params=params,
+        compiler_params=grant(14),
         name="final",
     )(part, field, saved, acc, inner, gx, left, right, grad_l, grad_r, *vel, *halo, ky, kz, ry, rz)
     return (new[None], kept[None])

time: 32 us -> 28.3 us (0.88)
  local copies, waits for them, and re-layouts: 3.06 us -> 1.27 us
  Pallas kernels: 10.7 us -> 9.02 us
    unnamed x26 -> x18, local copies, waits for them, and re-layouts: 3.06 us -> 1.27 us
    pallas_call x1, Pallas kernels: 4.95 us -> 4.23 us  [shards(): pl.pallas_call(functools.partial(final_kernel, ngrp), out_shape=(full, fu...]
    pallas_call x1, Pallas kernels: 1.1 us -> 0.48 us  [shards(): pl.pallas_call(first_kernel, out_shape=(full, jax.ShapeDtypeStruct((2, 4...]
    pallas_call x1, Pallas kernels: 1.76 us -> 1.18 us  [shards(): pl.pallas_call(pack_kernel, out_shape=(packed, packed), in_specs=[anywher...]
where the time goes in v4:
time: 28.3 us; the launch traced here: 28 us
  starting transfers between devices  16.3 us (58%)
  Pallas kernels  9.02 us (32%)
  between operations  1.48 us (5%)
  local copies, waits for them, and re-layouts  1.27 us (4%)
    ppermute x6, starting transfers between devices, gathered(): return [x] + [lax.ppermute(x, 'grp', turn) for turn in turns]  5.34 us
    ppermute x1, starting transfers between devices, shards(): grad_r = lax.ppermute(head, 'slab', down)  4.71 us
    pallas_call x1, Pallas kernels, shards(): pl.pallas_call(functools.partial(final_kernel, ngrp), out_shape=(full, fu...  4.23 us
    pallas_call x1, Pallas kernels, shards(): pl.pallas_call(functools.partial(inner_kernel, ngrp), out_shape=(full, fu...  3.12 us
    ppermute x1, starting transfers between devices, shards(): right = lax.ppermute(head, 'slab', down)  3.1 us
    ppermute x1, starting transfers between devices, shards(): left = lax.ppermute(tail, 'slab', up)  3.05 us
    unnamed x18, local copies, waits for them, and re-layouts  1.27 us
    pallas_call x1, Pallas kernels, shards(): pl.pallas_call(pack_kernel, out_shape=(packed, packed), in_specs=[anywher...  1.18 us
  transfers between devices with their start and end apart: 10, of which 0 were waited for; matrix products, arithmetic and copies ran while one was open for 0% of the time, Pallas kernels for 13%

profile of v4, /device:TPU:0, one launch (start us, length us, event | category | flops | bytes accessed | tf_op | source)
XLA Modules:
  0.0 28.0 jit_solution(2329146182784835778)
XLA Ops:
  0.6 1.2 %copy-done = f32[1,16,64,256]{3,2,1,0:T(8,128)S(1)} copy-done((f32[1,16,64,256]{3,2,1,0:T(8,128)S(1)}, f32[1,16,64,256]{3,2,1,0:T(8,128)}, u32[]{:S(2)}) %copy-start) | copy-done | bytes 1048600
  1.9 1.2 %pack.1 = (bf16[160,256]{1,0:T(8,128)(2,1)S(1)}, bf16[160,256]{1,0:T(8,128)(2,1)S(1)}) custom-call(f32[1,16,64,256]{3,2,1,0:T(8,128)S(1)} %copy-done, bf16[3,8,8,128]{3,2,1,0:T(8,128)(2,1)} %refs_0_.3), custom_call_target="tpu_custom_call" | custom-call | tf_op jit(solution)/shard_map/pack/pallas_call | solution.py:287
  3.0 3.0 %collective-permute-start = (bf16[160,256]{1,0:T(8,128)(2,1)S(1)}, bf16[160,256]{1,0:T(8,128)(2,1)S(1)}, u32[]{:S(2)}, u32[]{:S(2)}) collective-permute-start(bf16[160,256]{1,0:T(8,128)(2,1)S(1)} %get-tuple-element.12), channel_id=1, source_target_pairs={{0,1},{1,2},{2,3},{3,4},{4,5},{5,6},{6,7},{7,0},{8,9},{9,10},{10,1... | collective-permute-start | bytes 245768 | tf_op jit(solution)/shard_map/ppermute | solution.py:307
  6.1 3.1 %collective-permute-start.1 = (bf16[160,256]{1,0:T(8,128)(2,1)S(1)}, bf16[160,256]{1,0:T(8,128)(2,1)S(1)}, u32[]{:S(2)}, u32[]{:S(2)}) collective-permute-start(bf16[160,256]{1,0:T(8,128)(2,1)S(1)} %get-tuple-element.13), channel_id=1, source_target_pairs={{1,0},{2,1},{3,2},{4,3},{5,4},{6,5},{7,6},{0,7},{9,8},{10,9},{11,1... | collective-permute-start | bytes 245768 | tf_op jit(solution)/shard_map/ppermute | solution.py:308
  9.2 0.0 collective-permute-start.4
  9.2 1.6 %collective-permute-start.3 = (bf16[3,8,8,128]{3,2,1,0:T(8,128)(2,1)}, bf16[3,8,8,128]{3,2,1,0:T(8,128)(2,1)S(1)}, u32[]{:S(2)}, u32[]{:S(2)}) collective-permute-start(bf16[3,8,8,128]{3,2,1,0:T(8,128)(2,1)} %refs_0_.3), channel_id=1, source_target_pairs={{16,0},{24,8},{0,16},{8,24},{17,1},{25,9},{1,17},{9,25},{18,2},{26... | collective-permute-start | bytes 147464 | tf_op jit(solution)/shard_map/ppermute | solution.py:304
  10.8 1.5 %collective-permute-start.2 = (bf16[3,8,8,128]{3,2,1,0:T(8,128)(2,1)}, bf16[3,8,8,128]{3,2,1,0:T(8,128)(2,1)S(1)}, u32[]{:S(2)}, u32[]{:S(2)}) collective-permute-start(bf16[3,8,8,128]{3,2,1,0:T(8,128)(2,1)} %refs_0_.3), channel_id=1, source_target_pairs={{8,0},{16,8},{24,16},{0,24},{9,1},{17,9},{25,17},{1,25},{10,2},{18... | collective-permute-start | bytes 147464 | tf_op jit(solution)/shard_map/ppermute | solution.py:304
  12.9 0.0 collective-permute-done.tl
  12.9 0.0 collective-permute-done.1.tr
  12.9 0.0 copy-start.3
  13.0 0.0 copy-start.4
  13.0 0.0 copy-start.5
  13.0 0.0 copy-start.6
  13.0 0.0 copy-start.7
  13.0 0.0 copy-start.8
  13.0 0.5 %first.1 = (f32[16,64,256]{2,1,0:T(8,128)S(1)}, bf16[2,32,256]{2,1,0:T(8,128)(2,1)S(1)}, bf16[2,64,256]{2,1,0:T(8,128)(2,1)S(1)}, bf16[2,64,256]{2,1,0:T(8,128)(2,1)S(1)}) custom-call(f32[1]{0:T(128)S(6)} %copy.12.kap, f32[16,64,256]{2,1,0:T(8,128)S(1)} %bitcast.5, bf16[160,256]{1,0:T(8,128)(2,1)S(1)} %collective-permute-done.tl, ...), custom_call_target="tpu_custom_call" | custom-call | tf_op jit(solution)/shard_map/first/pallas_call | solution.py:310
  13.5 0.1 collective-permute-start.5
  13.6 4.7 %collective-permute-start.6 = (bf16[2,64,256]{2,1,0:T(8,128)(2,1)S(1)}, bf16[2,64,256]{2,1,0:T(8,128)(2,1)S(1)}, u32[]{:S(2)}, u32[]{:S(2)}) collective-permute-start(bf16[2,64,256]{2,1,0:T(8,128)(2,1)S(1)} %get-tuple-element.18), channel_id=1, source_target_pairs={{1,0},{2,1},{3,2},{4,3},{5,4},{6,5},{7,6},{0,7},{9,8},{10,9},{11,1... | collective-permute-start | bytes 196616 | tf_op jit(solution)/shard_map/ppermute | solution.py:320
  18.3 0.0 collective-permute-done.4.refs_3_
  18.3 0.9 %collective-permute-start.8 = (bf16[2,32,256]{2,1,0:T(8,128)(2,1)S(1)}, bf16[2,32,256]{2,1,0:T(8,128)(2,1)S(1)}, u32[]{:S(2)}, u32[]{:S(2)}) collective-permute-start(bf16[2,32,256]{2,1,0:T(8,128)(2,1)S(1)} %get-tuple-element.19.refs_4_), channel_id=1, source_target_pairs={{16,0},{24,8},{0,16},{8,24},{17,1},{25,9},{1,17},{9,25},{18,2},{26... | collective-permute-start | bytes 98312 | tf_op jit(solution)/shard_map/ppermute | solution.py:304
  19.2 1.4 %collective-permute-start.7 = (bf16[2,32,256]{2,1,0:T(8,128)(2,1)S(1)}, bf16[2,32,256]{2,1,0:T(8,128)(2,1)S(1)}, u32[]{:S(2)}, u32[]{:S(2)}) collective-permute-start(bf16[2,32,256]{2,1,0:T(8,128)(2,1)S(1)} %get-tuple-element.19.refs_4_), channel_id=1, source_target_pairs={{8,0},{16,8},{24,16},{0,24},{9,1},{17,9},{25,17},{1,25},{10,2},{18... | collective-permute-start | bytes 98312 | tf_op jit(solution)/shard_map/ppermute | solution.py:304
  20.6 0.0 copy-start.2
  20.6 3.1 %inner.1 = (f32[16,64,256]{2,1,0:T(8,128)S(1)}, f32[16,64,256]{2,1,0:T(8,128)S(1)}) custom-call(s32[1]{0:T(128)} %bitcast.part.index, f32[1]{0:T(128)S(6)} %copy.12.kap, f32[16,64,256]{2,1,0:T(8,128)S(1)} %bitcast.6, f32[16,64,256]{2,1,0:T(8,128)S(1)} %get-tuple-element.14.gx, bf16[3,8,8,128]{3,2,1,0:T(8,128)(2,1)} %refs_0_.3, ...), custom_call_target="tpu_custom_call" | custom-call | tf_op jit(solution)/shard_map/inner/pallas_call | solution.py:322
  23.8 4.2 %final.1 = (f32[16,64,256]{2,1,0:T(8,128)}, f32[16,64,256]{2,1,0:T(8,128)}) custom-call(s32[1]{0:T(128)} %bitcast.part.index, f32[16,64,256]{2,1,0:T(8,128)S(1)} %bitcast.7, f32[16,64,256]{2,1,0:T(8,128)S(1)} %bitcast.8, f32[16,64,256]{2,1,0:T(8,128)S(1)} %get-tuple-element.15.part, f32[16,64,256]{2,1,0:T(8,128)S(1)} %get-tuple-element.16.inner, ...), custom_call_target="tpu_custom_call" | custom-call | tf_op jit(solution)/shard_map/final/pallas_call | solution.py:330
  (18 shorter events, 0.0 us)
Async XLA Ops:
  0.6 1.2 %copy-start = (f32[1,16,64,256]{3,2,1,0:T(8,128)S(1)}, f32[1,16,64,256]{3,2,1,0:T(8,128)}, u32[]{:S(2)}) copy-start(f32[1,16,64,256]{3,2,1,0:T(8,128)} %theta.1) | copy-start | bytes 3145732
  1.9 11.1 %copy-start.1 = (f32[1,16,64,256]{3,2,1,0:T(8,128)S(1)}, f32[1,16,64,256]{3,2,1,0:T(8,128)}, u32[]{:S(2)}) copy-start(f32[1,16,64,256]{3,2,1,0:T(8,128)} %theta.1) | copy-start | bytes 3145732
  3.0 9.9 %collective-permute-start = (bf16[160,256]{1,0:T(8,128)(2,1)S(1)}, bf16[160,256]{1,0:T(8,128)(2,1)S(1)}, u32[]{:S(2)}, u32[]{:S(2)}) collective-permute-start(bf16[160,256]{1,0:T(8,128)(2,1)S(1)} %get-tuple-element.12), channel_id=1, source_target_pairs={{0,1},{1,2},{2,3},{3,4},{4,5},{5,6},{6,7},{7,0},{8,9},{9,10},{10,1... | collective-permute-start | bytes 245768 | tf_op jit(solution)/shard_map/ppermute | solution.py:307
  6.1 6.8 %collective-permute-start.1 = (bf16[160,256]{1,0:T(8,128)(2,1)S(1)}, bf16[160,256]{1,0:T(8,128)(2,1)S(1)}, u32[]{:S(2)}, u32[]{:S(2)}) collective-permute-start(bf16[160,256]{1,0:T(8,128)(2,1)S(1)} %get-tuple-element.13), channel_id=1, source_target_pairs={{1,0},{2,1},{3,2},{4,3},{5,4},{6,5},{7,6},{0,7},{9,8},{10,9},{11,1... | collective-permute-start | bytes 245768 | tf_op jit(solution)/shard_map/ppermute | solution.py:308
  9.2 9.1 %collective-permute-start.4 = (bf16[3,8,8,128]{3,2,1,0:T(8,128)(2,1)}, bf16[3,8,8,128]{3,2,1,0:T(8,128)(2,1)S(1)}, u32[]{:S(2)}, u32[]{:S(2)}) collective-permute-start(bf16[3,8,8,128]{3,2,1,0:T(8,128)(2,1)} %refs_0_.3), channel_id=1, source_target_pairs={{24,0},{0,8},{8,16},{16,24},{25,1},{1,9},{9,17},{17,25},{26,2},{2,... | collective-permute-start | bytes 147464 | tf_op jit(solution)/shard_map/ppermute | solution.py:304
  9.2 9.1 %collective-permute-start.3 = (bf16[3,8,8,128]{3,2,1,0:T(8,128)(2,1)}, bf16[3,8,8,128]{3,2,1,0:T(8,128)(2,1)S(1)}, u32[]{:S(2)}, u32[]{:S(2)}) collective-permute-start(bf16[3,8,8,128]{3,2,1,0:T(8,128)(2,1)} %refs_0_.3), channel_id=1, source_target_pairs={{16,0},{24,8},{0,16},{8,24},{17,1},{25,9},{1,17},{9,25},{18,2},{26... | collective-permute-start | bytes 147464 | tf_op jit(solution)/shard_map/ppermute | solution.py:304
  10.8 8.4 %collective-permute-start.2 = (bf16[3,8,8,128]{3,2,1,0:T(8,128)(2,1)}, bf16[3,8,8,128]{3,2,1,0:T(8,128)(2,1)S(1)}, u32[]{:S(2)}, u32[]{:S(2)}) collective-permute-start(bf16[3,8,8,128]{3,2,1,0:T(8,128)(2,1)} %refs_0_.3), channel_id=1, source_target_pairs={{8,0},{16,8},{24,16},{0,24},{9,1},{17,9},{25,17},{1,25},{10,2},{18... | collective-permute-start | bytes 147464 | tf_op jit(solution)/shard_map/ppermute | solution.py:304
  12.9 7.6 %copy-start.3 = (bf16[2,256,256]{2,1,0:T(8,128)(2,1)S(1)}, bf16[2,256,256]{2,1,0:T(8,128)(2,1)}, u32[]{:S(2)}) copy-start(bf16[2,256,256]{2,1,0:T(8,128)(2,1)} %constant.37.refs_5_.refs_9_) | copy-start | bytes 786436
  13.0 7.6 %copy-start.4 = (bf16[128,256]{1,0:T(8,128)(2,1)S(1)}, bf16[128,256]{1,0:T(8,128)(2,1)}, u32[]{:S(2)}) copy-start(bf16[128,256]{1,0:T(8,128)(2,1)} %constant.22.clone.refs_9_.refs_11_) | copy-start | bytes 196612
  13.0 7.6 %copy-start.5 = (bf16[4,64,64]{2,1,0:T(8,128)(2,1)S(1)}, bf16[4,64,64]{2,1,0:T(8,128)(2,1)}, u32[]{:S(2)}) copy-start(bf16[4,64,64]{2,1,0:T(8,128)(2,1)} %constant.21.clone.refs_8_.refs_10_) | copy-start | bytes 98308
  13.0 7.6 %copy-start.6 = (bf16[2,256,256]{2,1,0:T(8,128)(2,1)S(1)}, bf16[2,256,256]{2,1,0:T(8,128)(2,1)}, u32[]{:S(2)}) copy-start(bf16[2,256,256]{2,1,0:T(8,128)(2,1)} %constant.49.refs_7_) | copy-start | bytes 786436
  13.0 7.6 %copy-start.7 = (bf16[64,192]{1,0:T(8,128)(2,1)S(1)}, bf16[64,192]{1,0:T(8,128)(2,1)}, u32[]{:S(2)}) copy-start(bf16[64,192]{1,0:T(8,128)(2,1)} %constant.30.refs_4_.refs_8_) | copy-start | bytes 73732
  13.0 7.6 %copy-start.8 = (bf16[64,192]{1,0:T(8,128)(2,1)S(1)}, bf16[64,192]{1,0:T(8,128)(2,1)}, u32[]{:S(2)}) copy-start(bf16[64,192]{1,0:T(8,128)(2,1)} %constant.42.refs_6_) | copy-start | bytes 73732
  13.5 10.3 %collective-permute-start.5 = (bf16[2,64,256]{2,1,0:T(8,128)(2,1)S(1)}, bf16[2,64,256]{2,1,0:T(8,128)(2,1)S(1)}, u32[]{:S(2)}, u32[]{:S(2)}) collective-permute-start(bf16[2,64,256]{2,1,0:T(8,128)(2,1)S(1)} %get-tuple-element.17), channel_id=1, source_target_pairs={{0,1},{1,2},{2,3},{3,4},{4,5},{5,6},{6,7},{7,0},{8,9},{9,10},{10,1... | collective-permute-start | bytes 196616 | tf_op jit(solution)/shard_map/ppermute | solution.py:319
  13.6 10.2 %collective-permute-start.6 = (bf16[2,64,256]{2,1,0:T(8,128)(2,1)S(1)}, bf16[2,64,256]{2,1,0:T(8,128)(2,1)S(1)}, u32[]{:S(2)}, u32[]{:S(2)}) collective-permute-start(bf16[2,64,256]{2,1,0:T(8,128)(2,1)S(1)} %get-tuple-element.18), channel_id=1, source_target_pairs={{1,0},{2,1},{3,2},{4,3},{5,4},{6,5},{7,6},{0,7},{9,8},{10,9},{11,1... | collective-permute-start | bytes 196616 | tf_op jit(solution)/shard_map/ppermute | solution.py:320
  18.3 5.5 %collective-permute-start.9 = (bf16[2,32,256]{2,1,0:T(8,128)(2,1)S(1)}, bf16[2,32,256]{2,1,0:T(8,128)(2,1)S(1)}, u32[]{:S(2)}, u32[]{:S(2)}) collective-permute-start(bf16[2,32,256]{2,1,0:T(8,128)(2,1)S(1)} %get-tuple-element.19.refs_4_), channel_id=1, source_target_pairs={{24,0},{0,8},{8,16},{16,24},{25,1},{1,9},{9,17},{17,25},{26,2},{2,... | collective-permute-start | bytes 98312 | tf_op jit(solution)/shard_map/ppermute | solution.py:304
  18.3 5.5 %collective-permute-start.8 = (bf16[2,32,256]{2,1,0:T(8,128)(2,1)S(1)}, bf16[2,32,256]{2,1,0:T(8,128)(2,1)S(1)}, u32[]{:S(2)}, u32[]{:S(2)}) collective-permute-start(bf16[2,32,256]{2,1,0:T(8,128)(2,1)S(1)} %get-tuple-element.19.refs_4_), channel_id=1, source_target_pairs={{16,0},{24,8},{0,16},{8,24},{17,1},{25,9},{1,17},{9,25},{18,2},{26... | collective-permute-start | bytes 98312 | tf_op jit(solution)/shard_map/ppermute | solution.py:304
  19.2 4.6 %collective-permute-start.7 = (bf16[2,32,256]{2,1,0:T(8,128)(2,1)S(1)}, bf16[2,32,256]{2,1,0:T(8,128)(2,1)S(1)}, u32[]{:S(2)}, u32[]{:S(2)}) collective-permute-start(bf16[2,32,256]{2,1,0:T(8,128)(2,1)S(1)} %get-tuple-element.19.refs_4_), channel_id=1, source_target_pairs={{8,0},{16,8},{24,16},{0,24},{9,1},{17,9},{25,17},{1,25},{10,2},{18... | collective-permute-start | bytes 98312 | tf_op jit(solution)/shard_map/ppermute | solution.py:304
  20.6 3.2 %copy-start.2 = (f32[1,16,64,256]{3,2,1,0:T(8,128)S(1)}, f32[1,16,64,256]{3,2,1,0:T(8,128)}, u32[]{:S(2)}) copy-start(f32[1,16,64,256]{3,2,1,0:T(8,128)} %param.11) | copy-start | bytes 3145732

commit v5 on v4

--- a/solution.py
+++ b/solution.py
@@ -64,6 +64,11 @@
 
 def dot3(a, b):
     return dot(a[0], b[0]) + (dot(a[0], b[1]) + dot(a[1], b[0]))
+
+
+def widen(half):
+    mid = half.shape[1] // 2
+    return [jnp.concatenate([k, jnp.concatenate([k[mid:], k[:mid]], axis=0)], axis=1) for k in (half[0], half[1])]
 
 
 def along_y(op, x, ny):
@@ -111,7 +116,7 @@
 FIRST, COUNT = (0, 3, 5), (3, 2, 2)
 
 
-def pack_kernel(theta, velocity, head, tail, low, high, vel, sems):
+def pack_kernel(theta, velocity, head, tail, vel, low, high, sems):
     planes, ny, nz = theta.shape[1:]
     coarse, rows, nzc = velocity.shape[1:]
     copies = (
@@ -215,6 +220,7 @@
     planes, ny, nz = th.shape
     per = max(1, MXU // ny)
     kappa = kap[0]
+    kz, kz2 = widen(kz), widen(kz2)
     flow = flow_of(part, vel, None, ry, rz)
     for g in range(planes // per):
         at = slice(g * per, (g + 1) * per)
@@ -227,9 +233,10 @@
 
 
 def final_kernel(ngrp, index, th, reg, part, inner, gx, tl, tr, gl, gr, *refs):
-    vel, halo, (ky, kz, ry, rz, new, saved, flux, acc) = refs[:ngrp], refs[ngrp : 2 * ngrp], refs[2 * ngrp :]
+    vel, halo, (ky, kz, ry, rz, new_hbm, saved_hbm, new, saved, flux, acc, sems) = refs[:ngrp], refs[ngrp : 2 * ngrp], refs[2 * ngrp :]
     planes, ny, nz = th.shape
     per = max(1, MXU // ny)
+    kz = widen(kz)
     flow = flow_of(index, vel, halo, ry, rz)
     get = padded(th, tl, tr)
     outer = [g for g in range(planes // per) if not is_inner(g, per, planes)]
@@ -256,8 +263,16 @@
         kept = RK_A * reg[i] - STEP * (value + rest)
         saved[i] = kept
         new[i] = th[i] + RK_B * kept
-
+        if i % per == 0:
+            at = pl.ds(i, per)
+            for k, (src, dst) in enumerate(((saved, saved_hbm), (new, new_hbm))):
+                copies.append(pltpu.make_async_copy(src.at[at], dst.at[at], sems.at[2 * (i // per) + k]))
+                copies[-1].start()
+
+    copies = []
     x_derivative(flux_at, put, saved, planes)
+    for copy in copies:
+        copy.wait()
 
 
 def shards(theta, register, velocity, diffusivity):
@@ -268,8 +283,8 @@
     up = [(i, (i + 1) % nslab) for i in range(nslab)]
     down = [((i + 1) % nslab, i) for i in range(nslab)]
     op_y, op_z = blocked_operator(ny, BLK), blocked_operator(nz, BLK)
-    ky2, kz2 = host_stack(op_y @ op_y), host_split((op_z @ op_z).T)
-    ky, kz = host_stack(op_y), host_split(op_z.T)
+    ky2, kz2 = host_stack(op_y @ op_y), host_split((op_z @ op_z).T[:, : nz // 2])
+    ky, kz = host_stack(op_y), host_split(op_z.T[:, : nz // 2])
     turned = [np.roll(refine_operator(nyc), -g * (nyc // ngrp), axis=1) for g in range(ngrp)]
     ry = jnp.asarray(np.stack([np.tile(m, (1, 2)) for m in turned]), bf16)
     rz = jnp.asarray(refine_operator(nzc).T, bf16)
@@ -283,16 +298,14 @@
     smem = pl.BlockSpec(memory_space=pltpu.SMEM)
     grant = lambda mib: pltpu.CompilerParams(vmem_limit_bytes=mib * 1024 * 1024)
 
-    anywhere = pl.BlockSpec(memory_space=pl.ANY)
-    head, tail = pl.pallas_call(
+    head, tail, own = pl.pallas_call(
         pack_kernel,
-        out_shape=(packed, packed),
-        in_specs=[anywhere] * 2,
-        out_specs=(vmem,) * 2,
+        out_shape=(packed, packed, jax.ShapeDtypeStruct(velocity.shape, bf16)),
+        in_specs=[pl.BlockSpec(memory_space=pltpu.HBM)] * 2,
+        out_specs=(vmem,) * 3,
         scratch_shapes=[
             pltpu.VMEM((2, ny, nz), f32),
             pltpu.VMEM((2, ny, nz), f32),
-            pltpu.VMEM(velocity.shape, bf16),
             pltpu.SemaphoreType.DMA((3,)),
         ],
         compiler_params=grant(4),
@@ -306,7 +319,7 @@
     part = lax.axis_index("grp").astype(jnp.int32)[None]
     left = lax.ppermute(tail, "slab", up)
     right = lax.ppermute(head, "slab", down)
-    vel = gathered(velocity)
+    vel = gathered(own)
     gx, halo, tail, head = pl.pallas_call(
         first_kernel,
         out_shape=(full, jax.ShapeDtypeStruct((2, 4 * rows, nz), bf16), edge, edge),
@@ -331,8 +344,14 @@
         functools.partial(final_kernel, ngrp),
         out_shape=(full, full),
         in_specs=[smem] + [vmem] * (13 + 2 * ngrp),
-        out_specs=(vmem,) * 2,
-        scratch_shapes=[pltpu.VMEM((planes + 4, ny, nz), f32), pltpu.VMEM((planes, ny, nz), f32)],
+        out_specs=(pl.BlockSpec(memory_space=pltpu.HBM),) * 2,
+        scratch_shapes=[
+            pltpu.VMEM((planes, ny, nz), f32),
+            pltpu.VMEM((planes, ny, nz), f32),
+            pltpu.VMEM((planes + 4, ny, nz), f32),
+            pltpu.VMEM((planes, ny, nz), f32),
+            pltpu.SemaphoreType.DMA((2 * planes,)),
+        ],
         compiler_params=grant(14),
         name="final",
     )(part, field, saved, acc, inner, gx, left, right, grad_l, grad_r, *vel, *halo, ky, kz, ry, rz)

time: 28.3 us -> 26.9 us (0.951)
  Pallas kernels: 9.02 us -> 6.79 us
  local copies, waits for them, and re-layouts: 1.27 us -> 2.07 us
    pallas_call x1, Pallas kernels: 3.12 us -> 2.25 us  [shards(): pl.pallas_call(functools.partial(inner_kernel, ngrp), out_shape=(full, fu...]
    unnamed x18 -> x20, local copies, waits for them, and re-layouts: 1.27 us -> 2.07 us
    pallas_call x1, Pallas kernels: 1.18 us -> 0.42 us  [shards(): pl.pallas_call(pack_kernel, out_shape=(packed, packed, jax.ShapeDtypeStru...]
    pallas_call x1, Pallas kernels: 4.23 us -> 3.64 us  [shards(): pl.pallas_call(functools.partial(final_kernel, ngrp), out_shape=(full, fu...]
  transfers between devices with their start and end apart: 10 -> 10, of which waited for: 0 -> 0; matrix products, arithmetic and copies ran while one was open for 0% -> 0% of each run, Pallas kernels for 13% -> 10%
where the time goes in v5:
time: 26.9 us; the launch traced here: 26.6 us
  starting transfers between devices  16.3 us (61%)
  Pallas kernels  6.79 us (25%)
  local copies, waits for them, and re-layouts  2.07 us (8%)
  between operations  1.48 us (6%)
    ppermute x6, starting transfers between devices, gathered(): return [x] + [lax.ppermute(x, 'grp', turn) for turn in turns]  5.34 us
    ppermute x1, starting transfers between devices, shards(): grad_r = lax.ppermute(head, 'slab', down)  4.71 us
    pallas_call x1, Pallas kernels, shards(): pl.pallas_call(functools.partial(final_kernel, ngrp), out_shape=(full, fu...  3.64 us
    ppermute x1, starting transfers between devices, shards(): right = lax.ppermute(head, 'slab', down)  3.1 us
    ppermute x1, starting transfers between devices, shards(): left = lax.ppermute(tail, 'slab', up)  3.05 us
    pallas_call x1, Pallas kernels, shards(): pl.pallas_call(functools.partial(inner_kernel, ngrp), out_shape=(full, fu...  2.25 us
    unnamed x20, local copies, waits for them, and re-layouts  2.07 us
  transfers between devices with their start and end apart: 10, of which 0 were waited for; matrix products, arithmetic and copies ran while one was open for 0% of the time, Pallas kernels for 10%

profile of v5, /device:TPU:0, one launch (start us, length us, event | category | flops | bytes accessed | tf_op | source)
XLA Modules:
  0.0 26.6 jit_solution(3974073517093113736)
XLA Ops:
  0.6 1.2 %copy-done = f32[1,16,64,256]{3,2,1,0:T(8,128)S(1)} copy-done((f32[1,16,64,256]{3,2,1,0:T(8,128)S(1)}, f32[1,16,64,256]{3,2,1,0:T(8,128)}, u32[]{:S(2)}) %copy-start) | copy-done | bytes 1048600
  1.9 0.8 %copy-done.8 = bf16[3,8,8,128]{3,2,1,0:T(8,128)(2,1)S(1)} copy-done((bf16[3,8,8,128]{3,2,1,0:T(8,128)(2,1)S(1)}, bf16[3,8,8,128]{3,2,1,0:T(8,128)(2,1)}, u32[]{:S(2)}) %copy-start.8) | copy-done | bytes 49176
  2.7 0.4 %pack.1 = (bf16[160,256]{1,0:T(8,128)(2,1)S(1)}, bf16[160,256]{1,0:T(8,128)(2,1)S(1)}, bf16[3,8,8,128]{3,2,1,0:T(8,128)(2,1)S(1)}) custom-call(f32[1,16,64,256]{3,2,1,0:T(8,128)S(1)} %copy-done, bf16[3,8,8,128]{3,2,1,0:T(8,128)(2,1)S(1)} %copy-done.8), custom_call_target="tpu_custom_call" | custom-call | tf_op jit(solution)/shard_map/pack/pallas_call | solution.py:301
  3.1 3.0 %collective-permute-start = (bf16[160,256]{1,0:T(8,128)(2,1)S(1)}, bf16[160,256]{1,0:T(8,128)(2,1)S(1)}, u32[]{:S(2)}, u32[]{:S(2)}) collective-permute-start(bf16[160,256]{1,0:T(8,128)(2,1)S(1)} %get-tuple-element.13), channel_id=1, source_target_pairs={{0,1},{1,2},{2,3},{3,4},{4,5},{5,6},{6,7},{7,0},{8,9},{9,10},{10,1... | collective-permute-start | bytes 245768 | tf_op jit(solution)/shard_map/ppermute | solution.py:320
  6.1 3.1 %collective-permute-start.1 = (bf16[160,256]{1,0:T(8,128)(2,1)S(1)}, bf16[160,256]{1,0:T(8,128)(2,1)S(1)}, u32[]{:S(2)}, u32[]{:S(2)}) collective-permute-start(bf16[160,256]{1,0:T(8,128)(2,1)S(1)} %get-tuple-element.14), channel_id=1, source_target_pairs={{1,0},{2,1},{3,2},{4,3},{5,4},{6,5},{7,6},{0,7},{9,8},{10,9},{11,1... | collective-permute-start | bytes 245768 | tf_op jit(solution)/shard_map/ppermute | solution.py:321
  9.2 0.0 collective-permute-start.4
  9.2 1.6 %collective-permute-start.3 = (bf16[3,8,8,128]{3,2,1,0:T(8,128)(2,1)S(1)}, bf16[3,8,8,128]{3,2,1,0:T(8,128)(2,1)S(1)}, u32[]{:S(2)}, u32[]{:S(2)}) collective-permute-start(bf16[3,8,8,128]{3,2,1,0:T(8,128)(2,1)S(1)} %get-tuple-element.16.refs_0_), channel_id=1, source_target_pairs={{16,0},{24,8},{0,16},{8,24},{17,1},{25,9},{1,17},{9,25},{18,2},{26... | collective-permute-start | bytes 147464 | tf_op jit(solution)/shard_map/ppermute | solution.py:317
  10.8 1.5 %collective-permute-start.2 = (bf16[3,8,8,128]{3,2,1,0:T(8,128)(2,1)S(1)}, bf16[3,8,8,128]{3,2,1,0:T(8,128)(2,1)S(1)}, u32[]{:S(2)}, u32[]{:S(2)}) collective-permute-start(bf16[3,8,8,128]{3,2,1,0:T(8,128)(2,1)S(1)} %get-tuple-element.16.refs_0_), channel_id=1, source_target_pairs={{8,0},{16,8},{24,16},{0,24},{9,1},{17,9},{25,17},{1,25},{10,2},{18... | collective-permute-start | bytes 147464 | tf_op jit(solution)/shard_map/ppermute | solution.py:317
  13.0 0.0 collective-permute-done.1.tr
  13.0 0.0 copy-start.3
  13.0 0.0 copy-start.4
  13.0 0.0 copy-start.5
  13.0 0.0 copy-start.6
  13.0 0.0 copy-start.7
  13.0 0.0 copy-start.9
  13.1 0.5 %first.1 = (f32[16,64,256]{2,1,0:T(8,128)S(1)}, bf16[2,32,256]{2,1,0:T(8,128)(2,1)S(1)}, bf16[2,64,256]{2,1,0:T(8,128)(2,1)S(1)}, bf16[2,64,256]{2,1,0:T(8,128)(2,1)S(1)}) custom-call(f32[1]{0:T(128)S(6)} %copy.12.kap, f32[16,64,256]{2,1,0:T(8,128)S(1)} %bitcast.5, bf16[160,256]{1,0:T(8,128)(2,1)S(1)} %collective-permute-done.tl, ...), custom_call_target="tpu_custom_call" | custom-call | tf_op jit(solution)/shard_map/first/pallas_call | solution.py:323
  13.5 0.1 collective-permute-start.5
  13.6 4.7 %collective-permute-start.6 = (bf16[2,64,256]{2,1,0:T(8,128)(2,1)S(1)}, bf16[2,64,256]{2,1,0:T(8,128)(2,1)S(1)}, u32[]{:S(2)}, u32[]{:S(2)}) collective-permute-start(bf16[2,64,256]{2,1,0:T(8,128)(2,1)S(1)} %get-tuple-element.20), channel_id=1, source_target_pairs={{1,0},{2,1},{3,2},{4,3},{5,4},{6,5},{7,6},{0,7},{9,8},{10,9},{11,1... | collective-permute-start | bytes 196616 | tf_op jit(solution)/shard_map/ppermute | solution.py:333
  18.3 0.9 %collective-permute-start.8 = (bf16[2,32,256]{2,1,0:T(8,128)(2,1)S(1)}, bf16[2,32,256]{2,1,0:T(8,128)(2,1)S(1)}, u32[]{:S(2)}, u32[]{:S(2)}) collective-permute-start(bf16[2,32,256]{2,1,0:T(8,128)(2,1)S(1)} %get-tuple-element.21.refs_4_), channel_id=1, source_target_pairs={{16,0},{24,8},{0,16},{8,24},{17,1},{25,9},{1,17},{9,25},{18,2},{26... | collective-permute-start | bytes 98312 | tf_op jit(solution)/shard_map/ppermute | solution.py:317
  19.2 1.4 %collective-permute-start.7 = (bf16[2,32,256]{2,1,0:T(8,128)(2,1)S(1)}, bf16[2,32,256]{2,1,0:T(8,128)(2,1)S(1)}, u32[]{:S(2)}, u32[]{:S(2)}) collective-permute-start(bf16[2,32,256]{2,1,0:T(8,128)(2,1)S(1)} %get-tuple-element.21.refs_4_), channel_id=1, source_target_pairs={{8,0},{16,8},{24,16},{0,24},{9,1},{17,9},{25,17},{1,25},{10,2},{18... | collective-permute-start | bytes 98312 | tf_op jit(solution)/shard_map/ppermute | solution.py:317
  20.6 0.0 copy-start.2
  20.7 2.2 %inner.1 = (f32[16,64,256]{2,1,0:T(8,128)S(1)}, f32[16,64,256]{2,1,0:T(8,128)S(1)}) custom-call(s32[1]{0:T(128)} %bitcast.part.index, f32[1]{0:T(128)S(6)} %copy.12.kap, f32[16,64,256]{2,1,0:T(8,128)S(1)} %bitcast.6, f32[16,64,256]{2,1,0:T(8,128)S(1)} %get-tuple-element.15.gx, bf16[3,8,8,128]{3,2,1,0:T(8,128)(2,1)S(1)} %get-tuple-element.16.refs_0_, ...), custom_call_target="tpu_custom_call" | custom-call | tf_op jit(solution)/shard_map/inner/pallas_call | solution.py:335
  22.9 0.0 collective-permute-done.9.refs_7_
  23.0 3.6 %final.1 = (f32[16,64,256]{2,1,0:T(8,128)}, f32[16,64,256]{2,1,0:T(8,128)}) custom-call(s32[1]{0:T(128)} %bitcast.part.index, f32[16,64,256]{2,1,0:T(8,128)S(1)} %bitcast.7, f32[16,64,256]{2,1,0:T(8,128)S(1)} %bitcast.8, f32[16,64,256]{2,1,0:T(8,128)S(1)} %get-tuple-element.17.part, f32[16,64,256]{2,1,0:T(8,128)S(1)} %get-tuple-element.18.inner, ...), custom_call_target="tpu_custom_call" | custom-call | tf_op jit(solution)/shard_map/final/pallas_call | solution.py:343
  (20 shorter events, 0.0 us)
Async XLA Ops:
  0.6 1.2 %copy-start = (f32[1,16,64,256]{3,2,1,0:T(8,128)S(1)}, f32[1,16,64,256]{3,2,1,0:T(8,128)}, u32[]{:S(2)}) copy-start(f32[1,16,64,256]{3,2,1,0:T(8,128)} %theta.1) | copy-start | bytes 3145732
  1.9 0.8 %copy-start.8 = (bf16[3,8,8,128]{3,2,1,0:T(8,128)(2,1)S(1)}, bf16[3,8,8,128]{3,2,1,0:T(8,128)(2,1)}, u32[]{:S(2)}) copy-start(bf16[3,8,8,128]{3,2,1,0:T(8,128)(2,1)} %velocity.1) | copy-start | bytes 147460
  2.7 10.3 %copy-start.1 = (f32[1,16,64,256]{3,2,1,0:T(8,128)S(1)}, f32[1,16,64,256]{3,2,1,0:T(8,128)}, u32[]{:S(2)}) copy-start(f32[1,16,64,256]{3,2,1,0:T(8,128)} %theta.1) | copy-start | bytes 3145732
  3.1 9.9 %collective-permute-start = (bf16[160,256]{1,0:T(8,128)(2,1)S(1)}, bf16[160,256]{1,0:T(8,128)(2,1)S(1)}, u32[]{:S(2)}, u32[]{:S(2)}) collective-permute-start(bf16[160,256]{1,0:T(8,128)(2,1)S(1)} %get-tuple-element.13), channel_id=1, source_target_pairs={{0,1},{1,2},{2,3},{3,4},{4,5},{5,6},{6,7},{7,0},{8,9},{9,10},{10,1... | collective-permute-start | bytes 245768 | tf_op jit(solution)/shard_map/ppermute | solution.py:320
  6.1 6.8 %collective-permute-start.1 = (bf16[160,256]{1,0:T(8,128)(2,1)S(1)}, bf16[160,256]{1,0:T(8,128)(2,1)S(1)}, u32[]{:S(2)}, u32[]{:S(2)}) collective-permute-start(bf16[160,256]{1,0:T(8,128)(2,1)S(1)} %get-tuple-element.14), channel_id=1, source_target_pairs={{1,0},{2,1},{3,2},{4,3},{5,4},{6,5},{7,6},{0,7},{9,8},{10,9},{11,1... | collective-permute-start | bytes 245768 | tf_op jit(solution)/shard_map/ppermute | solution.py:321
  9.2 9.1 %collective-permute-start.4 = (bf16[3,8,8,128]{3,2,1,0:T(8,128)(2,1)S(1)}, bf16[3,8,8,128]{3,2,1,0:T(8,128)(2,1)S(1)}, u32[]{:S(2)}, u32[]{:S(2)}) collective-permute-start(bf16[3,8,8,128]{3,2,1,0:T(8,128)(2,1)S(1)} %get-tuple-element.16.refs_0_), channel_id=1, source_target_pairs={{24,0},{0,8},{8,16},{16,24},{25,1},{1,9},{9,17},{17,25},{26,2},{2,... | collective-permute-start | bytes 147464 | tf_op jit(solution)/shard_map/ppermute | solution.py:317
  9.2 9.1 %collective-permute-start.3 = (bf16[3,8,8,128]{3,2,1,0:T(8,128)(2,1)S(1)}, bf16[3,8,8,128]{3,2,1,0:T(8,128)(2,1)S(1)}, u32[]{:S(2)}, u32[]{:S(2)}) collective-permute-start(bf16[3,8,8,128]{3,2,1,0:T(8,128)(2,1)S(1)} %get-tuple-element.16.refs_0_), channel_id=1, source_target_pairs={{16,0},{24,8},{0,16},{8,24},{17,1},{25,9},{1,17},{9,25},{18,2},{26... | collective-permute-start | bytes 147464 | tf_op jit(solution)/shard_map/ppermute | solution.py:317
  10.8 8.4 %collective-permute-start.2 = (bf16[3,8,8,128]{3,2,1,0:T(8,128)(2,1)S(1)}, bf16[3,8,8,128]{3,2,1,0:T(8,128)(2,1)S(1)}, u32[]{:S(2)}, u32[]{:S(2)}) collective-permute-start(bf16[3,8,8,128]{3,2,1,0:T(8,128)(2,1)S(1)} %get-tuple-element.16.refs_0_), channel_id=1, source_target_pairs={{8,0},{16,8},{24,16},{0,24},{9,1},{17,9},{25,17},{1,25},{10,2},{18... | collective-permute-start | bytes 147464 | tf_op jit(solution)/shard_map/ppermute | solution.py:317
  13.0 7.6 %copy-start.3 = (bf16[2,256,128]{2,1,0:T(8,128)(2,1)S(1)}, bf16[2,256,128]{2,1,0:T(8,128)(2,1)}, u32[]{:S(2)}) copy-start(bf16[2,256,128]{2,1,0:T(8,128)(2,1)} %constant.37.refs_5_.refs_9_) | copy-start | bytes 393220
  13.0 7.6 %copy-start.4 = (bf16[128,256]{1,0:T(8,128)(2,1)S(1)}, bf16[128,256]{1,0:T(8,128)(2,1)}, u32[]{:S(2)}) copy-start(bf16[128,256]{1,0:T(8,128)(2,1)} %constant.22.clone.refs_9_.refs_11_) | copy-start | bytes 196612
  13.0 7.6 %copy-start.5 = (bf16[4,64,64]{2,1,0:T(8,128)(2,1)S(1)}, bf16[4,64,64]{2,1,0:T(8,128)(2,1)}, u32[]{:S(2)}) copy-start(bf16[4,64,64]{2,1,0:T(8,128)(2,1)} %constant.21.clone.refs_8_.refs_10_) | copy-start | bytes 98308
  13.0 7.6 %copy-start.6 = (bf16[64,192]{1,0:T(8,128)(2,1)S(1)}, bf16[64,192]{1,0:T(8,128)(2,1)}, u32[]{:S(2)}) copy-start(bf16[64,192]{1,0:T(8,128)(2,1)} %constant.30.refs_4_.refs_8_) | copy-start | bytes 73732
  13.0 7.6 %copy-start.7 = (bf16[2,256,128]{2,1,0:T(8,128)(2,1)S(1)}, bf16[2,256,128]{2,1,0:T(8,128)(2,1)}, u32[]{:S(2)}) copy-start(bf16[2,256,128]{2,1,0:T(8,128)(2,1)} %constant.49.refs_7_) | copy-start | bytes 393220
  13.0 7.6 %copy-start.9 = (bf16[64,192]{1,0:T(8,128)(2,1)S(1)}, bf16[64,192]{1,0:T(8,128)(2,1)}, u32[]{:S(2)}) copy-start(bf16[64,192]{1,0:T(8,128)(2,1)} %constant.42.refs_6_) | copy-start | bytes 73732
  13.5 9.4 %collective-permute-start.5 = (bf16[2,64,256]{2,1,0:T(8,128)(2,1)S(1)}, bf16[2,64,256]{2,1,0:T(8,128)(2,1)S(1)}, u32[]{:S(2)}, u32[]{:S(2)}) collective-permute-start(bf16[2,64,256]{2,1,0:T(8,128)(2,1)S(1)} %get-tuple-element.19), channel_id=1, source_target_pairs={{0,1},{1,2},{2,3},{3,4},{4,5},{5,6},{6,7},{7,0},{8,9},{9,10},{10,1... | collective-permute-start | bytes 196616 | tf_op jit(solution)/shard_map/ppermute | solution.py:332
  13.6 9.4 %collective-permute-start.6 = (bf16[2,64,256]{2,1,0:T(8,128)(2,1)S(1)}, bf16[2,64,256]{2,1,0:T(8,128)(2,1)S(1)}, u32[]{:S(2)}, u32[]{:S(2)}) collective-permute-start(bf16[2,64,256]{2,1,0:T(8,128)(2,1)S(1)} %get-tuple-element.20), channel_id=1, source_target_pairs={{1,0},{2,1},{3,2},{4,3},{5,4},{6,5},{7,6},{0,7},{9,8},{10,9},{11,1... | collective-permute-start | bytes 196616 | tf_op jit(solution)/shard_map/ppermute | solution.py:333
  18.3 4.6 %collective-permute-start.9 = (bf16[2,32,256]{2,1,0:T(8,128)(2,1)S(1)}, bf16[2,32,256]{2,1,0:T(8,128)(2,1)S(1)}, u32[]{:S(2)}, u32[]{:S(2)}) collective-permute-start(bf16[2,32,256]{2,1,0:T(8,128)(2,1)S(1)} %get-tuple-element.21.refs_4_), channel_id=1, source_target_pairs={{24,0},{0,8},{8,16},{16,24},{25,1},{1,9},{9,17},{17,25},{26,2},{2,... | collective-permute-start | bytes 98312 | tf_op jit(solution)/shard_map/ppermute | solution.py:317
  18.3 4.6 %collective-permute-start.8 = (bf16[2,32,256]{2,1,0:T(8,128)(2,1)S(1)}, bf16[2,32,256]{2,1,0:T(8,128)(2,1)S(1)}, u32[]{:S(2)}, u32[]{:S(2)}) collective-permute-start(bf16[2,32,256]{2,1,0:T(8,128)(2,1)S(1)} %get-tuple-element.21.refs_4_), channel_id=1, source_target_pairs={{16,0},{24,8},{0,16},{8,24},{17,1},{25,9},{1,17},{9,25},{18,2},{26... | collective-permute-start | bytes 98312 | tf_op jit(solution)/shard_map/ppermute | solution.py:317
  19.2 3.7 %collective-permute-start.7 = (bf16[2,32,256]{2,1,0:T(8,128)(2,1)S(1)}, bf16[2,32,256]{2,1,0:T(8,128)(2,1)S(1)}, u32[]{:S(2)}, u32[]{:S(2)}) collective-permute-start(bf16[2,32,256]{2,1,0:T(8,128)(2,1)S(1)} %get-tuple-element.21.refs_4_), channel_id=1, source_target_pairs={{8,0},{16,8},{24,16},{0,24},{9,1},{17,9},{25,17},{1,25},{10,2},{18... | collective-permute-start | bytes 98312 | tf_op jit(solution)/shard_map/ppermute | solution.py:317
  20.6 2.3 %copy-start.2 = (f32[1,16,64,256]{3,2,1,0:T(8,128)S(1)}, f32[1,16,64,256]{3,2,1,0:T(8,128)}, u32[]{:S(2)}) copy-start(f32[1,16,64,256]{3,2,1,0:T(8,128)} %param.11) | copy-start | bytes 3145732

commit v6 on v5

--- a/solution.py
+++ b/solution.py
@@ -152,7 +152,7 @@
 
 def first_kernel(kap, th, tl, tr, gx, halo, tail, head, work):
     planes, ny, nz = th.shape
-    kappa = kap[0]
+    kappa = kap[0:1, 0:1]
     def put(i, value):
         value = kappa * value
         gx[i] = value
@@ -219,7 +219,7 @@
     vel, (ky, kz, ky2, kz2, ry, rz, acc, flux) = refs[:ngrp], refs[ngrp:]
     planes, ny, nz = th.shape
     per = max(1, MXU // ny)
-    kappa = kap[0]
+    kappa = kap[0:1, 0:1]
     kz, kz2 = widen(kz), widen(kz2)
     flow = flow_of(part, vel, None, ry, rz)
     for g in range(planes // per):
@@ -310,12 +310,13 @@
         ],
         compiler_params=grant(4),
         name="pack",
-    )(theta, velocity)
+    )(pltpu.with_memory_space_constraint(theta, pltpu.HBM), pltpu.with_memory_space_constraint(velocity, pltpu.HBM))
 
     def gathered(x):
         turns = [[((i + t) % ngrp, i) for i in range(ngrp)] for t in range(1, ngrp)]
         return [x] + [lax.ppermute(x, "grp", turn) for turn in turns]
 
+    kappa = jnp.broadcast_to(diffusivity[:, None], (8, 128))
     part = lax.axis_index("grp").astype(jnp.int32)[None]
     left = lax.ppermute(tail, "slab", up)
     right = lax.ppermute(head, "slab", down)
@@ -323,23 +324,23 @@
     gx, halo, tail, head = pl.pallas_call(
         first_kernel,
         out_shape=(full, jax.ShapeDtypeStruct((2, 4 * rows, nz), bf16), edge, edge),
-        in_specs=[smem] + [vmem] * 3,
+        in_specs=[vmem] * 4,
         out_specs=(vmem,) * 4,
         scratch_shapes=[pltpu.VMEM((planes, ny, nz), f32)],
         compiler_params=grant(8),
         name="first",
-    )(diffusivity, field, left, right)
+    )(kappa, field, left, right)
     grad_l = lax.ppermute(tail, "slab", up)
     grad_r = lax.ppermute(head, "slab", down)
     halo = gathered(halo)
     acc, inner = pl.pallas_call(
         functools.partial(inner_kernel, ngrp),
         out_shape=(full, full),
-        in_specs=[smem] * 2 + [vmem] * (8 + ngrp),
+        in_specs=[smem] + [vmem] * (9 + ngrp),
         out_specs=(vmem,) * 2,
         compiler_params=grant(14),
         name="inner",
-    )(part, diffusivity, field, gx, *vel, ky, kz, ky2, kz2, ry, rz)
+    )(part, kappa, field, gx, *vel, ky, kz, ky2, kz2, ry, rz)
     new, kept = pl.pallas_call(
         functools.partial(final_kernel, ngrp),
         out_shape=(full, full),

time: 26.9 us -> 25.7 us (0.955)
  local copies, waits for them, and re-layouts: 2.07 us -> 0.05 us
  Pallas kernels: 6.79 us -> 7.63 us
    unnamed x20 -> x16, local copies, waits for them, and re-layouts: 2.07 us -> 0.05 us
    pallas_call x1, Pallas kernels: 0.42 us -> 1.1 us  [shards(): pl.pallas_call(pack_kernel, out_shape=(packed, packed, jax.ShapeDtypeStru...]
  transfers between devices with their start and end apart: 10 -> 10, of which waited for: 0 -> 0; matrix products, arithmetic and copies ran while one was open for 0% -> 0% of each run, Pallas kernels for 10% -> 11%
where the time goes in v6:
time: 25.7 us; the launch traced here: 25.5 us
  starting transfers between devices  16.3 us (63%)
  Pallas kernels  7.63 us (30%)
  between operations  1.48 us (6%)
    ppermute x6, starting transfers between devices, gathered(): return [x] + [lax.ppermute(x, 'grp', turn) for turn in turns]  5.34 us
    ppermute x1, starting transfers between devices, shards(): grad_r = lax.ppermute(head, 'slab', down)  4.71 us
    pallas_call x1, Pallas kernels, shards(): pl.pallas_call(functools.partial(final_kernel, ngrp), out_shape=(full, fu...  3.65 us
    ppermute x1, starting transfers between devices, shards(): right = lax.ppermute(head, 'slab', down)  3.1 us
    ppermute x1, starting transfers between devices, shards(): left = lax.ppermute(tail, 'slab', up)  3.05 us
    pallas_call x1, Pallas kernels, shards(): pl.pallas_call(functools.partial(inner_kernel, ngrp), out_shape=(full, fu...  2.26 us
    pallas_call x1, Pallas kernels, shards(): pl.pallas_call(pack_kernel, out_shape=(packed, packed, jax.ShapeDtypeStru...  1.1 us
    pallas_call x1, Pallas kernels, shards(): pl.pallas_call(first_kernel, out_shape=(full, jax.ShapeDtypeStruct((2, 4...  0.62 us
  transfers between devices with their start and end apart: 10, of which 0 were waited for; matrix products, arithmetic and copies ran while one was open for 0% of the time, Pallas kernels for 11%

profile of v6, /device:TPU:0, one launch (start us, length us, event | category | flops | bytes accessed | tf_op | source)
XLA Modules:
  0.0 25.5 jit_solution(160312583170873831)
XLA Ops:
  0.6 1.1 %pack.1 = (bf16[160,256]{1,0:T(8,128)(2,1)S(1)}, bf16[160,256]{1,0:T(8,128)(2,1)S(1)}, bf16[3,8,8,128]{3,2,1,0:T(8,128)(2,1)S(1)}) custom-call(f32[1,16,64,256]{3,2,1,0:T(8,128)} %theta.1, bf16[3,8,8,128]{3,2,1,0:T(8,128)(2,1)} %velocity.1), custom_call_target="tpu_custom_call" | custom-call | tf_op jit(solution)/shard_map/pack/pallas_call | solution.py:301
  1.7 3.0 %collective-permute-start = (bf16[160,256]{1,0:T(8,128)(2,1)S(1)}, bf16[160,256]{1,0:T(8,128)(2,1)S(1)}, u32[]{:S(2)}, u32[]{:S(2)}) collective-permute-start(bf16[160,256]{1,0:T(8,128)(2,1)S(1)} %get-tuple-element.13), channel_id=1, source_target_pairs={{0,1},{1,2},{2,3},{3,4},{4,5},{5,6},{6,7},{7,0},{8,9},{9,10},{10,1... | collective-permute-start | bytes 245768 | tf_op jit(solution)/shard_map/ppermute | solution.py:321
  4.8 3.1 %collective-permute-start.1 = (bf16[160,256]{1,0:T(8,128)(2,1)S(1)}, bf16[160,256]{1,0:T(8,128)(2,1)S(1)}, u32[]{:S(2)}, u32[]{:S(2)}) collective-permute-start(bf16[160,256]{1,0:T(8,128)(2,1)S(1)} %get-tuple-element.14), channel_id=1, source_target_pairs={{1,0},{2,1},{3,2},{4,3},{5,4},{6,5},{7,6},{0,7},{9,8},{10,9},{11,1... | collective-permute-start | bytes 245768 | tf_op jit(solution)/shard_map/ppermute | solution.py:322
  7.9 0.0 collective-permute-start.4
  7.9 1.6 %collective-permute-start.3 = (bf16[3,8,8,128]{3,2,1,0:T(8,128)(2,1)S(1)}, bf16[3,8,8,128]{3,2,1,0:T(8,128)(2,1)S(1)}, u32[]{:S(2)}, u32[]{:S(2)}) collective-permute-start(bf16[3,8,8,128]{3,2,1,0:T(8,128)(2,1)S(1)} %get-tuple-element.16.refs_0_), channel_id=1, source_target_pairs={{16,0},{24,8},{0,16},{8,24},{17,1},{25,9},{1,17},{9,25},{18,2},{26... | collective-permute-start | bytes 147464 | tf_op jit(solution)/shard_map/ppermute | solution.py:317
  9.5 1.5 %collective-permute-start.2 = (bf16[3,8,8,128]{3,2,1,0:T(8,128)(2,1)S(1)}, bf16[3,8,8,128]{3,2,1,0:T(8,128)(2,1)S(1)}, u32[]{:S(2)}, u32[]{:S(2)}) collective-permute-start(bf16[3,8,8,128]{3,2,1,0:T(8,128)(2,1)S(1)} %get-tuple-element.16.refs_0_), channel_id=1, source_target_pairs={{8,0},{16,8},{24,16},{0,24},{9,1},{17,9},{25,17},{1,25},{10,2},{18... | collective-permute-start | bytes 147464 | tf_op jit(solution)/shard_map/ppermute | solution.py:317
  11.6 0.0 collective-permute-done.tl
  11.7 0.0 copy-start.2
  11.7 0.0 copy-start.3
  11.7 0.0 copy-start.4
  11.7 0.0 copy-start.5
  11.7 0.0 copy-start.6
  11.7 0.0 copy-start.7
  11.7 0.6 %first.1 = (f32[16,64,256]{2,1,0:T(8,128)S(1)}, bf16[2,32,256]{2,1,0:T(8,128)(2,1)S(1)}, bf16[2,64,256]{2,1,0:T(8,128)(2,1)S(1)}, bf16[2,64,256]{2,1,0:T(8,128)(2,1)S(1)}) custom-call(f32[8,128]{1,0:T(8,128)S(1)} %broadcast_in_dim.19.kap, f32[16,64,256]{2,1,0:T(8,128)S(1)} %bitcast.7, bf16[160,256]{1,0:T(8,128)(2,1)S(1)} %collective-permute-done.tl, ...), custom_call_target="tpu_custom_call" | custom-call | tf_op jit(solution)/shard_map/first/pallas_call | solution.py:324
  12.4 0.1 collective-permute-start.5
  12.4 4.7 %collective-permute-start.6 = (bf16[2,64,256]{2,1,0:T(8,128)(2,1)S(1)}, bf16[2,64,256]{2,1,0:T(8,128)(2,1)S(1)}, u32[]{:S(2)}, u32[]{:S(2)}) collective-permute-start(bf16[2,64,256]{2,1,0:T(8,128)(2,1)S(1)} %get-tuple-element.20), channel_id=1, source_target_pairs={{1,0},{2,1},{3,2},{4,3},{5,4},{6,5},{7,6},{0,7},{9,8},{10,9},{11,1... | collective-permute-start | bytes 196616 | tf_op jit(solution)/shard_map/ppermute | solution.py:334
  17.1 0.0 collective-permute-done.4.refs_3_
  17.1 0.0 collective-permute-start.9
  17.1 0.0 collective-permute-done.3.refs_2_
  17.1 0.9 %collective-permute-start.8 = (bf16[2,32,256]{2,1,0:T(8,128)(2,1)S(1)}, bf16[2,32,256]{2,1,0:T(8,128)(2,1)S(1)}, u32[]{:S(2)}, u32[]{:S(2)}) collective-permute-start(bf16[2,32,256]{2,1,0:T(8,128)(2,1)S(1)} %get-tuple-element.21.refs_4_), channel_id=1, source_target_pairs={{16,0},{24,8},{0,16},{8,24},{17,1},{25,9},{1,17},{9,25},{18,2},{26... | collective-permute-start | bytes 98312 | tf_op jit(solution)/shard_map/ppermute | solution.py:317
  18.0 1.4 %collective-permute-start.7 = (bf16[2,32,256]{2,1,0:T(8,128)(2,1)S(1)}, bf16[2,32,256]{2,1,0:T(8,128)(2,1)S(1)}, u32[]{:S(2)}, u32[]{:S(2)}) collective-permute-start(bf16[2,32,256]{2,1,0:T(8,128)(2,1)S(1)} %get-tuple-element.21.refs_4_), channel_id=1, source_target_pairs={{8,0},{16,8},{24,16},{0,24},{9,1},{17,9},{25,17},{1,25},{10,2},{18... | collective-permute-start | bytes 98312 | tf_op jit(solution)/shard_map/ppermute | solution.py:317
  19.5 0.0 copy-start.1
  19.5 2.3 %inner.1 = (f32[16,64,256]{2,1,0:T(8,128)S(1)}, f32[16,64,256]{2,1,0:T(8,128)S(1)}) custom-call(s32[1]{0:T(128)} %bitcast.part.index, f32[8,128]{1,0:T(8,128)S(1)} %broadcast_in_dim.19.kap, f32[16,64,256]{2,1,0:T(8,128)S(1)} %bitcast.8, f32[16,64,256]{2,1,0:T(8,128)S(1)} %get-tuple-element.15.gx, bf16[3,8,8,128]{3,2,1,0:T(8,128)(2,1)S(1)} %get-tuple-element.16.refs_0_, ...), custom_call_target="tpu_custom_call" | custom-call | tf_op jit(solution)/shard_map/inner/pallas_call | solution.py:336
  21.8 3.6 %final.1 = (f32[16,64,256]{2,1,0:T(8,128)}, f32[16,64,256]{2,1,0:T(8,128)}) custom-call(s32[1]{0:T(128)} %bitcast.part.index, f32[16,64,256]{2,1,0:T(8,128)S(1)} %bitcast.9, f32[16,64,256]{2,1,0:T(8,128)S(1)} %bitcast.10, f32[16,64,256]{2,1,0:T(8,128)S(1)} %get-tuple-element.17.part, f32[16,64,256]{2,1,0:T(8,128)S(1)} %get-tuple-element.18.inner, ...), custom_call_target="tpu_custom_call" | custom-call | tf_op jit(solution)/shard_map/final/pallas_call | solution.py:344
  (17 shorter events, 0.0 us)
Async XLA Ops:
  0.6 11.0 %copy-start = (f32[1,16,64,256]{3,2,1,0:T(8,128)S(1)}, f32[1,16,64,256]{3,2,1,0:T(8,128)}, u32[]{:S(2)}) copy-start(f32[1,16,64,256]{3,2,1,0:T(8,128)} %theta.1) | copy-start | bytes 3145732
  1.7 9.9 %collective-permute-start = (bf16[160,256]{1,0:T(8,128)(2,1)S(1)}, bf16[160,256]{1,0:T(8,128)(2,1)S(1)}, u32[]{:S(2)}, u32[]{:S(2)}) collective-permute-start(bf16[160,256]{1,0:T(8,128)(2,1)S(1)} %get-tuple-element.13), channel_id=1, source_target_pairs={{0,1},{1,2},{2,3},{3,4},{4,5},{5,6},{6,7},{7,0},{8,9},{9,10},{10,1... | collective-permute-start | bytes 245768 | tf_op jit(solution)/shard_map/ppermute | solution.py:321
  4.8 6.8 %collective-permute-start.1 = (bf16[160,256]{1,0:T(8,128)(2,1)S(1)}, bf16[160,256]{1,0:T(8,128)(2,1)S(1)}, u32[]{:S(2)}, u32[]{:S(2)}) collective-permute-start(bf16[160,256]{1,0:T(8,128)(2,1)S(1)} %get-tuple-element.14), channel_id=1, source_target_pairs={{1,0},{2,1},{3,2},{4,3},{5,4},{6,5},{7,6},{0,7},{9,8},{10,9},{11,1... | collective-permute-start | bytes 245768 | tf_op jit(solution)/shard_map/ppermute | solution.py:322
  7.9 9.2 %collective-permute-start.4 = (bf16[3,8,8,128]{3,2,1,0:T(8,128)(2,1)S(1)}, bf16[3,8,8,128]{3,2,1,0:T(8,128)(2,1)S(1)}, u32[]{:S(2)}, u32[]{:S(2)}) collective-permute-start(bf16[3,8,8,128]{3,2,1,0:T(8,128)(2,1)S(1)} %get-tuple-element.16.refs_0_), channel_id=1, source_target_pairs={{24,0},{0,8},{8,16},{16,24},{25,1},{1,9},{9,17},{17,25},{26,2},{2,... | collective-permute-start | bytes 147464 | tf_op jit(solution)/shard_map/ppermute | solution.py:317
  7.9 9.2 %collective-permute-start.3 = (bf16[3,8,8,128]{3,2,1,0:T(8,128)(2,1)S(1)}, bf16[3,8,8,128]{3,2,1,0:T(8,128)(2,1)S(1)}, u32[]{:S(2)}, u32[]{:S(2)}) collective-permute-start(bf16[3,8,8,128]{3,2,1,0:T(8,128)(2,1)S(1)} %get-tuple-element.16.refs_0_), channel_id=1, source_target_pairs={{16,0},{24,8},{0,16},{8,24},{17,1},{25,9},{1,17},{9,25},{18,2},{26... | collective-permute-start | bytes 147464 | tf_op jit(solution)/shard_map/ppermute | solution.py:317
  9.5 8.5 %collective-permute-start.2 = (bf16[3,8,8,128]{3,2,1,0:T(8,128)(2,1)S(1)}, bf16[3,8,8,128]{3,2,1,0:T(8,128)(2,1)S(1)}, u32[]{:S(2)}, u32[]{:S(2)}) collective-permute-start(bf16[3,8,8,128]{3,2,1,0:T(8,128)(2,1)S(1)} %get-tuple-element.16.refs_0_), channel_id=1, source_target_pairs={{8,0},{16,8},{24,16},{0,24},{9,1},{17,9},{25,17},{1,25},{10,2},{18... | collective-permute-start | bytes 147464 | tf_op jit(solution)/shard_map/ppermute | solution.py:317
  11.7 7.8 %copy-start.2 = (bf16[2,256,128]{2,1,0:T(8,128)(2,1)S(1)}, bf16[2,256,128]{2,1,0:T(8,128)(2,1)}, u32[]{:S(2)}) copy-start(bf16[2,256,128]{2,1,0:T(8,128)(2,1)} %constant.37.refs_5_.refs_9_) | copy-start | bytes 393220
  11.7 7.8 %copy-start.3 = (bf16[128,256]{1,0:T(8,128)(2,1)S(1)}, bf16[128,256]{1,0:T(8,128)(2,1)}, u32[]{:S(2)}) copy-start(bf16[128,256]{1,0:T(8,128)(2,1)} %constant.22.clone.refs_9_.refs_11_) | copy-start | bytes 196612
  11.7 7.8 %copy-start.4 = (bf16[4,64,64]{2,1,0:T(8,128)(2,1)S(1)}, bf16[4,64,64]{2,1,0:T(8,128)(2,1)}, u32[]{:S(2)}) copy-start(bf16[4,64,64]{2,1,0:T(8,128)(2,1)} %constant.21.clone.refs_8_.refs_10_) | copy-start | bytes 98308
  11.7 7.8 %copy-start.5 = (bf16[64,192]{1,0:T(8,128)(2,1)S(1)}, bf16[64,192]{1,0:T(8,128)(2,1)}, u32[]{:S(2)}) copy-start(bf16[64,192]{1,0:T(8,128)(2,1)} %constant.30.refs_4_.refs_8_) | copy-start | bytes 73732
  11.7 7.7 %copy-start.6 = (bf16[2,256,128]{2,1,0:T(8,128)(2,1)S(1)}, bf16[2,256,128]{2,1,0:T(8,128)(2,1)}, u32[]{:S(2)}) copy-start(bf16[2,256,128]{2,1,0:T(8,128)(2,1)} %constant.49.refs_7_) | copy-start | bytes 393220
  11.7 7.7 %copy-start.7 = (bf16[64,192]{1,0:T(8,128)(2,1)S(1)}, bf16[64,192]{1,0:T(8,128)(2,1)}, u32[]{:S(2)}) copy-start(bf16[64,192]{1,0:T(8,128)(2,1)} %constant.42.refs_6_) | copy-start | bytes 73732
  12.4 9.4 %collective-permute-start.5 = (bf16[2,64,256]{2,1,0:T(8,128)(2,1)S(1)}, bf16[2,64,256]{2,1,0:T(8,128)(2,1)S(1)}, u32[]{:S(2)}, u32[]{:S(2)}) collective-permute-start(bf16[2,64,256]{2,1,0:T(8,128)(2,1)S(1)} %get-tuple-element.19), channel_id=1, source_target_pairs={{0,1},{1,2},{2,3},{3,4},{4,5},{5,6},{6,7},{7,0},{8,9},{9,10},{10,1... | collective-permute-start | bytes 196616 | tf_op jit(solution)/shard_map/ppermute | solution.py:333
  12.4 9.4 %collective-permute-start.6 = (bf16[2,64,256]{2,1,0:T(8,128)(2,1)S(1)}, bf16[2,64,256]{2,1,0:T(8,128)(2,1)S(1)}, u32[]{:S(2)}, u32[]{:S(2)}) collective-permute-start(bf16[2,64,256]{2,1,0:T(8,128)(2,1)S(1)} %get-tuple-element.20), channel_id=1, source_target_pairs={{1,0},{2,1},{3,2},{4,3},{5,4},{6,5},{7,6},{0,7},{9,8},{10,9},{11,1... | collective-permute-start | bytes 196616 | tf_op jit(solution)/shard_map/ppermute | solution.py:334
  17.1 4.6 %collective-permute-start.9 = (bf16[2,32,256]{2,1,0:T(8,128)(2,1)S(1)}, bf16[2,32,256]{2,1,0:T(8,128)(2,1)S(1)}, u32[]{:S(2)}, u32[]{:S(2)}) collective-permute-start(bf16[2,32,256]{2,1,0:T(8,128)(2,1)S(1)} %get-tuple-element.21.refs_4_), channel_id=1, source_target_pairs={{24,0},{0,8},{8,16},{16,24},{25,1},{1,9},{9,17},{17,25},{26,2},{2,... | collective-permute-start | bytes 98312 | tf_op jit(solution)/shard_map/ppermute | solution.py:317
  17.1 4.6 %collective-permute-start.8 = (bf16[2,32,256]{2,1,0:T(8,128)(2,1)S(1)}, bf16[2,32,256]{2,1,0:T(8,128)(2,1)S(1)}, u32[]{:S(2)}, u32[]{:S(2)}) collective-permute-start(bf16[2,32,256]{2,1,0:T(8,128)(2,1)S(1)} %get-tuple-element.21.refs_4_), channel_id=1, source_target_pairs={{16,0},{24,8},{0,16},{8,24},{17,1},{25,9},{1,17},{9,25},{18,2},{26... | collective-permute-start | bytes 98312 | tf_op jit(solution)/shard_map/ppermute | solution.py:317
  18.0 3.7 %collective-permute-start.7 = (bf16[2,32,256]{2,1,0:T(8,128)(2,1)S(1)}, bf16[2,32,256]{2,1,0:T(8,128)(2,1)S(1)}, u32[]{:S(2)}, u32[]{:S(2)}) collective-permute-start(bf16[2,32,256]{2,1,0:T(8,128)(2,1)S(1)} %get-tuple-element.21.refs_4_), channel_id=1, source_target_pairs={{8,0},{16,8},{24,16},{0,24},{9,1},{17,9},{25,17},{1,25},{10,2},{18... | collective-permute-start | bytes 98312 | tf_op jit(solution)/shard_map/ppermute | solution.py:317
  19.5 2.3 %copy-start.1 = (f32[1,16,64,256]{3,2,1,0:T(8,128)S(1)}, f32[1,16,64,256]{3,2,1,0:T(8,128)}, u32[]{:S(2)}) copy-start(f32[1,16,64,256]{3,2,1,0:T(8,128)} %param.11) | copy-start | bytes 3145732

commit v7 on v6

--- a/solution.py
+++ b/solution.py
@@ -116,7 +116,7 @@
 FIRST, COUNT = (0, 3, 5), (3, 2, 2)
 
 
-def pack_kernel(theta, velocity, head, tail, vel, low, high, sems):
+def pack_kernel(code, theta, velocity, out_a, out_b, vel, low, high, sems):
     planes, ny, nz = theta.shape[1:]
     coarse, rows, nzc = velocity.shape[1:]
     copies = (
@@ -128,7 +128,8 @@
         copy.start()
     for copy in copies:
         copy.wait()
-    for out, edge, upper in ((head, low, False), (tail, high, True)):
+
+    def fill(out, edge, upper):
         out[: 2 * ny] = edge[...].reshape(2 * ny, nz).astype(jnp.bfloat16)
         for q in range(8):
             c, k = SLOTS[min(q, 6)]
@@ -136,34 +137,70 @@
             top = 2 * ny + rows * (q // 2)
             out[top : top + rows, nzc * (q % 2) : nzc * (q % 2 + 1)] = vel[c, k]
 
-
-def padded(th, tl, tr):
-    planes, ny = th.shape[:2]
+    @pl.when(code[1] == 0)
+    def _():
+        fill(out_a, high, True)
+        fill(out_b, low, False)
+
+    @pl.when(code[1] != 0)
+    def _():
+        fill(out_a, low, False)
+        fill(out_b, high, True)
+
+
+def sides(code, got_a, got_b, edges, halo=None):
+    ny, nz = edges.shape[1:]
+
+    def fill(left, right):
+        for k, got in enumerate((left, right)):
+            edges[2 * k : 2 * k + 2] = got[: 2 * ny].reshape(2, ny, nz).astype(jnp.float32)
+            if halo is not None:
+                halo[k] = got[2 * ny :]
+
+    @pl.when(code[1] == 0)
+    def _():
+        fill(got_b, got_a)
+
+    @pl.when(code[1] != 0)
+    def _():
+        fill(got_a, got_b)
+
+
+def padded(th, edges):
+    planes = th.shape[0]
 
     def get(p):
         if p < 0:
-            return tl[ny * (p + 2) : ny * (p + 3)].astype(jnp.float32)
+            return edges[p + 2]
         if p >= planes:
-            return tr[ny * (p - planes) : ny * (p - planes + 1)].astype(jnp.float32)
+            return edges[p - planes + 2]
         return th[p]
 
     return get
 
 
-def first_kernel(kap, th, tl, tr, gx, halo, tail, head, work):
+def first_kernel(code, kap, th, got_a, got_b, gx, halo, out_a, out_b, work, edges):
     planes, ny, nz = th.shape
     kappa = kap[0:1, 0:1]
+    sides(code, got_a, got_b, edges, halo)
+
     def put(i, value):
-        value = kappa * value
-        gx[i] = value
-        if i < 2:
-            head[i] = value.astype(jnp.bfloat16)
-        if i >= planes - 2:
-            tail[i - (planes - 2)] = value.astype(jnp.bfloat16)
-
-    halo[0] = tl[2 * ny :]
-    halo[1] = tr[2 * ny :]
-    x_derivative(padded(th, tl, tr), put, work, planes)
+        gx[i] = kappa * value
+
+    x_derivative(padded(th, edges), put, work, planes)
+
+    def fill(out, start):
+        out[...] = gx[start : start + 2].reshape(2 * ny, nz).astype(jnp.bfloat16)
+
+    @pl.when(code[1] == 0)
+    def _():
+        fill(out_a, planes - 2)
+        fill(out_b, 0)
+
+    @pl.when(code[1] != 0)
+    def _():
+        fill(out_a, 0)
+        fill(out_b, planes - 2)
 
 
 def flow_of(part, vel, halo, ry, rz):
@@ -232,13 +269,15 @@
         acc[at] = value
 
 
-def final_kernel(ngrp, index, th, reg, part, inner, gx, tl, tr, gl, gr, *refs):
-    vel, halo, (ky, kz, ry, rz, new_hbm, saved_hbm, new, saved, flux, acc, sems) = refs[:ngrp], refs[ngrp : 2 * ngrp], refs[2 * ngrp :]
+def final_kernel(ngrp, index, th, reg, part, inner, gx, ta, tb, ga, gb, *refs):
+    vel, halo, (ky, kz, ry, rz, new_hbm, saved_hbm, new, saved, flux, acc, edges, grads, sems) = refs[:ngrp], refs[ngrp : 2 * ngrp], refs[2 * ngrp :]
     planes, ny, nz = th.shape
     per = max(1, MXU // ny)
     kz = widen(kz)
     flow = flow_of(index, vel, halo, ry, rz)
-    get = padded(th, tl, tr)
+    sides(index, ta, tb, edges)
+    sides(index, ga, gb, grads)
+    get = padded(th, edges)
     outer = [g for g in range(planes // per) if not is_inner(g, per, planes)]
     for g in outer:
         acc[g * per : (g + 1) * per] = cross(flow, th, ky, kz, g, per) + part[g * per : (g + 1) * per]
@@ -248,9 +287,9 @@
         f = flow(0, which + which[:1] * (per - len(which))).reshape(per, ny, nz)
         for i, p in enumerate(which):
             if p < 0:
-                d = gl[p + 2].astype(jnp.float32)
+                d = grads[p + 2]
             elif p >= planes:
-                d = gr[p - planes].astype(jnp.float32)
+                d = grads[p - planes + 2]
             else:
                 d = gx[p]
             flux[p + 2] = f[i] * get(p) - d
@@ -280,8 +319,8 @@
     nslab, ngrp = lax.axis_size("slab"), lax.axis_size("grp")
     nyc, nzc = ny // 2, nz // 2
     f32, bf16 = jnp.float32, jnp.bfloat16
-    up = [(i, (i + 1) % nslab) for i in range(nslab)]
-    down = [((i + 1) % nslab, i) for i in range(nslab)]
+    swap_a = [(i, i + 1 - 2 * (i % 2)) for i in range(nslab)]
+    swap_b = [(i, (i - 1 + 2 * (i % 2)) % nslab) for i in range(nslab)]
     op_y, op_z = blocked_operator(ny, BLK), blocked_operator(nz, BLK)
     ky2, kz2 = host_stack(op_y @ op_y), host_split((op_z @ op_z).T[:, : nz // 2])
     ky, kz = host_stack(op_y), host_split(op_z.T[:, : nz // 2])
@@ -292,16 +331,17 @@
     field, saved = theta[0], register[0]
     rows, coarse = velocity.shape[2], planes // 2
     full = jax.ShapeDtypeStruct((planes, ny, nz), f32)
-    edge = jax.ShapeDtypeStruct((2, ny, nz), bf16)
+    edge = jax.ShapeDtypeStruct((2 * ny, nz), bf16)
     packed = jax.ShapeDtypeStruct((2 * ny + 4 * rows, nz), bf16)
     vmem = pl.BlockSpec(memory_space=pltpu.VMEM)
     smem = pl.BlockSpec(memory_space=pltpu.SMEM)
     grant = lambda mib: pltpu.CompilerParams(vmem_limit_bytes=mib * 1024 * 1024)
 
-    head, tail, own = pl.pallas_call(
+    part = jnp.stack([lax.axis_index("grp"), lax.axis_index("slab") % 2]).astype(jnp.int32)
+    out_a, out_b, own = pl.pallas_call(
         pack_kernel,
         out_shape=(packed, packed, jax.ShapeDtypeStruct(velocity.shape, bf16)),
-        in_specs=[pl.BlockSpec(memory_space=pltpu.HBM)] * 2,
+        in_specs=[smem] + [pl.BlockSpec(memory_space=pltpu.HBM)] * 2,
         out_specs=(vmem,) * 3,
         scratch_shapes=[
             pltpu.VMEM((2, ny, nz), f32),
@@ -310,28 +350,27 @@
         ],
         compiler_params=grant(4),
         name="pack",
-    )(pltpu.with_memory_space_constraint(theta, pltpu.HBM), pltpu.with_memory_space_constraint(velocity, pltpu.HBM))
+    )(part, pltpu.with_memory_space_constraint(theta, pltpu.HBM), pltpu.with_memory_space_constraint(velocity, pltpu.HBM))
 
     def gathered(x):
         turns = [[((i + t) % ngrp, i) for i in range(ngrp)] for t in range(1, ngrp)]
         return [x] + [lax.ppermute(x, "grp", turn) for turn in turns]
 
     kappa = jnp.broadcast_to(diffusivity[:, None], (8, 128))
-    part = lax.axis_index("grp").astype(jnp.int32)[None]
-    left = lax.ppermute(tail, "slab", up)
-    right = lax.ppermute(head, "slab", down)
+    got_a = lax.ppermute(out_a, "slab", swap_a)
+    got_b = lax.ppermute(out_b, "slab", swap_b)
     vel = gathered(own)
-    gx, halo, tail, head = pl.pallas_call(
+    gx, halo, out_a, out_b = pl.pallas_call(
         first_kernel,
         out_shape=(full, jax.ShapeDtypeStruct((2, 4 * rows, nz), bf16), edge, edge),
-        in_specs=[vmem] * 4,
+        in_specs=[smem] + [vmem] * 4,
         out_specs=(vmem,) * 4,
-        scratch_shapes=[pltpu.VMEM((planes, ny, nz), f32)],
+        scratch_shapes=[pltpu.VMEM((planes, ny, nz), f32), pltpu.VMEM((4, ny, nz), f32)],
         compiler_params=grant(8),
         name="first",
-    )(kappa, field, left, right)
-    grad_l = lax.ppermute(tail, "slab", up)
-    grad_r = lax.ppermute(head, "slab", down)
+    )(part, kappa, field, got_a, got_b)
+    grad_a = lax.ppermute(out_a, "slab", swap_a)
+    grad_b = lax.ppermute(out_b, "slab", swap_b)
     halo = gathered(halo)
     acc, inner = pl.pallas_call(
         functools.partial(inner_kernel, ngrp),
@@ -351,11 +390,13 @@
             pltpu.VMEM((planes, ny, nz), f32),
             pltpu.VMEM((planes + 4, ny, nz), f32),
             pltpu.VMEM((planes, ny, nz), f32),
+            pltpu.VMEM((4, ny, nz), f32),
+            pltpu.VMEM((4, ny, nz), f32),
             pltpu.SemaphoreType.DMA((2 * planes,)),
         ],
         compiler_params=grant(14),
         name="final",
-    )(part, field, saved, acc, inner, gx, left, right, grad_l, grad_r, *vel, *halo, ky, kz, ry, rz)
+    )(part, field, saved, acc, inner, gx, got_a, got_b, grad_a, grad_b, *vel, *halo, ky, kz, ry, rz)
     return (new[None], kept[None])
 
 

time: 25.7 us -> 27.8 us (1.082)
  Pallas kernels: 7.63 us -> 9.87 us
    ppermute x4, starting transfers between devices: 10.9 us -> 10.2 us  [the longest x1 3.55 us: shards(): got_b = lax.ppermute(out_b, 'slab', swap_b)]
    pallas_call x1, Pallas kernels: 3.65 us -> 4.29 us  [shards(): pl.pallas_call(functools.partial(final_kernel, ngrp), out_shape=(full, fu...]
    pallas_call x1, Pallas kernels: 0.62 us -> 1.2 us  [shards(): pl.pallas_call(first_kernel, out_shape=(full, jax.ShapeDtypeStruct((2, 4...]
    ppermute x6, starting transfers between devices: 5.34 us -> 5.91 us  [gathered(): return [x] + [lax.ppermute(x, 'grp', turn) for turn in turns]]
    pallas_call x1, Pallas kernels: 2.26 us -> 2.82 us  [shards(): pl.pallas_call(functools.partial(inner_kernel, ngrp), out_shape=(full, fu...]
    pallas_call x1, Pallas kernels: 1.1 us -> 1.56 us  [shards(): pl.pallas_call(pack_kernel, out_shape=(packed, packed, jax.ShapeDtypeStru...]
  transfers between devices with their start and end apart: 10 -> 10, of which waited for: 0 -> 0; matrix products, arithmetic and copies ran while one was open for 0% -> 0% of each run, Pallas kernels for 11% -> 15%
where the time goes in v7:
time: 27.8 us; the launch traced here: 27.6 us
  starting transfers between devices  16.1 us (58%)
  Pallas kernels  9.87 us (36%)
  between operations  1.49 us (5%)
    ppermute x6, starting transfers between devices, gathered(): return [x] + [lax.ppermute(x, 'grp', turn) for turn in turns]  5.91 us
    pallas_call x1, Pallas kernels, shards(): pl.pallas_call(functools.partial(final_kernel, ngrp), out_shape=(full, fu...  4.29 us
    ppermute x1, starting transfers between devices, shards(): got_b = lax.ppermute(out_b, 'slab', swap_b)  3.55 us
    ppermute x1, starting transfers between devices, shards(): grad_b = lax.ppermute(out_b, 'slab', swap_b)  3.54 us
    ppermute x1, starting transfers between devices, shards(): got_a = lax.ppermute(out_a, 'slab', swap_a)  3.06 us
    pallas_call x1, Pallas kernels, shards(): pl.pallas_call(functools.partial(inner_kernel, ngrp), out_shape=(full, fu...  2.82 us
    pallas_call x1, Pallas kernels, shards(): pl.pallas_call(pack_kernel, out_shape=(packed, packed, jax.ShapeDtypeStru...  1.56 us
    pallas_call x1, Pallas kernels, shards(): pl.pallas_call(first_kernel, out_shape=(full, jax.ShapeDtypeStruct((2, 4...  1.2 us
  transfers between devices with their start and end apart: 10, of which 0 were waited for; matrix products, arithmetic and copies ran while one was open for 0% of the time, Pallas kernels for 15%

profile of v7, /device:TPU:0, one launch (start us, length us, event | category | flops | bytes accessed | tf_op | source)
XLA Modules:
  0.0 27.6 jit_solution(5099072211496890826)
XLA Ops:
  0.6 0.0 copy-start
  0.7 0.1 pad_add_fusion.code.part.index
  0.7 1.6 %pack.1 = (bf16[160,256]{1,0:T(8,128)(2,1)S(1)}, bf16[160,256]{1,0:T(8,128)(2,1)S(1)}, bf16[3,8,8,128]{3,2,1,0:T(8,128)(2,1)S(1)}) custom-call(s32[2]{0:T(128)S(1)} %pad_add_fusion.code.part.index, f32[1,16,64,256]{3,2,1,0:T(8,128)} %theta.1, bf16[3,8,8,128]{3,2,1,0:T(8,128)(2,1)} %velocity.1), custom_call_target="tpu_custom_call" | custom-call | tf_op jit(solution)/shard_map/pack/pallas_call | solution.py:341
  2.3 3.1 %collective-permute-start = (bf16[160,256]{1,0:T(8,128)(2,1)S(1)}, bf16[160,256]{1,0:T(8,128)(2,1)S(1)}, u32[]{:S(2)}, u32[]{:S(2)}) collective-permute-start(bf16[160,256]{1,0:T(8,128)(2,1)S(1)} %get-tuple-element.13), channel_id=1, source_target_pairs={{0,1},{1,0},{2,3},{3,2},{4,5},{5,4},{6,7},{7,6},{8,9},{9,8},{10,11... | collective-permute-start | bytes 245768 | tf_op jit(solution)/shard_map/ppermute | solution.py:360
  5.3 3.5 %collective-permute-start.1 = (bf16[160,256]{1,0:T(8,128)(2,1)S(1)}, bf16[160,256]{1,0:T(8,128)(2,1)S(1)}, u32[]{:S(2)}, u32[]{:S(2)}) collective-permute-start(bf16[160,256]{1,0:T(8,128)(2,1)S(1)} %get-tuple-element.14), channel_id=1, source_target_pairs={{0,7},{1,2},{2,1},{3,4},{4,3},{5,6},{6,5},{7,0},{8,15},{9,10},{10,... | collective-permute-start | bytes 245768 | tf_op jit(solution)/shard_map/ppermute | solution.py:361
  8.9 0.0 collective-permute-start.4
  8.9 1.5 %collective-permute-start.3 = (bf16[3,8,8,128]{3,2,1,0:T(8,128)(2,1)S(1)}, bf16[3,8,8,128]{3,2,1,0:T(8,128)(2,1)S(1)}, u32[]{:S(2)}, u32[]{:S(2)}) collective-permute-start(bf16[3,8,8,128]{3,2,1,0:T(8,128)(2,1)S(1)} %get-tuple-element.16.refs_0_), channel_id=1, source_target_pairs={{16,0},{24,8},{0,16},{8,24},{17,1},{25,9},{1,17},{9,25},{18,2},{26... | collective-permute-start | bytes 147464 | tf_op jit(solution)/shard_map/ppermute | solution.py:357
  10.4 1.5 %collective-permute-start.2 = (bf16[3,8,8,128]{3,2,1,0:T(8,128)(2,1)S(1)}, bf16[3,8,8,128]{3,2,1,0:T(8,128)(2,1)S(1)}, u32[]{:S(2)}, u32[]{:S(2)}) collective-permute-start(bf16[3,8,8,128]{3,2,1,0:T(8,128)(2,1)S(1)} %get-tuple-element.16.refs_0_), channel_id=1, source_target_pairs={{8,0},{16,8},{24,16},{0,24},{9,1},{17,9},{25,17},{1,25},{10,2},{18... | collective-permute-start | bytes 147464 | tf_op jit(solution)/shard_map/ppermute | solution.py:357
  12.5 0.0 collective-permute-done.1.got_b.tb
  12.5 0.0 copy-start.2
  12.6 0.0 copy-start.3
  12.6 0.0 copy-start.4
  12.6 0.0 copy-start.5
  12.6 0.0 copy-start.6
  12.6 0.0 copy-start.7
  12.6 1.2 %first.1 = (f32[16,64,256]{2,1,0:T(8,128)S(1)}, bf16[2,32,256]{2,1,0:T(8,128)(2,1)S(1)}, bf16[128,256]{1,0:T(8,128)(2,1)S(1)}, bf16[128,256]{1,0:T(8,128)(2,1)S(1)}) custom-call(s32[2]{0:T(128)S(1)} %pad_add_fusion.code.part.index, f32[8,128]{1,0:T(8,128)S(1)} %broadcast_in_dim.15.kap, f32[16,64,256]{2,1,0:T(8,128)S(1)} %bitcast.8, ...), custom_call_target="tpu_custom_call" | custom-call | tf_op jit(solution)/shard_map/first/pallas_call | solution.py:363
  13.8 0.1 collective-permute-start.5
  13.9 3.5 %collective-permute-start.6 = (bf16[128,256]{1,0:T(8,128)(2,1)S(1)}, bf16[128,256]{1,0:T(8,128)(2,1)S(1)}, u32[]{:S(2)}, u32[]{:S(2)}) collective-permute-start(bf16[128,256]{1,0:T(8,128)(2,1)S(1)} %get-tuple-element.20), channel_id=1, source_target_pairs={{0,7},{1,2},{2,1},{3,4},{4,3},{5,6},{6,5},{7,0},{8,15},{9,10},{10,... | collective-permute-start | bytes 196616 | tf_op jit(solution)/shard_map/ppermute | solution.py:373
  17.5 0.0 collective-permute-done.4.refs_3_
  17.5 1.6 %collective-permute-start.8 = (bf16[2,32,256]{2,1,0:T(8,128)(2,1)S(1)}, bf16[2,32,256]{2,1,0:T(8,128)(2,1)S(1)}, u32[]{:S(2)}, u32[]{:S(2)}) collective-permute-start(bf16[2,32,256]{2,1,0:T(8,128)(2,1)S(1)} %get-tuple-element.21.refs_4_), channel_id=1, source_target_pairs={{16,0},{24,8},{0,16},{8,24},{17,1},{25,9},{1,17},{9,25},{18,2},{26... | collective-permute-start | bytes 98312 | tf_op jit(solution)/shard_map/ppermute | solution.py:357
  19.0 1.4 %collective-permute-start.7 = (bf16[2,32,256]{2,1,0:T(8,128)(2,1)S(1)}, bf16[2,32,256]{2,1,0:T(8,128)(2,1)S(1)}, u32[]{:S(2)}, u32[]{:S(2)}) collective-permute-start(bf16[2,32,256]{2,1,0:T(8,128)(2,1)S(1)} %get-tuple-element.21.refs_4_), channel_id=1, source_target_pairs={{8,0},{16,8},{24,16},{0,24},{9,1},{17,9},{25,17},{1,25},{10,2},{18... | collective-permute-start | bytes 98312 | tf_op jit(solution)/shard_map/ppermute | solution.py:357
  20.5 0.0 copy-start.1
  20.5 2.8 %inner.1 = (f32[16,64,256]{2,1,0:T(8,128)S(1)}, f32[16,64,256]{2,1,0:T(8,128)S(1)}) custom-call(s32[2]{0:T(128)S(1)} %pad_add_fusion.code.part.index, f32[8,128]{1,0:T(8,128)S(1)} %broadcast_in_dim.15.kap, f32[16,64,256]{2,1,0:T(8,128)S(1)} %bitcast.9, f32[16,64,256]{2,1,0:T(8,128)S(1)} %get-tuple-element.15.gx, ...), custom_call_target="tpu_custom_call" | custom-call | tf_op jit(solution)/shard_map/inner/pallas_call | solution.py:375
  23.4 4.3 %final.1 = (f32[16,64,256]{2,1,0:T(8,128)}, f32[16,64,256]{2,1,0:T(8,128)}) custom-call(s32[2]{0:T(128)S(1)} %pad_add_fusion.code.part.index, f32[16,64,256]{2,1,0:T(8,128)S(1)} %bitcast.10, f32[16,64,256]{2,1,0:T(8,128)S(1)} %bitcast.11, f32[16,64,256]{2,1,0:T(8,128)S(1)} %get-tuple-element.17.part, f32[16,64,256]{2,1,0:T(8,128)S(1)} %get-tuple-element.18.inner, ...), custom_call_target="tpu_custom_call" | custom-call | tf_op jit(solution)/shard_map/final/pallas_call | solution.py:383
  (18 shorter events, 0.0 us)
Async XLA Ops:
  0.6 11.9 %copy-start = (f32[1,16,64,256]{3,2,1,0:T(8,128)S(1)}, f32[1,16,64,256]{3,2,1,0:T(8,128)}, u32[]{:S(2)}) copy-start(f32[1,16,64,256]{3,2,1,0:T(8,128)} %theta.1) | copy-start | bytes 3145732
  2.3 10.2 %collective-permute-start = (bf16[160,256]{1,0:T(8,128)(2,1)S(1)}, bf16[160,256]{1,0:T(8,128)(2,1)S(1)}, u32[]{:S(2)}, u32[]{:S(2)}) collective-permute-start(bf16[160,256]{1,0:T(8,128)(2,1)S(1)} %get-tuple-element.13), channel_id=1, source_target_pairs={{0,1},{1,0},{2,3},{3,2},{4,5},{5,4},{6,7},{7,6},{8,9},{9,8},{10,11... | collective-permute-start | bytes 245768 | tf_op jit(solution)/shard_map/ppermute | solution.py:360
  5.3 7.2 %collective-permute-start.1 = (bf16[160,256]{1,0:T(8,128)(2,1)S(1)}, bf16[160,256]{1,0:T(8,128)(2,1)S(1)}, u32[]{:S(2)}, u32[]{:S(2)}) collective-permute-start(bf16[160,256]{1,0:T(8,128)(2,1)S(1)} %get-tuple-element.14), channel_id=1, source_target_pairs={{0,7},{1,2},{2,1},{3,4},{4,3},{5,6},{6,5},{7,0},{8,15},{9,10},{10,... | collective-permute-start | bytes 245768 | tf_op jit(solution)/shard_map/ppermute | solution.py:361
  8.9 8.6 %collective-permute-start.4 = (bf16[3,8,8,128]{3,2,1,0:T(8,128)(2,1)S(1)}, bf16[3,8,8,128]{3,2,1,0:T(8,128)(2,1)S(1)}, u32[]{:S(2)}, u32[]{:S(2)}) collective-permute-start(bf16[3,8,8,128]{3,2,1,0:T(8,128)(2,1)S(1)} %get-tuple-element.16.refs_0_), channel_id=1, source_target_pairs={{24,0},{0,8},{8,16},{16,24},{25,1},{1,9},{9,17},{17,25},{26,2},{2,... | collective-permute-start | bytes 147464 | tf_op jit(solution)/shard_map/ppermute | solution.py:357
  8.9 8.6 %collective-permute-start.3 = (bf16[3,8,8,128]{3,2,1,0:T(8,128)(2,1)S(1)}, bf16[3,8,8,128]{3,2,1,0:T(8,128)(2,1)S(1)}, u32[]{:S(2)}, u32[]{:S(2)}) collective-permute-start(bf16[3,8,8,128]{3,2,1,0:T(8,128)(2,1)S(1)} %get-tuple-element.16.refs_0_), channel_id=1, source_target_pairs={{16,0},{24,8},{0,16},{8,24},{17,1},{25,9},{1,17},{9,25},{18,2},{26... | collective-permute-start | bytes 147464 | tf_op jit(solution)/shard_map/ppermute | solution.py:357
  10.4 8.6 %collective-permute-start.2 = (bf16[3,8,8,128]{3,2,1,0:T(8,128)(2,1)S(1)}, bf16[3,8,8,128]{3,2,1,0:T(8,128)(2,1)S(1)}, u32[]{:S(2)}, u32[]{:S(2)}) collective-permute-start(bf16[3,8,8,128]{3,2,1,0:T(8,128)(2,1)S(1)} %get-tuple-element.16.refs_0_), channel_id=1, source_target_pairs={{8,0},{16,8},{24,16},{0,24},{9,1},{17,9},{25,17},{1,25},{10,2},{18... | collective-permute-start | bytes 147464 | tf_op jit(solution)/shard_map/ppermute | solution.py:357
  12.5 7.9 %copy-start.2 = (bf16[2,256,128]{2,1,0:T(8,128)(2,1)S(1)}, bf16[2,256,128]{2,1,0:T(8,128)(2,1)}, u32[]{:S(2)}) copy-start(bf16[2,256,128]{2,1,0:T(8,128)(2,1)} %constant.53.refs_5_.refs_9_) | copy-start | bytes 393220
  12.6 7.9 %copy-start.3 = (bf16[128,256]{1,0:T(8,128)(2,1)S(1)}, bf16[128,256]{1,0:T(8,128)(2,1)}, u32[]{:S(2)}) copy-start(bf16[128,256]{1,0:T(8,128)(2,1)} %constant.38.clone.refs_9_.refs_11_) | copy-start | bytes 196612
  12.6 7.9 %copy-start.4 = (bf16[4,64,64]{2,1,0:T(8,128)(2,1)S(1)}, bf16[4,64,64]{2,1,0:T(8,128)(2,1)}, u32[]{:S(2)}) copy-start(bf16[4,64,64]{2,1,0:T(8,128)(2,1)} %constant.37.clone.refs_8_.refs_10_) | copy-start | bytes 98308
  12.6 7.8 %copy-start.5 = (bf16[64,192]{1,0:T(8,128)(2,1)S(1)}, bf16[64,192]{1,0:T(8,128)(2,1)}, u32[]{:S(2)}) copy-start(bf16[64,192]{1,0:T(8,128)(2,1)} %constant.46.refs_4_.refs_8_) | copy-start | bytes 73732
  12.6 7.8 %copy-start.6 = (bf16[2,256,128]{2,1,0:T(8,128)(2,1)S(1)}, bf16[2,256,128]{2,1,0:T(8,128)(2,1)}, u32[]{:S(2)}) copy-start(bf16[2,256,128]{2,1,0:T(8,128)(2,1)} %constant.65.refs_7_) | copy-start | bytes 393220
  12.6 7.8 %copy-start.7 = (bf16[64,192]{1,0:T(8,128)(2,1)S(1)}, bf16[64,192]{1,0:T(8,128)(2,1)}, u32[]{:S(2)}) copy-start(bf16[64,192]{1,0:T(8,128)(2,1)} %constant.58.refs_6_) | copy-start | bytes 73732
  13.8 9.5 %collective-permute-start.5 = (bf16[128,256]{1,0:T(8,128)(2,1)S(1)}, bf16[128,256]{1,0:T(8,128)(2,1)S(1)}, u32[]{:S(2)}, u32[]{:S(2)}) collective-permute-start(bf16[128,256]{1,0:T(8,128)(2,1)S(1)} %get-tuple-element.19), channel_id=1, source_target_pairs={{0,1},{1,0},{2,3},{3,2},{4,5},{5,4},{6,7},{7,6},{8,9},{9,8},{10,11... | collective-permute-start | bytes 196616 | tf_op jit(solution)/shard_map/ppermute | solution.py:372
  13.9 9.4 %collective-permute-start.6 = (bf16[128,256]{1,0:T(8,128)(2,1)S(1)}, bf16[128,256]{1,0:T(8,128)(2,1)S(1)}, u32[]{:S(2)}, u32[]{:S(2)}) collective-permute-start(bf16[128,256]{1,0:T(8,128)(2,1)S(1)} %get-tuple-element.20), channel_id=1, source_target_pairs={{0,7},{1,2},{2,1},{3,4},{4,3},{5,6},{6,5},{7,0},{8,15},{9,10},{10,... | collective-permute-start | bytes 196616 | tf_op jit(solution)/shard_map/ppermute | solution.py:373
  17.5 5.8 %collective-permute-start.9 = (bf16[2,32,256]{2,1,0:T(8,128)(2,1)S(1)}, bf16[2,32,256]{2,1,0:T(8,128)(2,1)S(1)}, u32[]{:S(2)}, u32[]{:S(2)}) collective-permute-start(bf16[2,32,256]{2,1,0:T(8,128)(2,1)S(1)} %get-tuple-element.21.refs_4_), channel_id=1, source_target_pairs={{24,0},{0,8},{8,16},{16,24},{25,1},{1,9},{9,17},{17,25},{26,2},{2,... | collective-permute-start | bytes 98312 | tf_op jit(solution)/shard_map/ppermute | solution.py:357
  17.5 5.8 %collective-permute-start.8 = (bf16[2,32,256]{2,1,0:T(8,128)(2,1)S(1)}, bf16[2,32,256]{2,1,0:T(8,128)(2,1)S(1)}, u32[]{:S(2)}, u32[]{:S(2)}) collective-permute-start(bf16[2,32,256]{2,1,0:T(8,128)(2,1)S(1)} %get-tuple-element.21.refs_4_), channel_id=1, source_target_pairs={{16,0},{24,8},{0,16},{8,24},{17,1},{25,9},{1,17},{9,25},{18,2},{26... | collective-permute-start | bytes 98312 | tf_op jit(solution)/shard_map/ppermute | solution.py:357
  19.0 4.3 %collective-permute-start.7 = (bf16[2,32,256]{2,1,0:T(8,128)(2,1)S(1)}, bf16[2,32,256]{2,1,0:T(8,128)(2,1)S(1)}, u32[]{:S(2)}, u32[]{:S(2)}) collective-permute-start(bf16[2,32,256]{2,1,0:T(8,128)(2,1)S(1)} %get-tuple-element.21.refs_4_), channel_id=1, source_target_pairs={{8,0},{16,8},{24,16},{0,24},{9,1},{17,9},{25,17},{1,25},{10,2},{18... | collective-permute-start | bytes 98312 | tf_op jit(solution)/shard_map/ppermute | solution.py:357
  20.5 2.9 %copy-start.1 = (f32[1,16,64,256]{3,2,1,0:T(8,128)S(1)}, f32[1,16,64,256]{3,2,1,0:T(8,128)}, u32[]{:S(2)}) copy-start(f32[1,16,64,256]{3,2,1,0:T(8,128)} %param.11) | copy-start | bytes 3145732

commit v8 on v7

--- a/solution.py
+++ b/solution.py
@@ -137,12 +137,12 @@
             top = 2 * ny + rows * (q // 2)
             out[top : top + rows, nzc * (q % 2) : nzc * (q % 2 + 1)] = vel[c, k]
 
-    @pl.when(code[1] == 0)
+    @pl.when((code[0] & 1) == 0)
     def _():
         fill(out_a, high, True)
         fill(out_b, low, False)
 
-    @pl.when(code[1] != 0)
+    @pl.when((code[0] & 1) != 0)
     def _():
         fill(out_a, low, False)
         fill(out_b, high, True)
@@ -157,11 +157,11 @@
             if halo is not None:
                 halo[k] = got[2 * ny :]
 
-    @pl.when(code[1] == 0)
+    @pl.when((code[0] & 1) == 0)
     def _():
         fill(got_b, got_a)
 
-    @pl.when(code[1] != 0)
+    @pl.when((code[0] & 1) != 0)
     def _():
         fill(got_a, got_b)
 
@@ -192,12 +192,12 @@
     def fill(out, start):
         out[...] = gx[start : start + 2].reshape(2 * ny, nz).astype(jnp.bfloat16)
 
-    @pl.when(code[1] == 0)
+    @pl.when((code[0] & 1) == 0)
     def _():
         fill(out_a, planes - 2)
         fill(out_b, 0)
 
-    @pl.when(code[1] != 0)
+    @pl.when((code[0] & 1) != 0)
     def _():
         fill(out_a, 0)
         fill(out_b, planes - 2)
@@ -207,7 +207,7 @@
     ngrp = len(vel)
     coarse, rows, nzc = vel[0].shape[1:]
 
-    wide = ry[part[0]]
+    wide = ry[part[0] >> 1]
     deep = jnp.concatenate([rz[...], rz[...]], axis=0)
     nyc = rows * ngrp
 
@@ -337,7 +337,7 @@
     smem = pl.BlockSpec(memory_space=pltpu.SMEM)
     grant = lambda mib: pltpu.CompilerParams(vmem_limit_bytes=mib * 1024 * 1024)
 
-    part = jnp.stack([lax.axis_index("grp"), lax.axis_index("slab") % 2]).astype(jnp.int32)
+    part = (lax.axis_index("grp") * 2 + lax.axis_index("slab") % 2).astype(jnp.int32)[None]
     out_a, out_b, own = pl.pallas_call(
         pack_kernel,
         out_shape=(packed, packed, jax.ShapeDtypeStruct(velocity.shape, bf16)),

time: 27.8 us -> 25.7 us (0.924)
  Pallas kernels: 9.87 us -> 7.8 us
    pallas_call x1, Pallas kernels: 2.82 us -> 2.28 us  [shards(): pl.pallas_call(functools.partial(inner_kernel, ngrp), out_shape=(full, fu...]
    pallas_call x1, Pallas kernels: 4.29 us -> 3.75 us  [shards(): pl.pallas_call(functools.partial(final_kernel, ngrp), out_shape=(full, fu...]
    pallas_call x1, Pallas kernels: 1.2 us -> 0.66 us  [shards(): pl.pallas_call(first_kernel, out_shape=(full, jax.ShapeDtypeStruct((2, 4...]
    pallas_call x1, Pallas kernels: 1.56 us -> 1.1 us  [shards(): pl.pallas_call(pack_kernel, out_shape=(packed, packed, jax.ShapeDtypeStru...]
  transfers between devices with their start and end apart: 10 -> 10, of which waited for: 0 -> 0; matrix products, arithmetic and copies ran while one was open for 0% -> 0% of each run, Pallas kernels for 15% -> 12%
where the time goes in v8:
time: 25.7 us; the launch traced here: 25.5 us
  starting transfers between devices  16.1 us (63%)
  Pallas kernels  7.8 us (30%)
  between operations  1.5 us (6%)
    ppermute x6, starting transfers between devices, gathered(): return [x] + [lax.ppermute(x, 'grp', turn) for turn in turns]  5.91 us
    pallas_call x1, Pallas kernels, shards(): pl.pallas_call(functools.partial(final_kernel, ngrp), out_shape=(full, fu...  3.75 us
    ppermute x1, starting transfers between devices, shards(): got_b = lax.ppermute(out_b, 'slab', swap_b)  3.55 us
    ppermute x1, starting transfers between devices, shards(): grad_b = lax.ppermute(out_b, 'slab', swap_b)  3.54 us
    ppermute x1, starting transfers between devices, shards(): got_a = lax.ppermute(out_a, 'slab', swap_a)  3.06 us
    pallas_call x1, Pallas kernels, shards(): pl.pallas_call(functools.partial(inner_kernel, ngrp), out_shape=(full, fu...  2.28 us
    pallas_call x1, Pallas kernels, shards(): pl.pallas_call(pack_kernel, out_shape=(packed, packed, jax.ShapeDtypeStru...  1.1 us
    pallas_call x1, Pallas kernels, shards(): pl.pallas_call(first_kernel, out_shape=(full, jax.ShapeDtypeStruct((2, 4...  0.66 us
  transfers between devices with their start and end apart: 10, of which 0 were waited for; matrix products, arithmetic and copies ran while one was open for 0% of the time, Pallas kernels for 12%

profile of v8, /device:TPU:0, one launch (start us, length us, event | category | flops | bytes accessed | tf_op | source)
XLA Modules:
  0.0 25.5 jit_solution(5757980595404228046)
XLA Ops:
  0.7 1.1 %pack.1 = (bf16[160,256]{1,0:T(8,128)(2,1)S(1)}, bf16[160,256]{1,0:T(8,128)(2,1)S(1)}, bf16[3,8,8,128]{3,2,1,0:T(8,128)(2,1)S(1)}) custom-call(s32[1]{0:T(128)} %bitcast.code.part.index, f32[1,16,64,256]{3,2,1,0:T(8,128)} %theta.1, bf16[3,8,8,128]{3,2,1,0:T(8,128)(2,1)} %velocity.1), custom_call_target="tpu_custom_call" | custom-call | tf_op jit(solution)/shard_map/pack/pallas_call | solution.py:341
  1.8 3.1 %collective-permute-start = (bf16[160,256]{1,0:T(8,128)(2,1)S(1)}, bf16[160,256]{1,0:T(8,128)(2,1)S(1)}, u32[]{:S(2)}, u32[]{:S(2)}) collective-permute-start(bf16[160,256]{1,0:T(8,128)(2,1)S(1)} %get-tuple-element.13), channel_id=1, source_target_pairs={{0,1},{1,0},{2,3},{3,2},{4,5},{5,4},{6,7},{7,6},{8,9},{9,8},{10,11... | collective-permute-start | bytes 245768 | tf_op jit(solution)/shard_map/ppermute | solution.py:360
  4.8 3.5 %collective-permute-start.1 = (bf16[160,256]{1,0:T(8,128)(2,1)S(1)}, bf16[160,256]{1,0:T(8,128)(2,1)S(1)}, u32[]{:S(2)}, u32[]{:S(2)}) collective-permute-start(bf16[160,256]{1,0:T(8,128)(2,1)S(1)} %get-tuple-element.14), channel_id=1, source_target_pairs={{0,7},{1,2},{2,1},{3,4},{4,3},{5,6},{6,5},{7,0},{8,15},{9,10},{10,... | collective-permute-start | bytes 245768 | tf_op jit(solution)/shard_map/ppermute | solution.py:361
  8.4 0.0 collective-permute-start.4
  8.4 1.5 %collective-permute-start.3 = (bf16[3,8,8,128]{3,2,1,0:T(8,128)(2,1)S(1)}, bf16[3,8,8,128]{3,2,1,0:T(8,128)(2,1)S(1)}, u32[]{:S(2)}, u32[]{:S(2)}) collective-permute-start(bf16[3,8,8,128]{3,2,1,0:T(8,128)(2,1)S(1)} %get-tuple-element.16.refs_0_), channel_id=1, source_target_pairs={{16,0},{24,8},{0,16},{8,24},{17,1},{25,9},{1,17},{9,25},{18,2},{26... | collective-permute-start | bytes 147464 | tf_op jit(solution)/shard_map/ppermute | solution.py:357
  9.9 1.5 %collective-permute-start.2 = (bf16[3,8,8,128]{3,2,1,0:T(8,128)(2,1)S(1)}, bf16[3,8,8,128]{3,2,1,0:T(8,128)(2,1)S(1)}, u32[]{:S(2)}, u32[]{:S(2)}) collective-permute-start(bf16[3,8,8,128]{3,2,1,0:T(8,128)(2,1)S(1)} %get-tuple-element.16.refs_0_), channel_id=1, source_target_pairs={{8,0},{16,8},{24,16},{0,24},{9,1},{17,9},{25,17},{1,25},{10,2},{18... | collective-permute-start | bytes 147464 | tf_op jit(solution)/shard_map/ppermute | solution.py:357
  12.0 0.0 collective-permute-done.1.got_b.tb
  12.0 0.0 copy-start.2
  12.0 0.0 copy-start.3
  12.0 0.0 copy-start.4
  12.1 0.0 copy-start.5
  12.1 0.0 copy-start.6
  12.1 0.0 copy-start.7
  12.1 0.7 %first.1 = (f32[16,64,256]{2,1,0:T(8,128)S(1)}, bf16[2,32,256]{2,1,0:T(8,128)(2,1)S(1)}, bf16[128,256]{1,0:T(8,128)(2,1)S(1)}, bf16[128,256]{1,0:T(8,128)(2,1)S(1)}) custom-call(s32[1]{0:T(128)} %bitcast.code.part.index, f32[8,128]{1,0:T(8,128)S(1)} %broadcast_in_dim.19.kap, f32[16,64,256]{2,1,0:T(8,128)S(1)} %bitcast.7, ...), custom_call_target="tpu_custom_call" | custom-call | tf_op jit(solution)/shard_map/first/pallas_call | solution.py:363
  12.8 0.1 collective-permute-start.5
  12.8 3.5 %collective-permute-start.6 = (bf16[128,256]{1,0:T(8,128)(2,1)S(1)}, bf16[128,256]{1,0:T(8,128)(2,1)S(1)}, u32[]{:S(2)}, u32[]{:S(2)}) collective-permute-start(bf16[128,256]{1,0:T(8,128)(2,1)S(1)} %get-tuple-element.20), channel_id=1, source_target_pairs={{0,7},{1,2},{2,1},{3,4},{4,3},{5,6},{6,5},{7,0},{8,15},{9,10},{10,... | collective-permute-start | bytes 196616 | tf_op jit(solution)/shard_map/ppermute | solution.py:373
  16.4 1.6 %collective-permute-start.8 = (bf16[2,32,256]{2,1,0:T(8,128)(2,1)S(1)}, bf16[2,32,256]{2,1,0:T(8,128)(2,1)S(1)}, u32[]{:S(2)}, u32[]{:S(2)}) collective-permute-start(bf16[2,32,256]{2,1,0:T(8,128)(2,1)S(1)} %get-tuple-element.21.refs_4_), channel_id=1, source_target_pairs={{16,0},{24,8},{0,16},{8,24},{17,1},{25,9},{1,17},{9,25},{18,2},{26... | collective-permute-start | bytes 98312 | tf_op jit(solution)/shard_map/ppermute | solution.py:357
  18.0 0.0 collective-permute-done.2.refs_1_
  18.0 1.4 %collective-permute-start.7 = (bf16[2,32,256]{2,1,0:T(8,128)(2,1)S(1)}, bf16[2,32,256]{2,1,0:T(8,128)(2,1)S(1)}, u32[]{:S(2)}, u32[]{:S(2)}) collective-permute-start(bf16[2,32,256]{2,1,0:T(8,128)(2,1)S(1)} %get-tuple-element.21.refs_4_), channel_id=1, source_target_pairs={{8,0},{16,8},{24,16},{0,24},{9,1},{17,9},{25,17},{1,25},{10,2},{18... | collective-permute-start | bytes 98312 | tf_op jit(solution)/shard_map/ppermute | solution.py:357
  19.4 0.0 copy-start.1
  19.4 2.3 %inner.1 = (f32[16,64,256]{2,1,0:T(8,128)S(1)}, f32[16,64,256]{2,1,0:T(8,128)S(1)}) custom-call(s32[1]{0:T(128)} %bitcast.code.part.index, f32[8,128]{1,0:T(8,128)S(1)} %broadcast_in_dim.19.kap, f32[16,64,256]{2,1,0:T(8,128)S(1)} %bitcast.8, f32[16,64,256]{2,1,0:T(8,128)S(1)} %get-tuple-element.15.gx, bf16[3,8,8,128]{3,2,1,0:T(8,128)(2,1)S(1)} %get-tuple-element.16.refs_0_, ...), custom_call_target="tpu_custom_call" | custom-call | tf_op jit(solution)/shard_map/inner/pallas_call | solution.py:375
  21.7 0.0 collective-permute-done.7.refs_5_
  21.7 0.0 collective-permute-done.5.ga
  21.7 3.8 %final.1 = (f32[16,64,256]{2,1,0:T(8,128)}, f32[16,64,256]{2,1,0:T(8,128)}) custom-call(s32[1]{0:T(128)} %bitcast.code.part.index, f32[16,64,256]{2,1,0:T(8,128)S(1)} %bitcast.9, f32[16,64,256]{2,1,0:T(8,128)S(1)} %bitcast.10, f32[16,64,256]{2,1,0:T(8,128)S(1)} %get-tuple-element.17.part, f32[16,64,256]{2,1,0:T(8,128)S(1)} %get-tuple-element.18.inner, ...), custom_call_target="tpu_custom_call" | custom-call | tf_op jit(solution)/shard_map/final/pallas_call | solution.py:383
  (17 shorter events, 0.0 us)
Async XLA Ops:
  0.6 11.4 %copy-start = (f32[1,16,64,256]{3,2,1,0:T(8,128)S(1)}, f32[1,16,64,256]{3,2,1,0:T(8,128)}, u32[]{:S(2)}) copy-start(f32[1,16,64,256]{3,2,1,0:T(8,128)} %theta.1) | copy-start | bytes 3145732
  1.8 10.2 %collective-permute-start = (bf16[160,256]{1,0:T(8,128)(2,1)S(1)}, bf16[160,256]{1,0:T(8,128)(2,1)S(1)}, u32[]{:S(2)}, u32[]{:S(2)}) collective-permute-start(bf16[160,256]{1,0:T(8,128)(2,1)S(1)} %get-tuple-element.13), channel_id=1, source_target_pairs={{0,1},{1,0},{2,3},{3,2},{4,5},{5,4},{6,7},{7,6},{8,9},{9,8},{10,11... | collective-permute-start | bytes 245768 | tf_op jit(solution)/shard_map/ppermute | solution.py:360
  4.8 7.2 %collective-permute-start.1 = (bf16[160,256]{1,0:T(8,128)(2,1)S(1)}, bf16[160,256]{1,0:T(8,128)(2,1)S(1)}, u32[]{:S(2)}, u32[]{:S(2)}) collective-permute-start(bf16[160,256]{1,0:T(8,128)(2,1)S(1)} %get-tuple-element.14), channel_id=1, source_target_pairs={{0,7},{1,2},{2,1},{3,4},{4,3},{5,6},{6,5},{7,0},{8,15},{9,10},{10,... | collective-permute-start | bytes 245768 | tf_op jit(solution)/shard_map/ppermute | solution.py:361
  8.4 8.0 %collective-permute-start.4 = (bf16[3,8,8,128]{3,2,1,0:T(8,128)(2,1)S(1)}, bf16[3,8,8,128]{3,2,1,0:T(8,128)(2,1)S(1)}, u32[]{:S(2)}, u32[]{:S(2)}) collective-permute-start(bf16[3,8,8,128]{3,2,1,0:T(8,128)(2,1)S(1)} %get-tuple-element.16.refs_0_), channel_id=1, source_target_pairs={{24,0},{0,8},{8,16},{16,24},{25,1},{1,9},{9,17},{17,25},{26,2},{2,... | collective-permute-start | bytes 147464 | tf_op jit(solution)/shard_map/ppermute | solution.py:357
  8.4 8.0 %collective-permute-start.3 = (bf16[3,8,8,128]{3,2,1,0:T(8,128)(2,1)S(1)}, bf16[3,8,8,128]{3,2,1,0:T(8,128)(2,1)S(1)}, u32[]{:S(2)}, u32[]{:S(2)}) collective-permute-start(bf16[3,8,8,128]{3,2,1,0:T(8,128)(2,1)S(1)} %get-tuple-element.16.refs_0_), channel_id=1, source_target_pairs={{16,0},{24,8},{0,16},{8,24},{17,1},{25,9},{1,17},{9,25},{18,2},{26... | collective-permute-start | bytes 147464 | tf_op jit(solution)/shard_map/ppermute | solution.py:357
  9.9 8.1 %collective-permute-start.2 = (bf16[3,8,8,128]{3,2,1,0:T(8,128)(2,1)S(1)}, bf16[3,8,8,128]{3,2,1,0:T(8,128)(2,1)S(1)}, u32[]{:S(2)}, u32[]{:S(2)}) collective-permute-start(bf16[3,8,8,128]{3,2,1,0:T(8,128)(2,1)S(1)} %get-tuple-element.16.refs_0_), channel_id=1, source_target_pairs={{8,0},{16,8},{24,16},{0,24},{9,1},{17,9},{25,17},{1,25},{10,2},{18... | collective-permute-start | bytes 147464 | tf_op jit(solution)/shard_map/ppermute | solution.py:357
  12.0 7.3 %copy-start.2 = (bf16[2,256,128]{2,1,0:T(8,128)(2,1)S(1)}, bf16[2,256,128]{2,1,0:T(8,128)(2,1)}, u32[]{:S(2)}) copy-start(bf16[2,256,128]{2,1,0:T(8,128)(2,1)} %constant.53.refs_5_.refs_9_) | copy-start | bytes 393220
  12.0 7.3 %copy-start.3 = (bf16[128,256]{1,0:T(8,128)(2,1)S(1)}, bf16[128,256]{1,0:T(8,128)(2,1)}, u32[]{:S(2)}) copy-start(bf16[128,256]{1,0:T(8,128)(2,1)} %constant.38.clone.refs_9_.refs_11_) | copy-start | bytes 196612
  12.0 7.3 %copy-start.4 = (bf16[4,64,64]{2,1,0:T(8,128)(2,1)S(1)}, bf16[4,64,64]{2,1,0:T(8,128)(2,1)}, u32[]{:S(2)}) copy-start(bf16[4,64,64]{2,1,0:T(8,128)(2,1)} %constant.37.clone.refs_8_.refs_10_) | copy-start | bytes 98308
  12.1 7.3 %copy-start.5 = (bf16[64,192]{1,0:T(8,128)(2,1)S(1)}, bf16[64,192]{1,0:T(8,128)(2,1)}, u32[]{:S(2)}) copy-start(bf16[64,192]{1,0:T(8,128)(2,1)} %constant.46.refs_4_.refs_8_) | copy-start | bytes 73732
  12.1 7.3 %copy-start.6 = (bf16[2,256,128]{2,1,0:T(8,128)(2,1)S(1)}, bf16[2,256,128]{2,1,0:T(8,128)(2,1)}, u32[]{:S(2)}) copy-start(bf16[2,256,128]{2,1,0:T(8,128)(2,1)} %constant.65.refs_7_) | copy-start | bytes 393220
  12.1 7.3 %copy-start.7 = (bf16[64,192]{1,0:T(8,128)(2,1)S(1)}, bf16[64,192]{1,0:T(8,128)(2,1)}, u32[]{:S(2)}) copy-start(bf16[64,192]{1,0:T(8,128)(2,1)} %constant.58.refs_6_) | copy-start | bytes 73732
  12.8 9.0 %collective-permute-start.5 = (bf16[128,256]{1,0:T(8,128)(2,1)S(1)}, bf16[128,256]{1,0:T(8,128)(2,1)S(1)}, u32[]{:S(2)}, u32[]{:S(2)}) collective-permute-start(bf16[128,256]{1,0:T(8,128)(2,1)S(1)} %get-tuple-element.19), channel_id=1, source_target_pairs={{0,1},{1,0},{2,3},{3,2},{4,5},{5,4},{6,7},{7,6},{8,9},{9,8},{10,11... | collective-permute-start | bytes 196616 | tf_op jit(solution)/shard_map/ppermute | solution.py:372
  12.8 8.9 %collective-permute-start.6 = (bf16[128,256]{1,0:T(8,128)(2,1)S(1)}, bf16[128,256]{1,0:T(8,128)(2,1)S(1)}, u32[]{:S(2)}, u32[]{:S(2)}) collective-permute-start(bf16[128,256]{1,0:T(8,128)(2,1)S(1)} %get-tuple-element.20), channel_id=1, source_target_pairs={{0,7},{1,2},{2,1},{3,4},{4,3},{5,6},{6,5},{7,0},{8,15},{9,10},{10,... | collective-permute-start | bytes 196616 | tf_op jit(solution)/shard_map/ppermute | solution.py:373
  16.4 5.3 %collective-permute-start.9 = (bf16[2,32,256]{2,1,0:T(8,128)(2,1)S(1)}, bf16[2,32,256]{2,1,0:T(8,128)(2,1)S(1)}, u32[]{:S(2)}, u32[]{:S(2)}) collective-permute-start(bf16[2,32,256]{2,1,0:T(8,128)(2,1)S(1)} %get-tuple-element.21.refs_4_), channel_id=1, source_target_pairs={{24,0},{0,8},{8,16},{16,24},{25,1},{1,9},{9,17},{17,25},{26,2},{2,... | collective-permute-start | bytes 98312 | tf_op jit(solution)/shard_map/ppermute | solution.py:357
  16.4 5.3 %collective-permute-start.8 = (bf16[2,32,256]{2,1,0:T(8,128)(2,1)S(1)}, bf16[2,32,256]{2,1,0:T(8,128)(2,1)S(1)}, u32[]{:S(2)}, u32[]{:S(2)}) collective-permute-start(bf16[2,32,256]{2,1,0:T(8,128)(2,1)S(1)} %get-tuple-element.21.refs_4_), channel_id=1, source_target_pairs={{16,0},{24,8},{0,16},{8,24},{17,1},{25,9},{1,17},{9,25},{18,2},{26... | collective-permute-start | bytes 98312 | tf_op jit(solution)/shard_map/ppermute | solution.py:357
  18.0 3.8 %collective-permute-start.7 = (bf16[2,32,256]{2,1,0:T(8,128)(2,1)S(1)}, bf16[2,32,256]{2,1,0:T(8,128)(2,1)S(1)}, u32[]{:S(2)}, u32[]{:S(2)}) collective-permute-start(bf16[2,32,256]{2,1,0:T(8,128)(2,1)S(1)} %get-tuple-element.21.refs_4_), channel_id=1, source_target_pairs={{8,0},{16,8},{24,16},{0,24},{9,1},{17,9},{25,17},{1,25},{10,2},{18... | collective-permute-start | bytes 98312 | tf_op jit(solution)/shard_map/ppermute | solution.py:357
  19.4 2.4 %copy-start.1 = (f32[1,16,64,256]{3,2,1,0:T(8,128)S(1)}, f32[1,16,64,256]{3,2,1,0:T(8,128)}, u32[]{:S(2)}) copy-start(f32[1,16,64,256]{3,2,1,0:T(8,128)} %param.11) | copy-start | bytes 3145732

commit v9 on v8

--- a/solution.py
+++ b/solution.py
@@ -88,7 +88,14 @@
     return m
 
 
-def x_derivative(get, put, work, planes):
+def x_derivative(get_at, put_at, work, planes):
+    ny = work.shape[1]
+    for top in range(0, ny, BLK):
+        rows = slice(top, top + BLK)
+        x_rows(lambda p: get_at(p, rows), lambda i, v: put_at(i, v, rows), work.at[:, rows], planes)
+
+
+def x_rows(get, put, work, planes):
     m = banded_lu(planes)
     ratio = (COEF_B / 4) / (COEF_A / 2)
     y1 = y2 = None
@@ -169,12 +176,12 @@
 def padded(th, edges):
     planes = th.shape[0]
 
-    def get(p):
+    def get(p, rows=slice(None)):
         if p < 0:
-            return edges[p + 2]
+            return edges[p + 2, rows]
         if p >= planes:
-            return edges[p - planes + 2]
-        return th[p]
+            return edges[p - planes + 2, rows]
+        return th[p, rows]
 
     return get
 
@@ -184,8 +191,8 @@
     kappa = kap[0:1, 0:1]
     sides(code, got_a, got_b, edges, halo)
 
-    def put(i, value):
-        gx[i] = kappa * value
+    def put(i, value, rows):
+        gx[i, rows] = kappa * value
 
     x_derivative(padded(th, edges), put, work, planes)
 
@@ -294,18 +301,18 @@
                 d = gx[p]
             flux[p + 2] = f[i] * get(p) - d
 
-    def flux_at(p):
-        return inner[p] if is_inner(p // per, per, planes) else flux[p + 2]
-
-    def put(i, value):
-        rest = part[i] if is_inner(i // per, per, planes) else acc[i]
-        kept = RK_A * reg[i] - STEP * (value + rest)
-        saved[i] = kept
-        new[i] = th[i] + RK_B * kept
+    def flux_at(p, rows):
+        return inner[p, rows] if is_inner(p // per, per, planes) else flux[p + 2, rows]
+
+    def put(i, value, rows):
+        rest = part[i, rows] if is_inner(i // per, per, planes) else acc[i, rows]
+        kept = RK_A * reg[i, rows] - STEP * (value + rest)
+        saved[i, rows] = kept
+        new[i, rows] = th[i, rows] + RK_B * kept
         if i % per == 0:
-            at = pl.ds(i, per)
-            for k, (src, dst) in enumerate(((saved, saved_hbm), (new, new_hbm))):
-                copies.append(pltpu.make_async_copy(src.at[at], dst.at[at], sems.at[2 * (i // per) + k]))
+            at = (pl.ds(i, per), pl.ds(rows.start, BLK))
+            for src, dst in ((saved, saved_hbm), (new, new_hbm)):
+                copies.append(pltpu.make_async_copy(src.at[at], dst.at[at], sems.at[len(copies)]))
                 copies[-1].start()
 
     copies = []

time: 25.7 us -> 25.3 us (0.984)
  Pallas kernels: 7.8 us -> 7.43 us
    pallas_call x1, Pallas kernels: 3.75 us -> 3.49 us  [shards(): pl.pallas_call(functools.partial(final_kernel, ngrp), out_shape=(full, fu...]
  transfers between devices with their start and end apart: 10 -> 10, of which waited for: 0 -> 0; matrix products, arithmetic and copies ran while one was open for 0% -> 0% of each run, Pallas kernels for 12% -> 11%
where the time goes in v9:
time: 25.3 us; the launch traced here: 25.1 us
  starting transfers between devices  16.1 us (64%)
  Pallas kernels  7.43 us (29%)
  between operations  1.5 us (6%)
    ppermute x6, starting transfers between devices, gathered(): return [x] + [lax.ppermute(x, 'grp', turn) for turn in turns]  5.91 us
    ppermute x1, starting transfers between devices, shards(): got_b = lax.ppermute(out_b, 'slab', swap_b)  3.55 us
    ppermute x1, starting transfers between devices, shards(): grad_b = lax.ppermute(out_b, 'slab', swap_b)  3.54 us
    pallas_call x1, Pallas kernels, shards(): pl.pallas_call(functools.partial(final_kernel, ngrp), out_shape=(full, fu...  3.49 us
    ppermute x1, starting transfers between devices, shards(): got_a = lax.ppermute(out_a, 'slab', swap_a)  3.06 us
    pallas_call x1, Pallas kernels, shards(): pl.pallas_call(functools.partial(inner_kernel, ngrp), out_shape=(full, fu...  2.28 us
    pallas_call x1, Pallas kernels, shards(): pl.pallas_call(pack_kernel, out_shape=(packed, packed, jax.ShapeDtypeStru...  1.1 us
    pallas_call x1, Pallas kernels, shards(): pl.pallas_call(first_kernel, out_shape=(full, jax.ShapeDtypeStruct((2, 4...  0.56 us
  transfers between devices with their start and end apart: 10, of which 0 were waited for; matrix products, arithmetic and copies ran while one was open for 0% of the time, Pallas kernels for 11%

profile of v9, /device:TPU:0, one launch (start us, length us, event | category | flops | bytes accessed | tf_op | source)
XLA Modules:
  0.0 25.1 jit_solution(15075184029977226702)
XLA Ops:
  0.7 1.1 %pack.1 = (bf16[160,256]{1,0:T(8,128)(2,1)S(1)}, bf16[160,256]{1,0:T(8,128)(2,1)S(1)}, bf16[3,8,8,128]{3,2,1,0:T(8,128)(2,1)S(1)}) custom-call(s32[1]{0:T(128)} %bitcast.code.part.index, f32[1,16,64,256]{3,2,1,0:T(8,128)} %theta.1, bf16[3,8,8,128]{3,2,1,0:T(8,128)(2,1)} %velocity.1), custom_call_target="tpu_custom_call" | custom-call | tf_op jit(solution)/shard_map/pack/pallas_call | solution.py:348
  1.8 3.1 %collective-permute-start = (bf16[160,256]{1,0:T(8,128)(2,1)S(1)}, bf16[160,256]{1,0:T(8,128)(2,1)S(1)}, u32[]{:S(2)}, u32[]{:S(2)}) collective-permute-start(bf16[160,256]{1,0:T(8,128)(2,1)S(1)} %get-tuple-element.13), channel_id=1, source_target_pairs={{0,1},{1,0},{2,3},{3,2},{4,5},{5,4},{6,7},{7,6},{8,9},{9,8},{10,11... | collective-permute-start | bytes 245768 | tf_op jit(solution)/shard_map/ppermute | solution.py:367
  4.8 3.5 %collective-permute-start.1 = (bf16[160,256]{1,0:T(8,128)(2,1)S(1)}, bf16[160,256]{1,0:T(8,128)(2,1)S(1)}, u32[]{:S(2)}, u32[]{:S(2)}) collective-permute-start(bf16[160,256]{1,0:T(8,128)(2,1)S(1)} %get-tuple-element.14), channel_id=1, source_target_pairs={{0,7},{1,2},{2,1},{3,4},{4,3},{5,6},{6,5},{7,0},{8,15},{9,10},{10,... | collective-permute-start | bytes 245768 | tf_op jit(solution)/shard_map/ppermute | solution.py:368
  8.4 0.0 collective-permute-start.4
  8.4 1.5 %collective-permute-start.3 = (bf16[3,8,8,128]{3,2,1,0:T(8,128)(2,1)S(1)}, bf16[3,8,8,128]{3,2,1,0:T(8,128)(2,1)S(1)}, u32[]{:S(2)}, u32[]{:S(2)}) collective-permute-start(bf16[3,8,8,128]{3,2,1,0:T(8,128)(2,1)S(1)} %get-tuple-element.16.refs_0_), channel_id=1, source_target_pairs={{16,0},{24,8},{0,16},{8,24},{17,1},{25,9},{1,17},{9,25},{18,2},{26... | collective-permute-start | bytes 147464 | tf_op jit(solution)/shard_map/ppermute | solution.py:364
  9.9 1.5 %collective-permute-start.2 = (bf16[3,8,8,128]{3,2,1,0:T(8,128)(2,1)S(1)}, bf16[3,8,8,128]{3,2,1,0:T(8,128)(2,1)S(1)}, u32[]{:S(2)}, u32[]{:S(2)}) collective-permute-start(bf16[3,8,8,128]{3,2,1,0:T(8,128)(2,1)S(1)} %get-tuple-element.16.refs_0_), channel_id=1, source_target_pairs={{8,0},{16,8},{24,16},{0,24},{9,1},{17,9},{25,17},{1,25},{10,2},{18... | collective-permute-start | bytes 147464 | tf_op jit(solution)/shard_map/ppermute | solution.py:364
  12.0 0.0 collective-permute-done.1.got_b.tb
  12.0 0.0 copy-start.2
  12.0 0.0 copy-start.3
  12.0 0.0 copy-start.4
  12.1 0.0 copy-start.5
  12.1 0.0 copy-start.6
  12.1 0.0 copy-start.7
  12.1 0.6 %first.1 = (f32[16,64,256]{2,1,0:T(8,128)S(1)}, bf16[2,32,256]{2,1,0:T(8,128)(2,1)S(1)}, bf16[128,256]{1,0:T(8,128)(2,1)S(1)}, bf16[128,256]{1,0:T(8,128)(2,1)S(1)}) custom-call(s32[1]{0:T(128)} %bitcast.code.part.index, f32[8,128]{1,0:T(8,128)S(1)} %broadcast_in_dim.19.kap, f32[16,64,256]{2,1,0:T(8,128)S(1)} %bitcast.7, ...), custom_call_target="tpu_custom_call" | custom-call | tf_op jit(solution)/shard_map/first/pallas_call | solution.py:370
  12.7 0.1 collective-permute-start.5
  12.7 3.5 %collective-permute-start.6 = (bf16[128,256]{1,0:T(8,128)(2,1)S(1)}, bf16[128,256]{1,0:T(8,128)(2,1)S(1)}, u32[]{:S(2)}, u32[]{:S(2)}) collective-permute-start(bf16[128,256]{1,0:T(8,128)(2,1)S(1)} %get-tuple-element.20), channel_id=1, source_target_pairs={{0,7},{1,2},{2,1},{3,4},{4,3},{5,6},{6,5},{7,0},{8,15},{9,10},{10,... | collective-permute-start | bytes 196616 | tf_op jit(solution)/shard_map/ppermute | solution.py:380
  16.3 1.6 %collective-permute-start.8 = (bf16[2,32,256]{2,1,0:T(8,128)(2,1)S(1)}, bf16[2,32,256]{2,1,0:T(8,128)(2,1)S(1)}, u32[]{:S(2)}, u32[]{:S(2)}) collective-permute-start(bf16[2,32,256]{2,1,0:T(8,128)(2,1)S(1)} %get-tuple-element.21.refs_4_), channel_id=1, source_target_pairs={{16,0},{24,8},{0,16},{8,24},{17,1},{25,9},{1,17},{9,25},{18,2},{26... | collective-permute-start | bytes 98312 | tf_op jit(solution)/shard_map/ppermute | solution.py:364
  17.8 0.0 collective-permute-done.2.refs_1_
  17.9 1.4 %collective-permute-start.7 = (bf16[2,32,256]{2,1,0:T(8,128)(2,1)S(1)}, bf16[2,32,256]{2,1,0:T(8,128)(2,1)S(1)}, u32[]{:S(2)}, u32[]{:S(2)}) collective-permute-start(bf16[2,32,256]{2,1,0:T(8,128)(2,1)S(1)} %get-tuple-element.21.refs_4_), channel_id=1, source_target_pairs={{8,0},{16,8},{24,16},{0,24},{9,1},{17,9},{25,17},{1,25},{10,2},{18... | collective-permute-start | bytes 98312 | tf_op jit(solution)/shard_map/ppermute | solution.py:364
  19.3 0.0 copy-start.1
  19.3 2.3 %inner.1 = (f32[16,64,256]{2,1,0:T(8,128)S(1)}, f32[16,64,256]{2,1,0:T(8,128)S(1)}) custom-call(s32[1]{0:T(128)} %bitcast.code.part.index, f32[8,128]{1,0:T(8,128)S(1)} %broadcast_in_dim.19.kap, f32[16,64,256]{2,1,0:T(8,128)S(1)} %bitcast.8, f32[16,64,256]{2,1,0:T(8,128)S(1)} %get-tuple-element.15.gx, bf16[3,8,8,128]{3,2,1,0:T(8,128)(2,1)S(1)} %get-tuple-element.16.refs_0_, ...), custom_call_target="tpu_custom_call" | custom-call | tf_op jit(solution)/shard_map/inner/pallas_call | solution.py:382
  21.6 0.0 collective-permute-done.9.refs_7_
  21.6 0.0 collective-permute-done.7.refs_5_
  21.6 3.5 %final.1 = (f32[16,64,256]{2,1,0:T(8,128)}, f32[16,64,256]{2,1,0:T(8,128)}) custom-call(s32[1]{0:T(128)} %bitcast.code.part.index, f32[16,64,256]{2,1,0:T(8,128)S(1)} %bitcast.9, f32[16,64,256]{2,1,0:T(8,128)S(1)} %bitcast.10, f32[16,64,256]{2,1,0:T(8,128)S(1)} %get-tuple-element.17.part, f32[16,64,256]{2,1,0:T(8,128)S(1)} %get-tuple-element.18.inner, ...), custom_call_target="tpu_custom_call" | custom-call | tf_op jit(solution)/shard_map/final/pallas_call | solution.py:390
  (17 shorter events, 0.0 us)
Async XLA Ops:
  0.6 11.4 %copy-start = (f32[1,16,64,256]{3,2,1,0:T(8,128)S(1)}, f32[1,16,64,256]{3,2,1,0:T(8,128)}, u32[]{:S(2)}) copy-start(f32[1,16,64,256]{3,2,1,0:T(8,128)} %theta.1) | copy-start | bytes 3145732
  1.8 10.2 %collective-permute-start = (bf16[160,256]{1,0:T(8,128)(2,1)S(1)}, bf16[160,256]{1,0:T(8,128)(2,1)S(1)}, u32[]{:S(2)}, u32[]{:S(2)}) collective-permute-start(bf16[160,256]{1,0:T(8,128)(2,1)S(1)} %get-tuple-element.13), channel_id=1, source_target_pairs={{0,1},{1,0},{2,3},{3,2},{4,5},{5,4},{6,7},{7,6},{8,9},{9,8},{10,11... | collective-permute-start | bytes 245768 | tf_op jit(solution)/shard_map/ppermute | solution.py:367
  4.8 7.2 %collective-permute-start.1 = (bf16[160,256]{1,0:T(8,128)(2,1)S(1)}, bf16[160,256]{1,0:T(8,128)(2,1)S(1)}, u32[]{:S(2)}, u32[]{:S(2)}) collective-permute-start(bf16[160,256]{1,0:T(8,128)(2,1)S(1)} %get-tuple-element.14), channel_id=1, source_target_pairs={{0,7},{1,2},{2,1},{3,4},{4,3},{5,6},{6,5},{7,0},{8,15},{9,10},{10,... | collective-permute-start | bytes 245768 | tf_op jit(solution)/shard_map/ppermute | solution.py:368
  8.4 7.9 %collective-permute-start.4 = (bf16[3,8,8,128]{3,2,1,0:T(8,128)(2,1)S(1)}, bf16[3,8,8,128]{3,2,1,0:T(8,128)(2,1)S(1)}, u32[]{:S(2)}, u32[]{:S(2)}) collective-permute-start(bf16[3,8,8,128]{3,2,1,0:T(8,128)(2,1)S(1)} %get-tuple-element.16.refs_0_), channel_id=1, source_target_pairs={{24,0},{0,8},{8,16},{16,24},{25,1},{1,9},{9,17},{17,25},{26,2},{2,... | collective-permute-start | bytes 147464 | tf_op jit(solution)/shard_map/ppermute | solution.py:364
  8.4 7.9 %collective-permute-start.3 = (bf16[3,8,8,128]{3,2,1,0:T(8,128)(2,1)S(1)}, bf16[3,8,8,128]{3,2,1,0:T(8,128)(2,1)S(1)}, u32[]{:S(2)}, u32[]{:S(2)}) collective-permute-start(bf16[3,8,8,128]{3,2,1,0:T(8,128)(2,1)S(1)} %get-tuple-element.16.refs_0_), channel_id=1, source_target_pairs={{16,0},{24,8},{0,16},{8,24},{17,1},{25,9},{1,17},{9,25},{18,2},{26... | collective-permute-start | bytes 147464 | tf_op jit(solution)/shard_map/ppermute | solution.py:364
  9.9 8.0 %collective-permute-start.2 = (bf16[3,8,8,128]{3,2,1,0:T(8,128)(2,1)S(1)}, bf16[3,8,8,128]{3,2,1,0:T(8,128)(2,1)S(1)}, u32[]{:S(2)}, u32[]{:S(2)}) collective-permute-start(bf16[3,8,8,128]{3,2,1,0:T(8,128)(2,1)S(1)} %get-tuple-element.16.refs_0_), channel_id=1, source_target_pairs={{8,0},{16,8},{24,16},{0,24},{9,1},{17,9},{25,17},{1,25},{10,2},{18... | collective-permute-start | bytes 147464 | tf_op jit(solution)/shard_map/ppermute | solution.py:364
  12.0 7.2 %copy-start.2 = (bf16[2,256,128]{2,1,0:T(8,128)(2,1)S(1)}, bf16[2,256,128]{2,1,0:T(8,128)(2,1)}, u32[]{:S(2)}) copy-start(bf16[2,256,128]{2,1,0:T(8,128)(2,1)} %constant.53.refs_5_.refs_9_) | copy-start | bytes 393220
  12.0 7.2 %copy-start.3 = (bf16[128,256]{1,0:T(8,128)(2,1)S(1)}, bf16[128,256]{1,0:T(8,128)(2,1)}, u32[]{:S(2)}) copy-start(bf16[128,256]{1,0:T(8,128)(2,1)} %constant.38.clone.refs_9_.refs_11_) | copy-start | bytes 196612
  12.0 7.2 %copy-start.4 = (bf16[4,64,64]{2,1,0:T(8,128)(2,1)S(1)}, bf16[4,64,64]{2,1,0:T(8,128)(2,1)}, u32[]{:S(2)}) copy-start(bf16[4,64,64]{2,1,0:T(8,128)(2,1)} %constant.37.clone.refs_8_.refs_10_) | copy-start | bytes 98308
  12.1 7.2 %copy-start.5 = (bf16[64,192]{1,0:T(8,128)(2,1)S(1)}, bf16[64,192]{1,0:T(8,128)(2,1)}, u32[]{:S(2)}) copy-start(bf16[64,192]{1,0:T(8,128)(2,1)} %constant.46.refs_4_.refs_8_) | copy-start | bytes 73732
  12.1 7.2 %copy-start.6 = (bf16[2,256,128]{2,1,0:T(8,128)(2,1)S(1)}, bf16[2,256,128]{2,1,0:T(8,128)(2,1)}, u32[]{:S(2)}) copy-start(bf16[2,256,128]{2,1,0:T(8,128)(2,1)} %constant.65.refs_7_) | copy-start | bytes 393220
  12.1 7.2 %copy-start.7 = (bf16[64,192]{1,0:T(8,128)(2,1)S(1)}, bf16[64,192]{1,0:T(8,128)(2,1)}, u32[]{:S(2)}) copy-start(bf16[64,192]{1,0:T(8,128)(2,1)} %constant.58.refs_6_) | copy-start | bytes 73732
  12.7 9.0 %collective-permute-start.5 = (bf16[128,256]{1,0:T(8,128)(2,1)S(1)}, bf16[128,256]{1,0:T(8,128)(2,1)S(1)}, u32[]{:S(2)}, u32[]{:S(2)}) collective-permute-start(bf16[128,256]{1,0:T(8,128)(2,1)S(1)} %get-tuple-element.19), channel_id=1, source_target_pairs={{0,1},{1,0},{2,3},{3,2},{4,5},{5,4},{6,7},{7,6},{8,9},{9,8},{10,11... | collective-permute-start | bytes 196616 | tf_op jit(solution)/shard_map/ppermute | solution.py:379
  12.7 8.9 %collective-permute-start.6 = (bf16[128,256]{1,0:T(8,128)(2,1)S(1)}, bf16[128,256]{1,0:T(8,128)(2,1)S(1)}, u32[]{:S(2)}, u32[]{:S(2)}) collective-permute-start(bf16[128,256]{1,0:T(8,128)(2,1)S(1)} %get-tuple-element.20), channel_id=1, source_target_pairs={{0,7},{1,2},{2,1},{3,4},{4,3},{5,6},{6,5},{7,0},{8,15},{9,10},{10,... | collective-permute-start | bytes 196616 | tf_op jit(solution)/shard_map/ppermute | solution.py:380
  16.3 5.3 %collective-permute-start.9 = (bf16[2,32,256]{2,1,0:T(8,128)(2,1)S(1)}, bf16[2,32,256]{2,1,0:T(8,128)(2,1)S(1)}, u32[]{:S(2)}, u32[]{:S(2)}) collective-permute-start(bf16[2,32,256]{2,1,0:T(8,128)(2,1)S(1)} %get-tuple-element.21.refs_4_), channel_id=1, source_target_pairs={{24,0},{0,8},{8,16},{16,24},{25,1},{1,9},{9,17},{17,25},{26,2},{2,... | collective-permute-start | bytes 98312 | tf_op jit(solution)/shard_map/ppermute | solution.py:364
  16.3 5.3 %collective-permute-start.8 = (bf16[2,32,256]{2,1,0:T(8,128)(2,1)S(1)}, bf16[2,32,256]{2,1,0:T(8,128)(2,1)S(1)}, u32[]{:S(2)}, u32[]{:S(2)}) collective-permute-start(bf16[2,32,256]{2,1,0:T(8,128)(2,1)S(1)} %get-tuple-element.21.refs_4_), channel_id=1, source_target_pairs={{16,0},{24,8},{0,16},{8,24},{17,1},{25,9},{1,17},{9,25},{18,2},{26... | collective-permute-start | bytes 98312 | tf_op jit(solution)/shard_map/ppermute | solution.py:364
  17.9 3.8 %collective-permute-start.7 = (bf16[2,32,256]{2,1,0:T(8,128)(2,1)S(1)}, bf16[2,32,256]{2,1,0:T(8,128)(2,1)S(1)}, u32[]{:S(2)}, u32[]{:S(2)}) collective-permute-start(bf16[2,32,256]{2,1,0:T(8,128)(2,1)S(1)} %get-tuple-element.21.refs_4_), channel_id=1, source_target_pairs={{8,0},{16,8},{24,16},{0,24},{9,1},{17,9},{25,17},{1,25},{10,2},{18... | collective-permute-start | bytes 98312 | tf_op jit(solution)/shard_map/ppermute | solution.py:364
  19.3 2.4 %copy-start.1 = (f32[1,16,64,256]{3,2,1,0:T(8,128)S(1)}, f32[1,16,64,256]{3,2,1,0:T(8,128)}, u32[]{:S(2)}) copy-start(f32[1,16,64,256]{3,2,1,0:T(8,128)} %param.11) | copy-start | bytes 3145732
